TPU v7x, 32 devices: a whole 2x2x4 slice. The times are simulated.
32 devices in a mesh: dp: 16 (over z, y, core), tensor: 2 (over x).
Axes of the slice: x: 2, y: 2, z: 4, core: 2. Of those that a mesh axis runs over, the one named last changes fastest.
Arguments:
- tokens_in: bfloat16 [24576, 1152], P(('dp', 'tensor')), may hold values from -6 to 6
- condition: bfloat16 [96, 1152], P('dp'), may hold values from -6 to 6
- ada_weight: bfloat16 [1152, 6912], replicated, may hold values from -0.1875 to 0.1875
- ada_bias: bfloat16 [6912], replicated, may hold values from -1.75 to 1.75
- qkv_weight: bfloat16 [1152, 3, 1152], P(None, None, 'tensor'), may hold values from -0.1875 to 0.1875
- qv_bias: bfloat16 [2, 1152], P(None, 'tensor'), may hold values from -1.75 to 1.75
- out_weight: bfloat16 [1152, 1152], P('tensor'), may hold values from -2 to 2
- out_bias: bfloat16 [1152], replicated, may hold values from -1.75 to 1.75
- up_weight: bfloat16 [1152, 4608], P(None, 'tensor'), may hold values from -0.1875 to 0.1875
- up_bias: bfloat16 [4608], P('tensor'), may hold values from -1.75 to 1.75
- down_weight: bfloat16 [4608, 1152], P('tensor'), may hold values from -0.09375 to 0.09375
- down_bias: bfloat16 [1152], replicated, may hold values from -1.75 to 1.75
- proj_in: bfloat16 [1152, 2048], replicated, may hold values from -0.1875 to 0.1875
- proj_in_bias: bfloat16 [2048], replicated, may hold values from -1.75 to 1.75
- proj_mid: bfloat16 [2048, 2048], replicated, may hold values from -0.125 to 0.125
- proj_mid_bias: bfloat16 [2048], replicated, may hold values from -1.75 to 1.75
- proj_last: bfloat16 [2048, 768], replicated, may hold values from -0.125 to 0.125
- proj_last_bias: bfloat16 [768], replicated, may hold values from -1.75 to 1.75
- enc_features: bfloat16 [24576, 768], P('dp'), may hold values from -6 to 6
- image_ids: int32 [24576], P('dp'), may hold values from 0 to 5, as said below
- target_rows: int32 [24576], P(('dp', 'tensor')), may hold values from 0 to 24575, as said below
- out_grad: bfloat16 [24576, 1152], P(('dp', 'tensor')), may hold values from -12 to 12
Outputs:
- block_out: bfloat16 [24576, 1152], P(('dp', 'tensor'))
- grad_tokens: float32 [24576, 1152], P(('dp', 'tensor'))
- grad_condition: float32 [96, 1152], P('dp')
- grad_ada_weight: float32 [1152, 6912], P(None, ('dp', 'tensor'))
- grad_ada_bias: float32 [6912], P(('dp', 'tensor'))
- grad_qkv_weight: float32 [1152, 3, 1152], P('dp', None, 'tensor')
- grad_qv_bias: float32 [2, 1152], P(None, 'tensor')
- grad_out_weight: float32 [1152, 1152], P('tensor', 'dp')
- grad_out_bias: float32 [1152], replicated
- grad_up_weight: float32 [1152, 4608], P('dp', 'tensor')
- grad_up_bias: float32 [4608], P('tensor')
- grad_down_weight: float32 [4608, 1152], P('tensor', 'dp')
- grad_down_bias: float32 [1152], replicated
- grad_proj_in: float32 [1152, 2048], P(None, ('dp', 'tensor'))
- grad_proj_in_bias: float32 [2048], replicated
- grad_proj_mid: float32 [2048, 2048], P(None, ('dp', 'tensor'))
- grad_proj_mid_bias: float32 [2048], replicated
- grad_proj_last: float32 [2048, 768], P(None, ('dp', 'tensor'))
- grad_proj_last_bias: float32 [768], replicated
Inputs may be any that keep to these rules, and one draw needn't show every extreme that they name: `image_ids`: within each block of 1536 tokens (one index of dp) the ids start at 0 and rise by one from image to image; each image holds 256 or 1024 tokens; a block holds k images of 1024 tokens and 6 - 4 * k of 256, and every k from 0 to 1 occurs in some block. `target_rows`: each token's row is the position, counted over all 24576 tokens, of a token of the same image.
All inputs are finite; a program needn't handle non-finite values.
Results may differ from a plain program's by a relative error of at most 0.025.
Values may be sent and summed in bfloat16 or wider, within the bound.
A program may use at most 576 MiB of HBM per device.

v0:
```python
import jax
import jax.numpy as jnp
from jax import lax
from jax.sharding import PartitionSpec as P

HEAD_DIM = 72
SHORT = 256


highest = lax.Precision.HIGHEST
eps_norm = 1e-06
repa_weight = 1000.0
neg_fill = -1e30


def dot_nt(left_arg, right_arg):
    return lax.dot_general(
        left_arg, right_arg, (((1,), (1,)), ((), ())), preferred_element_type=jnp.float32
    )


def dot_tn(left_arg, right_arg, precision=None):
    return lax.dot_general(
        left_arg,
        right_arg,
        (((0,), (0,)), ((), ())),
        precision=precision,
        preferred_element_type=jnp.float32,
    )


def layer_norm(values):
    center = values - jnp.mean(values, axis=-1, keepdims=True)
    inv_std = lax.rsqrt(jnp.mean(center * center, axis=-1, keepdims=True) + eps_norm)
    return (center * inv_std, inv_std)


def norm_back(normed, inv_std, grad_normed):
    return inv_std * (
        grad_normed
        - jnp.mean(grad_normed, axis=-1, keepdims=True)
        - normed * jnp.mean(grad_normed * normed, axis=-1, keepdims=True)
    )


def gelu_tanh(values):
    return jax.nn.gelu(values, approximate=True)


def align_loss(projected, target_vals):
    inner = jnp.sum(projected * target_vals, axis=1)
    norm_pred = lax.rsqrt(jnp.sum(projected * projected, axis=1) + eps_norm)
    norm_target = lax.rsqrt(jnp.sum(target_vals * target_vals, axis=1) + eps_norm)
    return -repa_weight * jnp.sum(inner * norm_pred * norm_target)


def block_rows(total_rows, unit_rows):
    count = total_rows // unit_rows
    best = 1
    for parts in range(1, count + 1):
        if count % parts == 0 and parts * unit_rows <= 1024:
            best = parts
    return best * unit_rows


def block_scores(queries, key_rows, image_ids, row_start, starts, block_len, score_scale):
    query_blk = queries[row_start : row_start + block_len]
    row_ids = image_ids[row_start : row_start + block_len]
    pieces = []
    for col_start in starts:

        def compute_block(col_start=col_start):
            products = (
                jnp.einsum(
                    "qhd,khd->hqk",
                    query_blk,
                    key_rows[col_start : col_start + block_len],
                    preferred_element_type=jnp.float32,
                )
                * score_scale
            )
            same_image = row_ids[:, None] == image_ids[col_start : col_start + block_len][None, :]
            return jnp.where(same_image[None], products, neg_fill)

        pieces.append(compute_block())
    return jnp.concatenate(pieces, axis=2)


def attention_forward(queries, key_rows, values, image_ids, block_len, score_scale):
    starts = list(range(0, queries.shape[0], block_len))
    outputs = []
    log_sums = []
    for row_start in starts:
        scores = block_scores(
            queries, key_rows, image_ids, row_start, starts, block_len, score_scale
        )
        row_max = jnp.max(scores, axis=2, keepdims=True)
        exponent = jnp.exp(scores - row_max)
        row_total = jnp.sum(exponent, axis=2, keepdims=True)
        prob_low = (exponent / row_total).astype(jnp.bfloat16)
        log_sums.append(row_max + jnp.log(row_total))
        summed = jnp.zeros((block_len, queries.shape[1], queries.shape[2]), jnp.float32)
        for position, col_start in enumerate(starts):

            def weigh_block(position=position, col_start=col_start, prob_low=prob_low):
                return jnp.einsum(
                    "hqk,khd->qhd",
                    prob_low[:, :, position * block_len : (position + 1) * block_len],
                    values[col_start : col_start + block_len],
                    preferred_element_type=jnp.float32,
                )

            summed = summed + weigh_block()
        outputs.append(summed.astype(jnp.bfloat16))
    return (jnp.concatenate(outputs, axis=0), jnp.concatenate(log_sums, axis=1))


def attention_backward(
    queries, key_rows, values, image_ids, log_sums, grad_heads, block_len, score_scale
):
    starts = list(range(0, queries.shape[0], block_len))
    grad_keys = jnp.zeros(key_rows.shape, jnp.float32)
    grad_values = jnp.zeros(values.shape, jnp.float32)
    grad_query_list = []
    for row_start in starts:
        query_blk = queries[row_start : row_start + block_len]
        grad_blk = grad_heads[row_start : row_start + block_len]
        scores = block_scores(
            queries, key_rows, image_ids, row_start, starts, block_len, score_scale
        )
        soft = jnp.exp(scores - log_sums[:, row_start : row_start + block_len])
        grad_pieces = []
        for col_start in starts:

            def pull_block(col_start=col_start):
                return jnp.einsum(
                    "qhd,khd->hqk",
                    grad_blk,
                    values[col_start : col_start + block_len],
                    preferred_element_type=jnp.float32,
                )

            grad_pieces.append(pull_block())
        grad_soft = jnp.concatenate(grad_pieces, axis=2)
        inner = jnp.sum(soft * grad_soft, axis=2, keepdims=True)
        grad_scores = (soft * (grad_soft - inner)).astype(jnp.bfloat16)
        soft_low = soft.astype(jnp.bfloat16)
        grad_query = jnp.zeros(query_blk.shape, jnp.float32)
        for position, col_start in enumerate(starts):

            def both_grads(position=position, col_start=col_start):
                piece = grad_scores[:, :, position * block_len : (position + 1) * block_len]
                soft_piece = soft_low[:, :, position * block_len : (position + 1) * block_len]
                return (
                    jnp.einsum(
                        "hqk,khd->qhd",
                        piece,
                        key_rows[col_start : col_start + block_len],
                        preferred_element_type=jnp.float32,
                    ),
                    jnp.einsum(
                        "hqk,qhd->khd", piece, query_blk, preferred_element_type=jnp.float32
                    ),
                    jnp.einsum(
                        "hqk,qhd->khd", soft_piece, grad_blk, preferred_element_type=jnp.float32
                    ),
                )

            part_query, part_key, part_value = both_grads()
            grad_query = grad_query + part_query
            grad_keys = grad_keys.at[col_start : col_start + block_len].add(part_key)
            grad_values = grad_values.at[col_start : col_start + block_len].add(part_value)
        grad_query_list.append(grad_query * score_scale)
    return (jnp.concatenate(grad_query_list, axis=0), grad_keys * score_scale, grad_values)


def column_set(matrix, data_count, tensor_count, tensor_rank):
    shaped = matrix.reshape(matrix.shape[0], data_count, tensor_count, -1)
    return lax.dynamic_index_in_dim(shaped, tensor_rank, axis=2, keepdims=False).reshape(
        matrix.shape[0], -1
    )


def shards(
    tokens_in,
    condition,
    ada_weight,
    ada_bias,
    qkv_weight,
    qv_bias,
    out_weight,
    out_bias,
    up_weight,
    up_bias,
    down_weight,
    down_bias,
    proj_in,
    proj_in_bias,
    proj_mid,
    proj_mid_bias,
    proj_last,
    proj_last_bias,
    enc_features,
    image_ids,
    target_rows,
    out_grad,
):
    tensor_count = lax.axis_size("tensor")
    data_count = lax.axis_size("dp")
    tensor_rank = lax.axis_index("tensor")
    data_rank = lax.axis_index("dp")
    local_rows, model_width = tokens_in.shape
    shard_rows = image_ids.shape[0]
    slot_count = condition.shape[0]
    local_cols = qkv_weight.shape[2]
    local_hidden = up_weight.shape[1]
    head_count = local_cols // HEAD_DIM
    score_scale = HEAD_DIM ** (-0.5)
    block_len = block_rows(shard_rows, SHORT)
    my_ids = lax.dynamic_slice_in_dim(image_ids, tensor_rank * local_rows, local_rows)
    one_hot = (my_ids[:, None] == jnp.arange(slot_count, dtype=jnp.int32)[None, :]).astype(
        jnp.float32
    )
    cond_float = condition.astype(jnp.float32)
    silu_cond, silu_back = jax.vjp(jax.nn.silu, cond_float)
    silu_low = silu_cond.astype(jnp.bfloat16)
    modulation = jnp.dot(
        silu_low, ada_weight, preferred_element_type=jnp.float32
    ) + ada_bias.astype(jnp.float32)
    per_token = jnp.dot(one_hot, modulation, precision=highest, preferred_element_type=jnp.float32)
    shift_one, scale_one, gate_one, shift_two, scale_two, gate_two = jnp.split(per_token, 6, axis=1)
    resid = tokens_in.astype(jnp.float32)
    normed_one, inv_one = layer_norm(resid)
    attn_in = (normed_one * (1.0 + scale_one) + shift_one).astype(jnp.bfloat16)
    attn_all = lax.all_gather(attn_in, "tensor", axis=0, tiled=True)
    qkv_flat_weight = qkv_weight.reshape(model_width, 3 * local_cols)
    qkv_flat = jnp.dot(attn_all, qkv_flat_weight, preferred_element_type=jnp.float32)
    bias_float = qv_bias.astype(jnp.float32)
    queries = (
        (qkv_flat[:, :local_cols] + bias_float[0])
        .astype(jnp.bfloat16)
        .reshape(shard_rows, head_count, HEAD_DIM)
    )
    key_rows = (
        qkv_flat[:, local_cols : 2 * local_cols]
        .astype(jnp.bfloat16)
        .reshape(shard_rows, head_count, HEAD_DIM)
    )
    values = (
        (qkv_flat[:, 2 * local_cols :] + bias_float[1])
        .astype(jnp.bfloat16)
        .reshape(shard_rows, head_count, HEAD_DIM)
    )
    attended, log_sums = attention_forward(
        queries, key_rows, values, image_ids, block_len, score_scale
    )
    attended = attended.reshape(shard_rows, local_cols)
    attn_branch = lax.psum_scatter(
        jnp.dot(attended, out_weight, preferred_element_type=jnp.float32).astype(jnp.bfloat16),
        "tensor",
        scatter_dimension=0,
        tiled=True,
    ).astype(jnp.float32) + out_bias.astype(jnp.float32)
    mid = resid + gate_one * attn_branch
    normed_two, inv_two = layer_norm(mid)
    mlp_in = (normed_two * (1.0 + scale_two) + shift_two).astype(jnp.bfloat16)
    mlp_all = lax.all_gather(mlp_in, "tensor", axis=0, tiled=True)
    pre_act = jnp.dot(mlp_all, up_weight, preferred_element_type=jnp.float32) + up_bias.astype(
        jnp.float32
    )
    act_value, act_back = jax.vjp(gelu_tanh, pre_act)
    hidden = act_value.astype(jnp.bfloat16)
    mlp_branch = lax.psum_scatter(
        jnp.dot(hidden, down_weight, preferred_element_type=jnp.float32).astype(jnp.bfloat16),
        "tensor",
        scatter_dimension=0,
        tiled=True,
    ).astype(jnp.float32) + down_bias.astype(jnp.float32)
    block_value = mid + gate_two * mlp_branch
    block_low = block_value.astype(jnp.bfloat16)
    first_pre = jnp.dot(
        block_low, proj_in, preferred_element_type=jnp.float32
    ) + proj_in_bias.astype(jnp.float32)
    first_value, first_back = jax.vjp(jax.nn.silu, first_pre)
    first_low = first_value.astype(jnp.bfloat16)
    second_pre = jnp.dot(
        first_low, proj_mid, preferred_element_type=jnp.float32
    ) + proj_mid_bias.astype(jnp.float32)
    second_value, second_back = jax.vjp(jax.nn.silu, second_pre)
    second_low = second_value.astype(jnp.bfloat16)
    projected = jnp.dot(
        second_low, proj_last, preferred_element_type=jnp.float32
    ) + proj_last_bias.astype(jnp.float32)
    target_vals = jnp.take(enc_features, target_rows - data_rank * shard_rows, axis=0).astype(
        jnp.float32
    )
    loss_value, loss_back = jax.vjp(lambda predicted: align_loss(predicted, target_vals), projected)
    grad_projected = loss_back(jnp.ones((), jnp.float32))[0]
    grad_last_low = grad_projected.astype(jnp.bfloat16)
    grad_second = second_back(dot_nt(grad_last_low, proj_last))[0]
    grad_second_low = grad_second.astype(jnp.bfloat16)
    grad_first = first_back(dot_nt(grad_second_low, proj_mid))[0]
    grad_first_low = grad_first.astype(jnp.bfloat16)
    grad_block = out_grad.astype(jnp.float32) + dot_nt(grad_first_low, proj_in)
    gate_two_grad = mlp_branch * grad_block
    grad_mlp_branch = gate_two * grad_block
    grad_mlp_all = lax.all_gather(
        grad_mlp_branch.astype(jnp.bfloat16), "tensor", axis=0, tiled=True
    )
    grad_down_local = dot_tn(hidden, grad_mlp_all)
    grad_pre = act_back(dot_nt(grad_mlp_all, down_weight))[0]
    grad_pre_low = grad_pre.astype(jnp.bfloat16)
    grad_up_local = dot_tn(mlp_all, grad_pre_low)
    up_bias_local = jnp.sum(grad_pre, axis=0)
    grad_mlp_in = lax.psum_scatter(
        dot_nt(grad_pre_low, up_weight).astype(jnp.bfloat16),
        "tensor",
        scatter_dimension=0,
        tiled=True,
    ).astype(jnp.float32)
    scale_two_grad = grad_mlp_in * normed_two
    grad_mid = grad_block + norm_back(normed_two, inv_two, grad_mlp_in * (1.0 + scale_two))
    gate_one_grad = attn_branch * grad_mid
    grad_attn_branch = gate_one * grad_mid
    grad_attn_all = lax.all_gather(
        grad_attn_branch.astype(jnp.bfloat16), "tensor", axis=0, tiled=True
    )
    grad_out_local = dot_tn(attended, grad_attn_all)
    grad_heads = (
        dot_nt(grad_attn_all, out_weight)
        .astype(jnp.bfloat16)
        .reshape(shard_rows, head_count, HEAD_DIM)
    )
    grad_queries, grad_keys, grad_values = attention_backward(
        queries, key_rows, values, image_ids, log_sums, grad_heads, block_len, score_scale
    )
    grad_queries = grad_queries.reshape(shard_rows, local_cols)
    grad_keys = grad_keys.reshape(shard_rows, local_cols)
    grad_values = grad_values.reshape(shard_rows, local_cols)
    qv_local = jnp.stack([jnp.sum(grad_queries, axis=0), jnp.sum(grad_values, axis=0)])
    grad_qkv_low = jnp.concatenate([grad_queries, grad_keys, grad_values], axis=1).astype(
        jnp.bfloat16
    )
    grad_qkv_local = dot_tn(attn_all, grad_qkv_low).reshape(model_width, 3, local_cols)
    grad_attn_in = lax.psum_scatter(
        dot_nt(grad_qkv_low, qkv_flat_weight).astype(jnp.bfloat16),
        "tensor",
        scatter_dimension=0,
        tiled=True,
    ).astype(jnp.float32)
    scale_one_grad = grad_attn_in * normed_one
    grad_tokens = grad_mid + norm_back(normed_one, inv_one, grad_attn_in * (1.0 + scale_one))
    token_mod_grad = jnp.concatenate(
        [grad_attn_in, scale_one_grad, gate_one_grad, grad_mlp_in, scale_two_grad, gate_two_grad],
        axis=1,
    )
    slot_grad_part = dot_tn(one_hot, token_mod_grad, precision=highest)
    slot_grad = lax.psum(slot_grad_part.astype(jnp.bfloat16), "tensor").astype(jnp.float32)
    slot_low = slot_grad.astype(jnp.bfloat16)
    grad_condition = silu_back(dot_nt(slot_low, ada_weight))[0]
    ada_cols = dot_tn(silu_low, column_set(slot_low, data_count, tensor_count, tensor_rank))
    ada_bias_cols = jnp.sum(
        column_set(slot_grad, data_count, tensor_count, tensor_rank), axis=0, keepdims=True
    )
    block_grads = (
        lax.psum_scatter(
            grad_qkv_local.astype(jnp.bfloat16), "dp", scatter_dimension=0, tiled=True
        ).astype(jnp.float32),
        lax.psum_scatter(
            grad_out_local.astype(jnp.bfloat16), "dp", scatter_dimension=1, tiled=True
        ).astype(jnp.float32),
        lax.psum_scatter(
            grad_up_local.astype(jnp.bfloat16), "dp", scatter_dimension=0, tiled=True
        ).astype(jnp.float32),
        lax.psum_scatter(
            grad_down_local.astype(jnp.bfloat16), "dp", scatter_dimension=1, tiled=True
        ).astype(jnp.float32),
        lax.psum_scatter(
            ada_cols.astype(jnp.bfloat16), "dp", scatter_dimension=1, tiled=True
        ).astype(jnp.float32),
        lax.psum_scatter(
            ada_bias_cols.astype(jnp.bfloat16), "dp", scatter_dimension=1, tiled=True
        ).astype(jnp.float32),
    )
    qv_full = lax.dynamic_update_slice_in_dim(
        jnp.zeros((2, model_width), jnp.float32), qv_local, tensor_rank * local_cols, axis=1
    )
    up_full = lax.dynamic_update_slice_in_dim(
        jnp.zeros((local_hidden * tensor_count,), jnp.float32),
        up_bias_local,
        tensor_rank * local_hidden,
        axis=0,
    )
    bias_sums = lax.psum(
        (
            qv_full,
            up_full,
            jnp.sum(grad_attn_branch, axis=0),
            jnp.sum(grad_mlp_branch, axis=0),
            jnp.sum(grad_first, axis=0),
            jnp.sum(grad_second, axis=0),
            jnp.sum(grad_projected, axis=0),
        ),
        ("dp", "tensor"),
    )
    qv_grad = lax.dynamic_slice_in_dim(bias_sums[0], tensor_rank * local_cols, local_cols, axis=1)
    up_bias_grad = lax.dynamic_slice_in_dim(
        bias_sums[1], tensor_rank * local_hidden, local_hidden, axis=0
    )
    proj_grads = (
        lax.psum_scatter(
            dot_tn(block_low, grad_first_low), ("dp", "tensor"), scatter_dimension=1, tiled=True
        ),
        lax.psum_scatter(
            dot_tn(first_low, grad_second_low), ("dp", "tensor"), scatter_dimension=1, tiled=True
        ),
        lax.psum_scatter(
            dot_tn(second_low, grad_last_low), ("dp", "tensor"), scatter_dimension=1, tiled=True
        ),
    )
    return (
        block_low,
        grad_tokens,
        grad_condition,
        block_grads[4],
        block_grads[5].reshape(-1),
        block_grads[0],
        qv_grad,
        block_grads[1],
        bias_sums[2],
        block_grads[2],
        up_bias_grad,
        block_grads[3],
        bias_sums[3],
        proj_grads[0],
        bias_sums[4],
        proj_grads[1],
        bias_sums[5],
        proj_grads[2],
        bias_sums[6],
    )


def solution(mesh):
    in_specs = (
        P(("dp", "tensor"), None),
        P("dp", None),
        P(),
        P(),
        P(None, None, "tensor"),
        P(None, "tensor"),
        P("tensor", None),
        P(),
        P(None, "tensor"),
        P("tensor"),
        P("tensor", None),
        P(),
        P(),
        P(),
        P(),
        P(),
        P(),
        P(),
        P("dp", None),
        P("dp"),
        P(("dp", "tensor")),
        P(("dp", "tensor"), None),
    )
    out_specs = (
        P(("dp", "tensor"), None),
        P(("dp", "tensor"), None),
        P("dp", None),
        P(None, ("dp", "tensor")),
        P(("dp", "tensor")),
        P("dp", None, "tensor"),
        P(None, "tensor"),
        P("tensor", "dp"),
        P(),
        P("dp", "tensor"),
        P("tensor"),
        P("tensor", "dp"),
        P(),
        P(None, ("dp", "tensor")),
        P(),
        P(None, ("dp", "tensor")),
        P(),
        P(None, ("dp", "tensor")),
        P(),
    )
    return jax.shard_map(shards, mesh=mesh, in_specs=in_specs, out_specs=out_specs, check_vma=False)
```

profile of v0, /device:TPU:0, one launch (start us, length us, event | category | flops | bytes accessed | tf_op | source)
XLA Modules:
  0.0 2050.4 jit_solution(1787245910555877220)
XLA Ops:
  41.1 49.7 %all-gather.5.cloned.1.call-done = bf16[1536,1152]{1,0:T(8,128)(2,1)} async-done(((bf16[768,1152]{1,0:T(8,128)(2,1)}), bf16[1536,1152]{1,0:T(8,128)(2,1)}) %all-gather.5.cloned.1.call-update) | async-done | bytes 3538960 | tf_op jit(solution)/shard_map/all_gather | solution.py:235
  156.3 26.1 %fusion.8 = (bf16[8,768,1536]{1,2,0:T(8,128)(2,1)}, bf16[8,768,1536]{1,2,0:T(8,128)(2,1)}) fusion(f32[8,768]{1,0:T(8,128)S(1)} %log_add_fusion.1, f32[8,768,768]{1,2,0:T(8,128)} %copy-done.6, f32[8,768,768]{1,2,0:T(8,128)} %get-tuple-element.177, f32[8,768]{1,0:T(8,128)S(1)} %fusion.4, f32[8,768]{1,0:T(8,128)S(1)} %reduce_max.48), kind=kLoop, calls=%fused_computation.21 | loop fusion | flops 56623104 | bytes 75571200 | tf_op jit(solution)/shard_map/convert_element_type | solution.py:147
  182.4 26.4 %fusion.11 = (bf16[8,768,1536]{1,2,0:T(8,128)(2,1)}, bf16[8,768,1536]{1,2,0:T(8,128)(2,1)}) fusion(f32[8,768]{1,0:T(8,128)S(1)} %log_add_fusion, f32[8,768,768]{1,2,0:T(8,128)} %copy-done.5, f32[8,768,768]{1,2,0:T(8,128)} %get-tuple-element.173, f32[8,768]{1,0:T(8,128)S(1)} %fusion.5, f32[8,768]{1,0:T(8,128)S(1)} %reduce_max.51), kind=kLoop, calls=%fused_computation.22 | loop fusion | flops 56623104 | bytes 75571200 | tf_op jit(solution)/shard_map/convert_element_type | solution.py:147
  235.0 47.8 %reduce-scatter.20.cloned.1.call-done = bf16[768,1152]{1,0:T(8,128)(2,1)} async-done(((bf16[1536,1152]{1,0:T(8,128)(2,1)}), bf16[768,1152]{1,0:T(8,128)(2,1)}) %reduce-scatter.20.cloned.1.call-update) | async-done | bytes 1769488 | tf_op jit(solution)/shard_map/reduce_scatter | solution.py:258
  294.4 49.2 %all-gather.7.cloned.1.call-done = bf16[1536,1152]{1,0:T(8,128)(2,1)} async-done(((bf16[768,1152]{1,0:T(8,128)(2,1)}), bf16[1536,1152]{1,0:T(8,128)(2,1)}) %all-gather.7.cloned.1.call-update) | async-done | bytes 3538960 | tf_op jit(solution)/shard_map/all_gather | solution.py:267
  361.7 15.8 convolution_convert_fusion.8
  386.6 38.7 %reduce-scatter.22.cloned.1.call-done = bf16[768,1152]{1,0:T(8,128)(2,1)} async-done(((bf16[1536,1152]{1,0:T(8,128)(2,1)}), bf16[768,1152]{1,0:T(8,128)(2,1)}) %reduce-scatter.22.cloned.1.call-update) | async-done | bytes 1769488 | tf_op jit(solution)/shard_map/reduce_scatter | solution.py:273
  479.2 49.5 %all-gather.9.cloned.1.call-done = bf16[1536,1152]{1,0:T(8,128)(2,1)} async-done(((bf16[768,1152]{1,0:T(8,128)(2,1)}), bf16[1536,1152]{1,0:T(8,128)(2,1)}) %all-gather.9.cloned.1.call-update) | async-done | bytes 3538960 | tf_op jit(solution)/shard_map/all_gather | solution.py:307
  528.7 22.1 %fusion.158 = (f32[2304]{0:T(1024)}, bf16[1536,2304]{1,0:T(8,128)(2,1)S(1)}) fusion(f32[1536,2304]{1,0:T(8,128)} %copy-done.101, bf16[1536,1152]{1,0:T(8,128)(2,1)} %all-gather.9.cloned.1.call-done, bf16[2304,1152]{1,0:T(8,128)(2,1)} %param.48), kind=kOutput, calls=%fused_computation.241 | convolution fusion | flops 8228042752 | bytes 30090240 | tf_op jit(solution)/shard_map/dot_general | solution.py:17
  567.2 47.8 %reduce-scatter.24.cloned.1.call-done = bf16[768,1152]{1,0:T(8,128)(2,1)} async-done(((bf16[1536,1152]{1,0:T(8,128)(2,1)}), bf16[768,1152]{1,0:T(8,128)(2,1)}) %reduce-scatter.24.cloned.1.call-update) | async-done | bytes 1769488 | tf_op jit(solution)/shard_map/reduce_scatter | solution.py:315
  628.3 49.1 %all-gather.11.cloned.1.call-done = bf16[1536,1152]{1,0:T(8,128)(2,1)} async-done(((bf16[768,1152]{1,0:T(8,128)(2,1)}), bf16[1536,1152]{1,0:T(8,128)(2,1)}) %all-gather.11.cloned.1.call-update) | async-done | bytes 3538960 | tf_op jit(solution)/shard_map/all_gather | solution.py:325
  729.4 54.6 %multiply_convert_fusion.1 = bf16[8,768,1536]{1,2,0:T(8,128)(2,1)} fusion(f32[8,768,768]{1,2,0:T(8,128)} %fusion.176, f32[8,768,768]{1,2,0:T(8,128)} %fusion.175, f32[8,768]{1,0:T(8,128)S(1)} %copy-done.63, f32[8,768,768]{1,2,0:T(8,128)} %copy-done.6, f32[8,768,768]{1,2,0:T(8,128)} %get-tuple-element.177), kind=kOutput, calls=%fused_computation.11 | output fusion | flops 94379520 | bytes 94396416 | tf_op jit(solution)/shard_map/sub | solution.py:146
  818.0 55.2 %multiply_convert_fusion = bf16[8,768,1536]{1,2,0:T(8,128)(2,1)} fusion(f32[8,768,768]{1,2,0:T(8,128)} %fusion.178, f32[8,768,768]{1,2,0:T(8,128)} %fusion.177, f32[8,768]{1,0:T(8,128)S(1)} %copy-done.61, f32[8,768,768]{1,2,0:T(8,128)} %copy-done.5, f32[8,768,768]{1,2,0:T(8,128)} %get-tuple-element.173), kind=kOutput, calls=%fused_computation.7 | output fusion | flops 94379520 | bytes 94396416 | tf_op jit(solution)/shard_map/sub | solution.py:146
  915.5 47.8 %reduce-scatter.26.cloned.1.call-done = bf16[768,1152]{1,0:T(8,128)(2,1)} async-done(((bf16[1536,1152]{1,0:T(8,128)(2,1)}), bf16[768,1152]{1,0:T(8,128)(2,1)}) %reduce-scatter.26.cloned.1.call-update) | async-done | bytes 1769488 | tf_op jit(solution)/shard_map/reduce_scatter | solution.py:345
  992.0 16.2 convolution_convert_fusion.1
  1008.3 14.4 convolution_convert_fusion.2
  1099.4 80.4 %reduce-scatter.28.cloned.1.call-done = bf16[72,2304]{1,0:T(8,128)(2,1)} async-done(((bf16[1152,2304]{1,0:T(8,128)(2,1)}), bf16[72,2304]{1,0:T(8,128)(2,1)}) %reduce-scatter.28.cloned.1.call-update) | async-done | bytes 331792 | tf_op jit(solution)/shard_map/reduce_scatter | solution.py:372
  1184.1 56.9 %reduce-scatter.42.cloned.1.call-done = bf16[576,72]{0,1:T(8,128)(2,1)} async-done(((bf16[576,1152]{0,1:T(8,128)(2,1)}), bf16[576,72]{0,1:T(8,128)(2,1)}) %reduce-scatter.42.cloned.1.call-update) | async-done | bytes 82960
  1242.6 73.5 %reduce-scatter.38.cloned.1.call-done = bf16[72,1728]{1,0:T(8,128)(2,1)} async-done(((bf16[1152,1728]{1,0:T(8,128)(2,1)}), bf16[72,1728]{1,0:T(8,128)(2,1)}) %reduce-scatter.38.cloned.1.call-update) | async-done | bytes 248848
  1318.0 41.7 %all-reduce.3 = (f32[2,1152]{1,0:T(2,128)S(1)}, f32[1152]{0:T(1024)}, f32[4608]{0:T(1024)S(1)}, f32[1152]{0:T(1024)}, f32[2048]{0:T(1024)}, /*index=5*/f32[2048]{0:T(1024)}, f32[768]{0:T(1024)}) all-reduce(f32[2,1152]{1,0:T(2,128)S(1)} %dynamic_update_slice.6, ...), channel_id=1, replica_groups=mesh['dp'=16,'tensor'=2] {'dp','tensor'}, use_global_device_ids=true, to_apply=%region_31.32 | all-reduce | flops 14080 | bytes 112640 | tf_op jit(solution)/shard_map/psum | solution.py:394
  1361.4 62.2 %all-reduce.1 = bf16[1,3456]{1,0:T(2,128)(2,1)S(1)} all-reduce(bf16[1,3456]{1,0:T(2,128)(2,1)S(1)} %convert_element_type.244), channel_id=7, replica_groups=mesh['dp'=16,'tensor'=2] {'dp'}, use_global_device_ids=true, to_apply=%region_26.27.clone | all-reduce | flops 3456 | bytes 13824
  1436.9 106.1 %reduce-scatter.36.cloned.1.call-done = f32[2048,24]{0,1:T(8,128)} async-done(((f32[2048,768]{0,1:T(8,128)}), f32[2048,24]{0,1:T(8,128)}) %reduce-scatter.36.cloned.1.call-update) | async-done | bytes 196624 | tf_op jit(solution)/shard_map/reduce_scatter | solution.py:417
  1543.0 141.2 %reduce-scatter.32.cloned.1.call-done = f32[1152,64]{0,1:T(8,128)} async-done(((f32[1152,2048]{0,1:T(8,128)}), f32[1152,64]{0,1:T(8,128)}) %reduce-scatter.32.cloned.1.call-update) | async-done | bytes 294928 | tf_op jit(solution)/shard_map/reduce_scatter | solution.py:411
  1684.2 359.2 %reduce-scatter.34.cloned.1.call-done = f32[2048,64]{0,1:T(8,128)} async-done(((f32[2048,2048]{0,1:T(8,128)}), f32[2048,64]{0,1:T(8,128)}) %reduce-scatter.34.cloned.1.call-update) | async-done | bytes 524304 | tf_op jit(solution)/shard_map/reduce_scatter | solution.py:414
  (399 shorter events, 502.4 us)
Async XLA Ops:
  7.2 439.2 %copy-start = (bf16[2048,768]{1,0:T(8,128)(2,1)S(1)}, bf16[2048,768]{1,0:T(8,128)(2,1)}, u32[]{:S(2)}) copy-start(bf16[2048,768]{1,0:T(8,128)(2,1)} %param.54) | copy-start | bytes 9437188
  7.2 83.6 %all-gather.5.cloned.1.call-start = ((), (), s32[]{:S(2)}) async-start(), calls=%async_computation.12 | async-start | bytes 5308416 | tf_op jit(solution)/shard_map/all_gather | solution.py:235
  38.6 244.1 %reduce-scatter.20.cloned.1.call-start = ((), (), s32[]{:S(2)}) async-start(), calls=%async_computation.13 | async-start | bytes 5308416 | tf_op jit(solution)/shard_map/reduce_scatter | solution.py:258
  234.9 108.7 %all-gather.7.cloned.1.call-start = ((), (), s32[]{:S(2)}) async-start(), calls=%async_computation.14 | async-start | bytes 5308416 | tf_op jit(solution)/shard_map/all_gather | solution.py:267
  294.1 131.2 %reduce-scatter.22.cloned.1.call-start = ((), (), s32[]{:S(2)}) async-start(), calls=%async_computation.15 | async-start | bytes 5308416 | tf_op jit(solution)/shard_map/reduce_scatter | solution.py:273
  377.5 151.2 %all-gather.9.cloned.1.call-start = ((), (), s32[]{:S(2)}) async-start(), calls=%async_computation.16 | async-start | bytes 5308416 | tf_op jit(solution)/shard_map/all_gather | solution.py:307
  479.2 135.8 %reduce-scatter.24.cloned.1.call-start = ((), (), s32[]{:S(2)}) async-start(), calls=%async_computation.17 | async-start | bytes 5308416 | tf_op jit(solution)/shard_map/reduce_scatter | solution.py:315
  567.1 110.3 %all-gather.11.cloned.1.call-start = ((), (), s32[]{:S(2)}) async-start(), calls=%async_computation.18 | async-start | bytes 5308416 | tf_op jit(solution)/shard_map/all_gather | solution.py:325
  627.9 335.4 %reduce-scatter.26.cloned.1.call-start = ((), (), s32[]{:S(2)}) async-start(), calls=%async_computation.19 | async-start | bytes 5308416 | tf_op jit(solution)/shard_map/reduce_scatter | solution.py:345
  915.5 135.1 %all-reduce.6.cloned.1.call-start = ((), (), s32[]{:S(2)}) async-start(), calls=%async_computation.20 | async-start | bytes 221184 | tf_op jit(solution)/shard_map/psum | solution.py:358
  992.0 105.6 %reduce-scatter.30.cloned.1.call-start = ((), (), s32[]{:S(2)}) async-start(), calls=%async_computation.22 | async-start | bytes 5640192 | tf_op jit(solution)/shard_map/reduce_scatter | solution.py:375
  1008.2 171.6 %reduce-scatter.28.cloned.1.call-start = ((), (), s32[]{:S(2)}) async-start(), calls=%async_computation.21 | async-start | bytes 5640192 | tf_op jit(solution)/shard_map/reduce_scatter | solution.py:372
  1022.7 218.3 %reduce-scatter.42.cloned.1.call-start = ((), (), s32[]{:S(2)}) async-start(), calls=%async_computation.28 | async-start | bytes 1566720
  1030.5 285.5 %reduce-scatter.38.cloned.1.call-start = ((), (), s32[]{:S(2)}) async-start(), calls=%async_computation.26 | async-start | bytes 4386816
  1050.5 384.3 %reduce-scatter.40.cloned.1.call-start = ((), (), s32[]{:S(2)}) async-start(), calls=%async_computation.27 | async-start | bytes 8460288
  1057.6 485.4 %reduce-scatter.36.cloned.1.call-start = ((), (), s32[]{:S(2)}) async-start(), calls=%async_computation.25 | async-start | bytes 6488064 | tf_op jit(solution)/shard_map/reduce_scatter | solution.py:417
  1066.9 617.4 %reduce-scatter.32.cloned.1.call-start = ((), (), s32[]{:S(2)}) async-start(), calls=%async_computation.23 | async-start | bytes 9732096 | tf_op jit(solution)/shard_map/reduce_scatter | solution.py:411
  1078.2 965.2 %reduce-scatter.34.cloned.1.call-start = ((), (), s32[]{:S(2)}) async-start(), calls=%async_computation.24 | async-start | bytes 17301504 | tf_op jit(solution)/shard_map/reduce_scatter | solution.py:414
  1092.8 88.9 %copy-start.70 = (f32[8,72]{1,0:T(8,128)S(1)}, f32[8,72]{1,0:T(8,128)}, u32[]{:S(2)}) copy-start(f32[8,72]{1,0:T(8,128)} %get-tuple-element.153) | copy-start | bytes 6916
  1092.8 88.9 %copy-start.30 = (f32[8,72,768]{2,1,0:T(8,128)S(1)}, f32[8,72,768]{2,1,0:T(8,128)}, u32[]{:S(2)}) copy-start(f32[8,72,768]{2,1,0:T(8,128)} %get-tuple-element.186) | copy-start | bytes 5308420
  1097.2 220.9 %copy-start.80 = (f32[2048]{0:T(1024)S(1)}, f32[2048]{0:T(1024)}, u32[]{:S(2)}) copy-start(f32[2048]{0:T(1024)} %get-tuple-element.191) | copy-start | bytes 24580
  1097.2 220.9 %copy-start.81 = (f32[2048]{0:T(1024)S(1)}, f32[2048]{0:T(1024)}, u32[]{:S(2)}) copy-start(f32[2048]{0:T(1024)} %get-tuple-element.189) | copy-start | bytes 24580
  1097.2 327.1 %copy-start.48 = (bf16[6,6912]{1,0:T(8,128)(2,1)S(1)}, bf16[6,6912]{1,0:T(8,128)(2,1)}, u32[]{:S(2)}) copy-start(bf16[6,6912]{1,0:T(8,128)(2,1)} %all-reduce.6.cloned.1.call-done) | copy-start | bytes 248836
  1424.3 619.1 %copy-start.1 = (bf16[2048,768]{1,0:T(8,128)(2,1)S(1)}, bf16[2048,768]{1,0:T(8,128)(2,1)}, u32[]{:S(2)}) copy-start(bf16[2048,768]{1,0:T(8,128)(2,1)} %param.54) | copy-start | bytes 9437188
  (108 other events, 1538.1 us)
Sparse Core Ops, SparseCore 0:
  38.8 52.0 all-gather.4
  235.1 47.6 reduce-scatter.19
  294.2 49.3 all-gather.6
  377.6 47.6 reduce-scatter.21
  479.3 49.3 all-gather.8
  567.2 47.6 reduce-scatter.23
  628.0 49.3 all-gather.10
  915.6 47.6 reduce-scatter.25
  992.1 21.1 all-reduce.5
  1017.2 79.8 reduce-scatter.29
  1101.2 78.6 reduce-scatter.27
  1183.4 57.5 reduce-scatter.41
  1244.9 71.0 reduce-scatter.37
  1320.0 101.4 reduce-scatter.39
  1428.5 114.4 reduce-scatter.35
  1549.3 134.8 reduce-scatter.31
  1687.0 356.3 reduce-scatter.33
where the time goes:
time: 2060 us; the launch traced here: 2050 us
  waiting for transfers between devices  1200 us (58%)
  matrix products  409 us (20%)
  other arithmetic  253 us (12%)
  blocking collectives  104 us (5%)
  local copies, waits for them, and re-layouts  69.9 us (3%)
    reduce_scatter x1, waiting for transfers between devices, shards(): lax.psum_scatter(dot_tn(first_low, grad_second_low), ('dp', 'tensor'), sc...  359 us
    reduce_scatter x1, waiting for transfers between devices, shards(): lax.psum_scatter(dot_tn(block_low, grad_first_low), ('dp', 'tensor'), sca...  141 us
    unnamed x20, waiting for transfers between devices  131 us
    sub x2, other arithmetic, attention_backward(): grad_scores = (soft * (grad_soft - inner)).astype(jnp.bfloat16)  110 us
    reduce_scatter x1, waiting for transfers between devices, shards(): lax.psum_scatter(dot_tn(second_low, grad_last_low), ('dp', 'tensor'), sca...  106 us
    dot_general x9, matrix products, dot_tn(): lax.dot_general(left_arg, right_arg, (((0,), (0,)), ((), ())), precision=...  95.2 us
    dot_general x8, matrix products, dot_nt(): lax.dot_general(left_arg, right_arg, (((1,), (1,)), ((), ())), preferred_...  88.5 us
    reduce_scatter x1, waiting for transfers between devices, shards(): lax.psum_scatter(grad_up_local.astype(jnp.bfloat16), 'dp', scatter_dimens...  80.4 us
  transfers between devices with their start and end apart: 17, of which 14 were waited for; matrix products, arithmetic and copies ran while one was open for 7% of the time, Pallas kernels for 0%

commit v1 on v0

--- a/solution.py
+++ b/solution.py
@@ -1,6 +1,10 @@
+import functools
+
 import jax
 import jax.numpy as jnp
 from jax import lax
+from jax.experimental import pallas as pl
+from jax.experimental.pallas import tpu as pltpu
 from jax.sharding import PartitionSpec as P
 
 HEAD_DIM = 72
@@ -441,6 +445,526 @@
     )
 
 
+LANES = 128
+MESH = pl.DeviceIdType.MESH
+bf16 = jnp.bfloat16
+f32 = jnp.float32
+
+
+def pairs_of(move):
+    found = []
+    for index in range(32):
+        x, core, y, z = index % 2, (index // 2) % 2, (index // 4) % 2, index // 8
+        z2, y2, c2, x2 = move(z, y, core, x)
+        if (z2, y2, c2, x2) != (z, y, core, x):
+            found.append((index, ((z2 * 2 + y2) * 2 + c2) * 2 + x2))
+    return found
+
+
+def send(value, move):
+    return lax.ppermute(value, ("dp", "tensor"), pairs_of(move))
+
+
+def to_diag(z, y, c, x):
+    return (z, y, x, c)
+
+
+def to_cycle(z, y, c, x):
+    return (z, y, c, c) if c != x else (z, y, 1 - c, x)
+
+
+def to_core(z, y, c, x):
+    return (z, y, 1 - c, x)
+
+
+def to_x(z, y, c, x):
+    return (z, y, c, 1 - x)
+
+
+def to_y(z, y, c, x):
+    return (z, 1 - y, c, x)
+
+
+def to_z_near(z, y, c, x):
+    return (z ^ 1, y, c, x)
+
+
+def to_z_far(z, y, c, x):
+    return (z ^ 2, y, c, x)
+
+
+def pick(array, index, axis):
+    return lax.dynamic_index_in_dim(array, index, axis=axis, keepdims=False)
+
+
+def halve(array, axis, bit, move):
+    got = send(pick(array, 1 - bit, axis), move)
+    kept = pick(array, bit, axis)
+    return (kept.astype(f32) + got.astype(f32)).astype(bf16)
+
+
+def gather_kernel(own_ref, out_ref, local_sem, send_sem, recv_sem):
+    dp = lax.axis_index("dp")
+    x = lax.axis_index("tensor")
+    core = dp % 2
+    other = dp + 1 - 2 * core
+    barrier = pltpu.get_barrier_semaphore()
+    pl.semaphore_signal(barrier, inc=1, device_id=(other, x), device_id_type=MESH)
+    pl.semaphore_wait(barrier, 1)
+    away = pltpu.make_async_remote_copy(
+        src_ref=own_ref,
+        dst_ref=out_ref.at[core],
+        send_sem=send_sem,
+        recv_sem=recv_sem,
+        device_id=(other, x),
+        device_id_type=MESH,
+    )
+    away.start()
+    here = pltpu.make_async_copy(own_ref, out_ref.at[core], local_sem)
+    here.start()
+    here.wait()
+    away.wait()
+
+
+def gather_cores(own):
+    rows, width = own.shape
+    return pl.pallas_call(
+        gather_kernel,
+        out_shape=jax.ShapeDtypeStruct((2, rows, width), own.dtype),
+        in_specs=[pl.BlockSpec(memory_space=pltpu.VMEM)],
+        out_specs=pl.BlockSpec(memory_space=pl.ANY),
+        scratch_shapes=[pltpu.SemaphoreType.DMA] * 3,
+        compiler_params=pltpu.CompilerParams(collective_id=0, has_side_effects=True, vmem_limit_bytes=16 << 20),
+        cost_estimate=pl.CostEstimate(flops=0, bytes_accessed=12000000, transcendentals=0),
+        name="gather_cores",
+    )(own).reshape(2 * rows, width)
+
+
+def attend_kernel(factor, starts, counts, q_ref, k_ref, v_ref, o_ref):
+    def unit(index, carry):
+        rows = pl.ds(pl.multiple_of(index * SHORT, SHORT), SHORT)
+
+        def run(length):
+            cols = pl.ds(pl.multiple_of(starts[index] * SHORT, SHORT), length)
+            scores = dot_nt(k_ref[cols, :], q_ref[rows, :])
+            top = jnp.max(scores, axis=0, keepdims=True)
+            exponent = jnp.exp((scores - top) * factor)
+            total = jnp.sum(exponent, axis=0, keepdims=True)
+            prob_low = (exponent * (1.0 / total)).astype(bf16)
+            summed = dot_tn(v_ref[cols, :], prob_low)
+            o_ref[rows, :] = summed.T.astype(bf16)
+
+        @pl.when(counts[index] == 1)
+        def _():
+            run(SHORT)
+
+        @pl.when(counts[index] != 1)
+        def _():
+            run(4 * SHORT)
+
+        return carry
+
+    lax.fori_loop(0, q_ref.shape[0] // SHORT, unit, 0)
+
+
+def attend(starts, counts, qkv, heads, factor):
+    rows = qkv.shape[0]
+
+    def spec(part):
+        return pl.BlockSpec((rows, LANES), lambda h, *_: (0, part * heads + h))
+
+    return pl.pallas_call(
+        functools.partial(attend_kernel, factor),
+        out_shape=jax.ShapeDtypeStruct((rows, heads * LANES), bf16),
+        grid_spec=pltpu.PrefetchScalarGridSpec(
+            num_scalar_prefetch=2,
+            grid=(heads,),
+            in_specs=[spec(0), spec(1), spec(2)],
+            out_specs=spec(0),
+        ),
+        compiler_params=pltpu.CompilerParams(vmem_limit_bytes=48 << 20),
+        cost_estimate=pl.CostEstimate(flops=20 * 10**9, bytes_accessed=13 * 10**6, transcendentals=10**7),
+        name="attend",
+    )(starts, counts, qkv, qkv, qkv)
+
+
+def attend_back_kernel(
+    factor, starts, counts, q_ref, k_ref, v_ref, g_ref, out_ref, bias_ref, key_acc, value_acc, query_low
+):
+    part = pl.program_id(1)
+    rows_all = q_ref.shape[0]
+
+    @pl.when(part == 0)
+    def _():
+        key_acc[...] = jnp.zeros_like(key_acc)
+        value_acc[...] = jnp.zeros_like(value_acc)
+        bias_ref[...] = jnp.zeros_like(bias_ref)
+
+        def unit(index, carry):
+            rows = pl.ds(pl.multiple_of(index * SHORT, SHORT), SHORT)
+
+            def run(length):
+                cols = pl.ds(pl.multiple_of(starts[index] * SHORT, SHORT), length)
+                queries = q_ref[rows, :]
+                grads = g_ref[rows, :]
+                keys = k_ref[cols, :]
+                scores = dot_nt(keys, queries)
+                top = jnp.max(scores, axis=0, keepdims=True)
+                exponent = jnp.exp((scores - top) * factor)
+                total = jnp.sum(exponent, axis=0, keepdims=True)
+                soft = exponent * (1.0 / total)
+                grad_soft = dot_nt(v_ref[cols, :], grads)
+                inner = jnp.sum(soft * grad_soft, axis=0, keepdims=True)
+                grad_scores = (soft * (grad_soft - inner)).astype(bf16)
+                value_acc[cols, :] += jnp.dot(soft.astype(bf16), grads, preferred_element_type=f32)
+                key_acc[cols, :] += jnp.dot(grad_scores, queries, preferred_element_type=f32)
+                grad_query = dot_tn(keys, grad_scores).T * factor
+                query_low[rows, :] = grad_query.astype(bf16)
+                bias_ref[0:1, :] += jnp.sum(grad_query, axis=0, keepdims=True)
+
+            @pl.when(counts[index] == 1)
+            def _():
+                run(SHORT)
+
+            @pl.when(counts[index] != 1)
+            def _():
+                run(4 * SHORT)
+
+            return carry
+
+        lax.fori_loop(0, rows_all // SHORT, unit, 0)
+        bias_ref[1:2, :] = jnp.sum(value_acc[...], axis=0, keepdims=True)
+        out_ref[...] = query_low[...]
+
+    @pl.when(part == 1)
+    def _():
+        out_ref[...] = (key_acc[...] * factor).astype(bf16)
+
+    @pl.when(part == 2)
+    def _():
+        out_ref[...] = value_acc[...].astype(bf16)
+
+
+def attend_back(starts, counts, qkv, grad_heads, heads, factor):
+    rows = qkv.shape[0]
+
+    def spec(part):
+        return pl.BlockSpec((rows, LANES), lambda h, p, *_: (0, part * heads + h))
+
+    return pl.pallas_call(
+        functools.partial(attend_back_kernel, factor),
+        out_shape=(
+            jax.ShapeDtypeStruct((rows, 3 * heads * LANES), bf16),
+            jax.ShapeDtypeStruct((8, heads * LANES), f32),
+        ),
+        grid_spec=pltpu.PrefetchScalarGridSpec(
+            num_scalar_prefetch=2,
+            grid=(heads, 3),
+            in_specs=[spec(0), spec(1), spec(2), spec(0)],
+            out_specs=(
+                pl.BlockSpec((rows, LANES), lambda h, p, *_: (0, p * heads + h)),
+                pl.BlockSpec((8, LANES), lambda h, p, *_: (0, h)),
+            ),
+            scratch_shapes=[
+                pltpu.VMEM((rows, LANES), f32),
+                pltpu.VMEM((rows, LANES), f32),
+                pltpu.VMEM((rows, LANES), bf16),
+            ],
+        ),
+        compiler_params=pltpu.CompilerParams(vmem_limit_bytes=48 << 20),
+        cost_estimate=pl.CostEstimate(flops=40 * 10**9, bytes_accessed=25 * 10**6, transcendentals=10**7),
+        name="attend_back",
+    )(starts, counts, qkv, qkv, qkv, grad_heads)
+
+
+def after(value, earlier):
+    return lax.optimization_barrier((value, earlier))[0]
+
+
+def paired_shards(
+    tokens_in,
+    condition,
+    ada_weight,
+    ada_bias,
+    qkv_weight,
+    qv_bias,
+    out_weight,
+    out_bias,
+    up_weight,
+    up_bias,
+    down_weight,
+    down_bias,
+    proj_in,
+    proj_in_bias,
+    proj_mid,
+    proj_mid_bias,
+    proj_last,
+    proj_last_bias,
+    enc_features,
+    image_ids,
+    target_rows,
+    out_grad,
+):
+    dp = lax.axis_index("dp")
+    x = lax.axis_index("tensor")
+    core = dp % 2
+    y = (dp // 2) % 2
+    z = dp // 4
+    z_near = z % 2
+    z_far = z // 2
+    place = dp * 2 + x
+    home = core == x
+    group = (dp // 2) * 2 + x
+    local_rows, width = tokens_in.shape
+    shard_rows = image_ids.shape[0]
+    slots = condition.shape[0]
+    units = local_rows // SHORT
+    local_cols = qkv_weight.shape[2]
+    local_hidden = up_weight.shape[1]
+    heads = local_cols // HEAD_DIM
+    padded = heads * LANES
+    factor = HEAD_DIM ** (-0.5)
+
+    def swap(value):
+        return jnp.where(home, value, send(value, to_diag))
+
+    tokens = swap(tokens_in)
+    packed_ids = send(image_ids, to_core)
+    ids = jnp.where(home, image_ids, packed_ids)
+    cond_low = jnp.where(home, condition, send(condition, to_core))
+    qkv_half = swap(after(qkv_weight.reshape(width, 3 * local_cols), tokens))
+    out_half = swap(after(out_weight, qkv_half))
+    up_half = swap(after(up_weight, out_half))
+    down_half = swap(after(down_weight, up_half))
+    features = jnp.where(home, enc_features, send(enc_features, to_core))
+    rows_low = swap(after(target_rows, down_half))
+    grad_out = swap(after(out_grad, down_half))
+    bias_pack = jnp.concatenate([qv_bias.reshape(-1), up_bias])
+    bias_half = swap(bias_pack).astype(f32)
+    qv_half = bias_half[: 2 * local_cols].reshape(2, local_cols)
+    up_bias_half = bias_half[2 * local_cols :]
+
+    unit_ids = ids.reshape(-1, SHORT)[:, 0]
+    same = unit_ids[:, None] == unit_ids[None, :]
+    starts = jnp.argmax(same, axis=1).astype(jnp.int32)
+    counts = jnp.sum(same.astype(jnp.int32), axis=1).astype(jnp.int32)
+    my_units = lax.dynamic_slice_in_dim(unit_ids, core * units, units)
+    one_hot = (my_units[:, None] == jnp.arange(slots, dtype=jnp.int32)[None, :]).astype(f32)
+
+    silu_cond, silu_back = jax.vjp(jax.nn.silu, cond_low.astype(f32))
+    silu_low = silu_cond.astype(bf16)
+    silu_all = lax.dynamic_update_index_in_dim(jnp.zeros((16, slots, width), bf16), silu_low, group, axis=0)
+    for move in (to_x, to_y, to_z_near, to_z_far):
+        silu_all = silu_all + send(silu_all, move)
+    modulation = jnp.dot(silu_low, ada_weight, preferred_element_type=f32) + ada_bias.astype(f32)
+    per_unit = jnp.dot(one_hot, modulation, precision=highest, preferred_element_type=f32)
+    shift_one, scale_one, gate_one, shift_two, scale_two, gate_two = [
+        piece[:, None, :] for piece in jnp.split(per_unit, 6, axis=1)
+    ]
+
+    def by_unit(array):
+        return array.reshape(units, SHORT, -1)
+
+    def flat(array):
+        return array.reshape(local_rows, -1)
+
+    def reduce_cores(left, matrix, product):
+        mine = lax.dynamic_slice_in_dim(left, core * local_rows, local_rows)
+        theirs = lax.dynamic_slice_in_dim(left, (1 - core) * local_rows, local_rows)
+        got = send(product(theirs, matrix).astype(bf16), to_core)
+        return product(mine, matrix).astype(bf16).astype(f32) + got.astype(f32)
+
+    def dot_nn(left, right):
+        return jnp.dot(left, right, preferred_element_type=f32)
+
+    resid = by_unit(tokens.astype(f32))
+    normed_one, inv_one = layer_norm(resid)
+    attn_in = flat((normed_one * (1.0 + scale_one) + shift_one).astype(bf16))
+    attn_all = gather_cores(attn_in)
+
+    def pad_heads(array):
+        lead = array.shape[:-1]
+        shaped = array.reshape(lead + (-1, HEAD_DIM))
+        widths = [(0, 0)] * (len(lead) + 1) + [(0, LANES - HEAD_DIM)]
+        return jnp.pad(shaped, widths).reshape(lead + (-1,))
+
+    qkv_pad = pad_heads(qkv_half)
+    out_pad = jnp.pad(
+        out_half.reshape(heads, HEAD_DIM, width), ((0, 0), (0, LANES - HEAD_DIM), (0, 0))
+    ).reshape(padded, width)
+    qkv_bias = pad_heads(jnp.concatenate([qv_half[0], jnp.zeros_like(qv_half[0]), qv_half[1]]))
+    qkv = (dot_nn(attn_all, qkv_pad) + qkv_bias).astype(bf16)
+    attended = attend(starts, counts, qkv, heads, factor)
+    attn_branch = by_unit(reduce_cores(attended, out_pad, dot_nn) + out_bias.astype(f32))
+    mid = resid + gate_one * attn_branch
+
+    normed_two, inv_two = layer_norm(mid)
+    mlp_in = flat((normed_two * (1.0 + scale_two) + shift_two).astype(bf16))
+    mlp_all = gather_cores(mlp_in)
+    pre_act = dot_nn(mlp_all, up_half) + up_bias_half
+    act_value, act_back = jax.vjp(gelu_tanh, pre_act)
+    hidden = act_value.astype(bf16)
+    mlp_branch = by_unit(reduce_cores(hidden, down_half, dot_nn) + down_bias.astype(f32))
+    block_value = mid + gate_two * mlp_branch
+    block_low = flat(block_value.astype(bf16))
+
+    first_pre = dot_nn(block_low, proj_in) + proj_in_bias.astype(f32)
+    first_value, first_back = jax.vjp(jax.nn.silu, first_pre)
+    first_low = first_value.astype(bf16)
+    second_pre = dot_nn(first_low, proj_mid) + proj_mid_bias.astype(f32)
+    second_value, second_back = jax.vjp(jax.nn.silu, second_pre)
+    second_low = second_value.astype(bf16)
+    projected = dot_nn(second_low, proj_last) + proj_last_bias.astype(f32)
+    target_vals = jnp.take(features, rows_low - group * shard_rows, axis=0).astype(f32)
+    loss_back = jax.vjp(lambda predicted: align_loss(predicted, target_vals), projected)[1]
+    grad_projected = loss_back(jnp.ones((), f32))[0]
+    grad_last_low = grad_projected.astype(bf16)
+    grad_second = second_back(dot_nt(grad_last_low, proj_last))[0]
+    grad_second_low = grad_second.astype(bf16)
+    grad_first = first_back(dot_nt(grad_second_low, proj_mid))[0]
+    grad_first_low = grad_first.astype(bf16)
+    grad_block = by_unit(grad_out.astype(f32) + dot_nt(grad_first_low, proj_in))
+
+    grad_mlp_branch = gate_two * grad_block
+    grad_mlp_all = gather_cores(flat(grad_mlp_branch.astype(bf16)))
+    grad_pre = act_back(dot_nt(grad_mlp_all, down_half))[0]
+    grad_pre_low = grad_pre.astype(bf16)
+    grad_mlp_in = by_unit(reduce_cores(grad_pre_low, up_half, dot_nt))
+    grad_mid = grad_block + norm_back(normed_two, inv_two, grad_mlp_in * (1.0 + scale_two))
+
+    grad_attn_branch = gate_one * grad_mid
+    grad_attn_all = gather_cores(flat(grad_attn_branch.astype(bf16)))
+    grad_heads = dot_nt(grad_attn_all, out_pad).astype(bf16)
+    grad_qkv, qkv_bias_sums = attend_back(starts, counts, qkv, grad_heads, heads, factor)
+    grad_attn_in = by_unit(reduce_cores(grad_qkv, qkv_pad, dot_nt))
+    grad_tokens = grad_mid + norm_back(normed_one, inv_one, grad_attn_in * (1.0 + scale_one))
+
+    def spread(array, rows):
+        return array.reshape(2, 2, 2, 2, rows, array.shape[-1])
+
+    def over_zy(array):
+        array = halve(array, 2, y, to_y)
+        array = halve(array, 1, z_near, to_z_near)
+        return halve(array, 0, z_far, to_z_far)
+
+    def over_pair(array, axis):
+        turned = send(pick(array, 1 - x, axis), to_cycle)
+        straight = swap(pick(array, x, axis))
+        return (turned.astype(f32) + straight.astype(f32)).astype(bf16)
+
+    proj_rows = proj_in.shape[1] // 32
+    grads_in = dot_tn(grad_first_low, block_low).astype(bf16)
+    grads_mid = dot_tn(grad_second_low, first_low).astype(bf16)
+    grads_last = dot_tn(grad_last_low, second_low).astype(bf16)
+
+    def over_all(array):
+        rows = array.shape[0] // 32
+        array = array.reshape(2, 2, 2, 2, 2, rows, array.shape[1])
+        array = halve(array, 3, core, to_core)
+        array = halve(array, 2, y, to_y)
+        array = halve(array, 2, x, to_x)
+        array = halve(array, 1, z_near, to_z_near)
+        return halve(array, 0, z_far, to_z_far)
+
+    near_in = over_all(grads_in)
+    near_mid = over_all(grads_mid)
+    last = over_all(grads_last)
+
+    grads_down = dot_tn(grad_mlp_all, hidden).astype(bf16)
+    grads_up = dot_tn(mlp_all, grad_pre_low).astype(bf16)
+    row_count = width // 16
+    up_sum = over_zy(over_pair(spread(grads_up, row_count), 3))
+    down_sum = over_zy(over_pair(spread(grads_down, row_count), 3))
+
+    grads_out = dot_tn(grad_attn_all, attended).astype(bf16)
+    grads_qkv = dot_tn(attn_all, grad_qkv).astype(bf16)
+
+    def trim(array):
+        return array.reshape(array.shape[:-1] + (-1, LANES))[..., :HEAD_DIM].reshape(array.shape[:-1] + (-1,))
+
+    qkv_sum = over_pair(over_zy(spread(trim(grads_qkv), row_count)), 0)
+    out_sum = over_pair(over_zy(spread(trim(grads_out), row_count)), 0)
+
+    def unit_sum(array):
+        return jnp.sum(array, axis=1)
+
+    mod_units = jnp.concatenate(
+        [
+            unit_sum(grad_attn_in),
+            unit_sum(grad_attn_in * normed_one),
+            unit_sum(attn_branch * grad_mid),
+            unit_sum(grad_mlp_in),
+            unit_sum(grad_mlp_in * normed_two),
+            unit_sum(mlp_branch * grad_block),
+        ],
+        axis=1,
+    )
+    slot_part = dot_tn(one_hot, mod_units, precision=highest)
+    slot_grad = slot_part + send(slot_part, to_core)
+    slot_low = slot_grad.astype(bf16)
+    grad_condition = swap(silu_back(dot_nt(slot_low, ada_weight))[0])
+    mod_cols = slot_low.shape[1] // 32
+    slot_cols = slot_low.reshape(slots, 2, 2, 2, 2, 2, mod_cols)
+    slot_cols = pick(slot_cols, core, 4)
+    slot_mine = lax.dynamic_update_index_in_dim(
+        jnp.zeros((16,) + slot_cols.shape, bf16), slot_cols, group, axis=0
+    )
+    for axis, bit, move in ((5, x, to_x), (4, y, to_y), (3, z_near, to_z_near), (2, z_far, to_z_far)):
+        slot_mine = pick(slot_mine, bit, axis) + send(pick(slot_mine, 1 - bit, axis), move)
+    slot_mine = slot_mine.reshape(16 * slots, mod_cols)
+    grad_ada = dot_tn(silu_all.reshape(16 * slots, width), slot_mine)
+    ada_bias_grad = jnp.sum(slot_mine.astype(f32), axis=0)
+
+    qv_sums = trim(qkv_bias_sums[:2])
+    qv_full = lax.dynamic_update_slice_in_dim(jnp.zeros((2, width), f32), qv_sums, core * local_cols, axis=1)
+    up_full = lax.dynamic_update_slice_in_dim(
+        jnp.zeros((2 * local_hidden,), f32), jnp.sum(grad_pre, axis=0), core * local_hidden, axis=0
+    )
+    pieces = [
+        qv_full.reshape(-1),
+        up_full,
+        jnp.sum(flat(grad_attn_branch), axis=0),
+        jnp.sum(flat(grad_mlp_branch), axis=0),
+        jnp.sum(grad_first, axis=0),
+        jnp.sum(grad_second, axis=0),
+        jnp.sum(grad_projected, axis=0),
+    ]
+    sums = jnp.concatenate(pieces)
+    for move in (to_core, to_x, to_y, to_z_near, to_z_far):
+        sums = sums + send(sums, move)
+    found = []
+    offset = 0
+    for piece in pieces:
+        found.append(sums[offset : offset + piece.shape[0]])
+        offset += piece.shape[0]
+    qv_grad = lax.dynamic_slice_in_dim(found[0].reshape(2, width), x * local_cols, local_cols, axis=1)
+    up_bias_grad = lax.dynamic_slice_in_dim(found[1], x * local_hidden, local_hidden, axis=0)
+
+    block_out = swap(block_low)
+    tokens_out = swap(flat(grad_tokens).astype(bf16))
+    return (
+        block_out,
+        tokens_out.astype(f32),
+        grad_condition,
+        grad_ada,
+        ada_bias_grad,
+        qkv_sum.astype(f32).reshape(row_count, 3, local_cols),
+        qv_grad,
+        out_sum.astype(f32).T,
+        found[2],
+        up_sum.astype(f32),
+        up_bias_grad,
+        down_sum.astype(f32).T,
+        found[3],
+        near_in.astype(f32).T,
+        found[4],
+        near_mid.astype(f32).T,
+        found[5],
+        last.astype(f32).T,
+        found[6],
+    )
+
+
 def solution(mesh):
     in_specs = (
         P(("dp", "tensor"), None),
@@ -487,4 +1011,6 @@
         P(None, ("dp", "tensor")),
         P(),
     )
-    return jax.shard_map(shards, mesh=mesh, in_specs=in_specs, out_specs=out_specs, check_vma=False)
+    paired = mesh.shape["tensor"] == 2 and mesh.shape["dp"] == 16
+    body = paired_shards if paired else shards
+    return jax.shard_map(body, mesh=mesh, in_specs=in_specs, out_specs=out_specs, check_vma=False)

time: 2060 us -> 1090 us (0.53)
  waiting for transfers between devices: 1200 us -> 288 us
  Pallas kernels: 0 us -> 194 us
  other arithmetic: 253 us -> 98.6 us
  matrix products: 409 us -> 258 us
  blocking collectives: 104 us -> 0 us
  starting transfers between devices: 1.72 us -> 99.8 us
  local copies, waits for them, and re-layouts: 69.9 us -> 136 us
    reduce_scatter x9 -> x0, waiting for transfers between devices: 869 us -> none  [the longest x1 359 us: shards(): lax.psum_scatter(dot_tn(first_low, grad_second_low), ('dp', 'tensor'), sc...]
    ppermute x0 -> x67, waiting for transfers between devices: none -> 288 us  [send(): return lax.ppermute(value, ('dp', 'tensor'), pairs_of(move))]
    all_gather x4 -> x0, waiting for transfers between devices: 198 us -> none  [the longest x1 49.7 us: shards(): attn_all = lax.all_gather(attn_in, 'tensor', axis=0, tiled=True)]
    pallas_call x0 -> x6, Pallas kernels: none -> 194 us  [the longest x1 77.1 us: attend_back(): pl.pallas_call(functools.partial(attend_back_kernel, factor), out_shape=(...]
    dot_general x33 -> x11, matrix products: 225 us -> 88.5 us  [the longest x9 80.4 us: dot_nn(): return jnp.dot(left, right, preferred_element_type=f32)]
    unnamed x20 -> x0, waiting for transfers between devices: 131 us -> none
    sub x2 -> x0, other arithmetic: 110 us -> none  [attention_backward(): grad_scores = (soft * (grad_soft - inner)).astype(jnp.bfloat16)]
    ppermute x0 -> x67, starting transfers between devices: none -> 99.8 us  [send(): return lax.ppermute(value, ('dp', 'tensor'), pairs_of(move))]
  transfers between devices with their start and end apart: 17 -> 67, of which waited for: 14 -> 25; matrix products, arithmetic and copies ran while one was open for 7% -> 44% of each run, Pallas kernels for 0% -> 18%
where the time goes in v1:
time: 1090 us; the launch traced here: 1080 us
  waiting for transfers between devices  288 us (26%)
  matrix products  258 us (24%)
  Pallas kernels  194 us (18%)
  local copies, waits for them, and re-layouts  136 us (12%)
  starting transfers between devices  99.8 us (9%)
  other arithmetic  98.6 us (9%)
    ppermute x67, waiting for transfers between devices, send(): return lax.ppermute(value, ('dp', 'tensor'), pairs_of(move))  288 us
    dot_general x10, matrix products, dot_nt(): lax.dot_general(left_arg, right_arg, (((1,), (1,)), ((), ())), preferred_...  102 us
    ppermute x67, starting transfers between devices, send(): return lax.ppermute(value, ('dp', 'tensor'), pairs_of(move))  99.8 us
    dot_general x9, matrix products, dot_nn(): return jnp.dot(left, right, preferred_element_type=f32)  80.4 us
    pallas_call x1, Pallas kernels, attend_back(): pl.pallas_call(functools.partial(attend_back_kernel, factor), out_shape=(...  77.1 us
    pallas_call x4, Pallas kernels, gather_cores(): pl.pallas_call(gather_kernel, out_shape=jax.ShapeDtypeStruct((2, rows, wi...  74 us
    dot_general x9, matrix products, dot_tn(): lax.dot_general(left_arg, right_arg, (((0,), (0,)), ((), ())), precision=...  67.5 us
    pallas_call x1, Pallas kernels, attend(): pl.pallas_call(functools.partial(attend_kernel, factor), out_shape=jax.Sh...  43.2 us
  transfers between devices with their start and end apart: 67, of which 25 were waited for; matrix products, arithmetic and copies ran while one was open for 44% of the time, Pallas kernels for 18%

profile of v1, /device:TPU:0, one launch (start us, length us, event | category | flops | bytes accessed | tf_op | source)
XLA Modules:
  0.0 1077.9 jit_solution(2467355408081404279)
XLA Ops:
  8.6 24.8 %collective-permute-start.1 = (s32[1536]{0:T(1024)S(1)}, s32[1536]{0:T(1024)S(1)}, u32[]{:S(2)}, u32[]{:S(2)}) collective-permute-start(s32[1536]{0:T(1024)S(1)} %copy-done.98), channel_id=1, source_target_pairs={{0,2},{1,3},{2,0},{3,1},{4,6},{5,7},{6,4},{7,5},{8,10},{9,11},{10,... | collective-permute-start | bytes 18440 | tf_op jit(solution)/shard_map/ppermute | solution.py:465
  55.0 54.5 %gather_cores.4 = bf16[2,768,1152]{2,1,0:T(8,128)(2,1)S(1)} custom-call(bf16[768,1152]{1,0:T(8,128)(2,1)S(1)} %fusion.21.own_ref), custom_call_target="tpu_custom_call" | custom-call | bytes 12000000 | tf_op jit(solution)/shard_map/gather_cores/pallas_call | solution.py:531
  111.4 14.9 %add_convert_fusion.q_ref.k_ref.v_ref = bf16[1536,3072]{1,0:T(8,128)(2,1)} fusion(bf16[1536,1152]{1,0:T(8,128)(2,1)S(1)} %bitcast.334, bf16[1152,3072]{0,1:T(8,128)(2,1)S(1)} %bitcast.358, f32[3072]{0:T(1024)S(1)} %pad_bitcast_fusion), kind=kOutput, calls=%fused_computation.3 | convolution fusion | flops 10881073152 | bytes 20066304 | tf_op jit(solution)/shard_map/dot_general | solution.py:778
  126.3 43.2 %attend.1 = bf16[1536,1024]{1,0:T(8,128)(2,1)S(1)} custom-call(s32[6]{0:T(128)S(1)} %get-tuple-element.28.starts, s32[6]{0:T(128)S(1)} %fusion.119.counts, bf16[1536,3072]{1,0:T(8,128)(2,1)} %add_convert_fusion.q_ref.k_ref.v_ref, bf16[1536,3072]{1,0:T(8,128)(2,1)} %add_convert_fusion.q_ref.k_ref.v_ref, bf16[1536,3072]{1,0:T(8,128)(2,1)} %add_convert_fusion.q_ref.k_ref.v_ref), custom_call_target="tpu_custom_call" | custom-call | flops 20000000000 | bytes 13000000 | tf_op jit(solution)/shard_map/attend/pallas_call | solution.py:576
  176.9 14.9 %collective-permute-start.8 = (bf16[2304,1152]{1,0:T(8,128)(2,1)}, bf16[2304,1152]{1,0:T(8,128)(2,1)}, u32[]{:S(2)}, u32[]{:S(2)}) collective-permute-start(bf16[2304,1152]{1,0:T(8,128)(2,1)} %param.32), channel_id=1, source_target_pairs={{1,2},{2,1},{5,6},{6,5},{9,10},{10,9},{13,14},{14,13},{17,18},{18,... | collective-permute-start | bytes 15925256 | tf_op jit(solution)/shard_map/ppermute | solution.py:465
  196.6 49.1 %collective-permute-done.19 = bf16[16,6,1152]{2,1,0:T(8,128)(2,1)S(1)} collective-permute-done((bf16[16,6,1152]{2,1,0:T(8,128)(2,1)S(1)}, bf16[16,6,1152]{2,1,0:T(8,128)(2,1)S(1)}, u32[]{:S(2)}, u32[]{:S(2)}) %collective-permute-start.19) | collective-permute-done | bytes 221216 | tf_op jit(solution)/shard_map/ppermute | solution.py:465
  288.0 15.6 %multiply_convert_fusion = (bf16[1536,2304]{1,0:T(8,128)(2,1)}, f32[1536,2304]{1,0:T(8,128)}) fusion(f32[2304]{0:T(1024)S(1)} %copy-done.97, bf16[1536,1152]{1,0:T(8,128)(2,1)S(1)} %bitcast.336, bf16[1152,2304]{1,0:T(8,128)(2,1)S(1)} %bitcast.346), kind=kOutput, calls=%fused_computation.10 | convolution fusion | flops 8189116416 | bytes 30090240 | tf_op jit(solution)/shard_map/dot_general | solution.py:778
  380.7 14.5 %fusion.140 = (f32[2048]{0:T(1024)}, bf16[768,2048]{1,0:T(8,128)(2,1)S(1)}) fusion(f32[768,2048]{1,0:T(8,128)} %copy-done.109, f32[2048]{0:T(1024)S(1)} %copy-done.99, bf16[2048,2048]{1,0:T(8,128)(2,1)} %param.36, bf16[768,2048]{1,0:T(8,128)(2,1)} %get-tuple-element.201), kind=kOutput, calls=%fused_computation.326 | convolution fusion | flops 6461323264 | bytes 20987904 | tf_op jit(solution)/shard_map/dot_general | solution.py:21
  430.6 13.3 %convolution_convert_fusion = bf16[1152,2304]{1,0:T(8,128)(2,1)} fusion(bf16[1536,1152]{1,0:T(8,128)(2,1)S(1)} %bitcast.340, bf16[1536,2304]{1,0:T(8,128)(2,1)} %get-tuple-element.191), kind=kOutput, calls=%fused_computation.12 | convolution fusion | flops 8156381184 | bytes 15925248 | tf_op jit(solution)/shard_map/dot_general | solution.py:27
  444.0 19.9 %fusion.132 = (f32[2304]{0:T(1024)}, bf16[1536,2304]{1,0:T(8,128)(2,1)}) fusion(f32[1536,2304]{1,0:T(8,128)} %get-tuple-element.192, bf16[1536,1152]{1,0:T(8,128)(2,1)S(1)} %bitcast.341, bf16[2304,1152]{1,0:T(8,128)(2,1)S(1)} %bitcast.362), kind=kOutput, calls=%fused_computation.320 | convolution fusion | flops 8228042752 | bytes 30090240 | tf_op jit(solution)/shard_map/dot_general | solution.py:21
  472.0 13.2 %convolution_convert_fusion.1 = bf16[1152,2304]{1,0:T(8,128)(2,1)} fusion(bf16[1536,1152]{1,0:T(8,128)(2,1)S(1)} %bitcast.337, bf16[1536,2304]{1,0:T(8,128)(2,1)} %get-tuple-element.150), kind=kOutput, calls=%fused_computation.13 | convolution fusion | flops 8156381184 | bytes 15925248 | tf_op jit(solution)/shard_map/dot_general | solution.py:27
  534.2 11.2 %fusion.60 = (f32[768]{0:T(1024)S(1)}, f32[768]{0:T(1024)S(1)}, f32[768,1152]{1,0:T(8,128)}, bf16[768,1152]{1,0:T(8,128)(2,1)S(1)}) fusion(f32[3,1152]{1,0:T(4,128)S(1)} %copy-done.65, bf16[768,1152]{1,0:T(8,128)(2,1)} %collective-permute-done.14, f32[768]{0:T(1024)S(1)} %copy-done.81, f32[768,1152]{1,0:T(8,128)S(1)} %copy-done.15, ...), kind=kOutput, calls=%fused_computation.111 | convolution fusion | flops 4085709312 | bytes 19490308 | tf_op jit(solution)/shard_map/dot_general | solution.py:21
  561.0 77.1 %attend_back.1 = (bf16[1536,3072]{1,0:T(8,128)(2,1)}, f32[8,1024]{1,0:T(8,128)S(1)}) custom-call(s32[6]{0:T(128)S(1)} %copy-done.11, s32[6]{0:T(128)S(1)} %copy-done.13, bf16[1536,3072]{1,0:T(8,128)(2,1)} %add_convert_fusion.q_ref.k_ref.v_ref, bf16[1536,3072]{1,0:T(8,128)(2,1)} %add_convert_fusion.q_ref.k_ref.v_ref, ...), custom_call_target="tpu_custom_call" | custom-call | flops 40000000000 | bytes 25000000 | tf_op jit(solution)/shard_map/attend_back/pallas_call | solution.py:654
  651.7 14.0 %fusion.11 = bf16[144,8,24,128]{3,1,2,0:T(8,128)(2,1)S(1)} fusion(bf16[1536,1152]{1,0:T(8,128)(2,1)S(1)} %bitcast.335, bf16[1536,3072]{1,0:T(8,128)(2,1)} %get-tuple-element.35), kind=kOutput, calls=%fused_computation.30 | convolution fusion | flops 10875174912 | bytes 20054016 | tf_op jit(solution)/shard_map/dot_general | solution.py:27
  706.7 11.2 %reshape_reshape.7 = bf16[2,2,2,2,72,576]{4,3,2,1,0,5:T(2,128)(2,1)} reshape(bf16[1152,8,72]{0,2,1:T(8,128)(2,1)} %slice.92) | data formatting | bytes 2654208 | tf_op jit(solution)/shard_map/reshape;reshape | solution.py:843
  736.1 16.2 %collective-permute-done.63 = bf16[2,2,2,24,2048]{4,3,0,1,2:T(8,128)(2,1)S(1)} collective-permute-done((bf16[2,2,2,24,2048]{4,3,0,1,2:T(8,128)(2,1)}, bf16[2,2,2,24,2048]{4,3,0,1,2:T(8,128)(2,1)S(1)}, u32[]{:S(2)}, u32[]{:S(2)}) %collective-permute-start.63) | collective-permute-done | bytes 786464 | tf_op jit(solution)/shard_map/ppermute | solution.py:465
  753.8 16.8 %collective-permute-done.37 = bf16[2,2,2,72,576]{4,3,2,1,0:T(8,128)(2,1)S(1)} collective-permute-done((bf16[2,2,2,72,576]{4,3,2,1,0:T(8,128)(2,1)S(1)}, bf16[2,2,2,72,576]{4,3,2,1,0:T(8,128)(2,1)S(1)}, u32[]{:S(2)}, u32[]{:S(2)}) %collective-permute-start.37) | collective-permute-done | bytes 663584 | tf_op jit(solution)/shard_map/ppermute | solution.py:465
  799.1 13.8 %collective-permute-done.39 = bf16[2,72,576]{1,0,2:T(2,128)(2,1)S(1)} collective-permute-done((bf16[2,72,576]{1,0,2:T(2,128)(2,1)S(1)}, bf16[2,72,576]{1,0,2:T(2,128)(2,1)S(1)}, u32[]{:S(2)}, u32[]{:S(2)}) %collective-permute-start.39) | collective-permute-done | bytes 165920 | tf_op jit(solution)/shard_map/ppermute | solution.py:465
  829.5 12.2 %fusion.59 = (f32[768]{0:T(1024)S(1)}, f32[768]{0:T(1024)S(1)}, f32[768,1152]{1,0:T(8,128)S(1)}) fusion(f32[3,1152]{1,0:T(4,128)S(1)} %copy-done.76, f32[768]{0:T(1024)S(1)} %copy-done.85, f32[768]{0:T(1024)S(1)} %copy-done.83, bf16[768,1152]{1,0:T(8,128)(2,1)S(1)} %copy-done.17, bf16[768,1152]{1,0:T(8,128)(2,1)} %collective-permute-done.15, ...), kind=kOutput, calls=%fused_computation.110 | convolution fusion | flops 5445548032 | bytes 18900484 | tf_op jit(solution)/shard_map/dot_general | solution.py:21
  884.7 24.1 %collective-permute-done.49 = bf16[2,2,72,2304]{3,2,0,1:T(8,128)(2,1)} collective-permute-done((bf16[2,2,72,2304]{3,2,0,1:T(8,128)(2,1)}, bf16[2,2,72,2304]{3,2,0,1:T(8,128)(2,1)}, u32[]{:S(2)}, u32[]{:S(2)}) %collective-permute-start.49) | collective-permute-done | bytes 1327136 | tf_op jit(solution)/shard_map/ppermute | solution.py:465
  926.2 37.1 %collective-permute-done.25 = bf16[16,6,2,216]{3,0,2,1:T(8,128)(2,1)S(1)} collective-permute-done((bf16[16,6,2,216]{3,0,2,1:T(8,128)(2,1)S(1)}, bf16[16,6,2,216]{3,0,2,1:T(8,128)(2,1)S(1)}, u32[]{:S(2)}, u32[]{:S(2)}) %collective-permute-start.25) | collective-permute-done | bytes 82976 | tf_op jit(solution)/shard_map/ppermute | solution.py:465
  979.9 30.6 %collective-permute-done.56 = bf16[64,1152]{1,0:T(8,128)(2,1)S(1)} collective-permute-done((bf16[64,1152]{1,0:T(8,128)(2,1)S(1)}, bf16[64,1152]{1,0:T(8,128)(2,1)S(1)}, u32[]{:S(2)}, u32[]{:S(2)}) %collective-permute-start.56) | collective-permute-done | bytes 147488 | tf_op jit(solution)/shard_map/ppermute | solution.py:465
  1025.1 11.4 %collective-permute-done.58 = bf16[2,2,2,64,2048]{4,3,0,1,2:T(8,128)(2,1)S(1)} collective-permute-done((bf16[2,2,2,64,2048]{4,3,0,1,2:T(8,128)(2,1)S(1)}, bf16[2,2,2,64,2048]{4,3,0,1,2:T(8,128)(2,1)S(1)}, u32[]{:S(2)}, u32[]{:S(2)}) %collective-permute-start.58) | collective-permute-done | bytes 2097184 | tf_op jit(solution)/shard_map/ppermute | solution.py:465
  1040.3 13.1 %collective-permute-done.59 = bf16[2,2,64,2048]{3,2,0,1:T(8,128)(2,1)S(1)} collective-permute-done((bf16[2,2,64,2048]{3,2,0,1:T(8,128)(2,1)S(1)}, bf16[2,2,64,2048]{3,2,0,1:T(8,128)(2,1)S(1)}, u32[]{:S(2)}, u32[]{:S(2)}) %collective-permute-start.59) | collective-permute-done | bytes 1048608 | tf_op jit(solution)/shard_map/ppermute | solution.py:465
  (602 shorter events, 508.4 us)
Async XLA Ops:
  50.4 119.5 %collective-permute-start.7 = (bf16[1152,2304]{1,0:T(8,128)(2,1)}, bf16[1152,2304]{1,0:T(8,128)(2,1)}, u32[]{:S(2)}, u32[]{:S(2)}) collective-permute-start(bf16[1152,2304]{1,0:T(8,128)(2,1)} %param.30), channel_id=1, source_target_pairs={{1,2},{2,1},{5,6},{6,5},{9,10},{10,9},{13,14},{14,13},{17,18},{18,... | collective-permute-start | bytes 15925256 | tf_op jit(solution)/shard_map/ppermute | solution.py:465
  176.9 126.7 %collective-permute-start.8 = (bf16[2304,1152]{1,0:T(8,128)(2,1)}, bf16[2304,1152]{1,0:T(8,128)(2,1)}, u32[]{:S(2)}, u32[]{:S(2)}) collective-permute-start(bf16[2304,1152]{1,0:T(8,128)(2,1)} %param.32), channel_id=1, source_target_pairs={{1,2},{2,1},{5,6},{6,5},{9,10},{10,9},{13,14},{14,13},{17,18},{18,... | collective-permute-start | bytes 15925256 | tf_op jit(solution)/shard_map/ppermute | solution.py:465
  195.2 80.2 %collective-permute-start.6 = (bf16[768,1152]{1,0:T(8,128)(2,1)}, bf16[768,1152]{1,0:T(8,128)(2,1)}, u32[]{:S(2)}, u32[]{:S(2)}) collective-permute-start(bf16[768,1152]{1,0:T(8,128)(2,1)} %convolution_convert_fusion.8), channel_id=1, source_target_pairs={{0,2},{1,3},{2,0},{3,1},{4,6},{5,7},{6,4},{7,5},{8,10},{9,11},{10,... | collective-permute-start | bytes 5308424 | tf_op jit(solution)/shard_map/ppermute | solution.py:465
  195.3 50.4 %collective-permute-start.19 = (bf16[16,6,1152]{2,1,0:T(8,128)(2,1)S(1)}, bf16[16,6,1152]{2,1,0:T(8,128)(2,1)S(1)}, u32[]{:S(2)}, u32[]{:S(2)}) collective-permute-start(bf16[16,6,1152]{2,1,0:T(8,128)(2,1)S(1)} %constant_dynamic-update-slice_fusion.1), channel_id=1, source_target_pairs={{0,1},{1,0},{2,3},{3,2},{4,5},{5,4},{6,7},{7,6},{8,9},{9,8},{10,11... | collective-permute-start | bytes 663560 | tf_op jit(solution)/shard_map/ppermute | solution.py:465
  264.3 52.4 %collective-permute-start.13 = (bf16[1536,768]{1,0:T(8,128)(2,1)}, bf16[1536,768]{1,0:T(8,128)(2,1)}, u32[]{:S(2)}, u32[]{:S(2)}) collective-permute-start(bf16[1536,768]{1,0:T(8,128)(2,1)} %param.40), channel_id=1, source_target_pairs={{0,2},{1,3},{2,0},{3,1},{4,6},{5,7},{6,4},{7,5},{8,10},{9,11},{10,... | collective-permute-start | bytes 7077896 | tf_op jit(solution)/shard_map/ppermute | solution.py:465
  331.7 85.1 %collective-permute-start.11 = (bf16[768,1152]{1,0:T(8,128)(2,1)}, bf16[768,1152]{1,0:T(8,128)(2,1)}, u32[]{:S(2)}, u32[]{:S(2)}) collective-permute-start(bf16[768,1152]{1,0:T(8,128)(2,1)} %param.43), channel_id=1, source_target_pairs={{1,2},{2,1},{5,6},{6,5},{9,10},{10,9},{13,14},{14,13},{17,18},{18,... | collective-permute-start | bytes 5308424 | tf_op jit(solution)/shard_map/ppermute | solution.py:465
  348.5 332.8 %collective-permute-start.10 = (bf16[768,1152]{1,0:T(8,128)(2,1)}, bf16[768,1152]{1,0:T(8,128)(2,1)}, u32[]{:S(2)}, u32[]{:S(2)}) collective-permute-start(bf16[768,1152]{1,0:T(8,128)(2,1)} %get-tuple-element.153), channel_id=1, source_target_pairs={{1,2},{2,1},{5,6},{6,5},{9,10},{10,9},{13,14},{14,13},{17,18},{18,... | collective-permute-start | bytes 5308424 | tf_op jit(solution)/shard_map/ppermute | solution.py:465
  487.9 40.5 %collective-permute-start.62 = (bf16[2,2,2,2,24,2048]{5,4,0,1,3,2:T(8,128)(2,1)}, bf16[2,2,2,2,24,2048]{5,4,0,1,3,2:T(8,128)(2,1)}, u32[]{:S(2)}, u32[]{:S(2)}) collective-permute-start(bf16[2,2,2,2,24,2048]{5,4,0,1,3,2:T(8,128)(2,1)} %bitcast.330), channel_id=1, source_target_pairs={{0,2},{1,3},{2,0},{3,1},{4,6},{5,7},{6,4},{7,5},{8,10},{9,11},{10,... | collective-permute-start | bytes 4718600 | tf_op jit(solution)/shard_map/ppermute | solution.py:465
  488.3 46.0 %collective-permute-start.14 = (bf16[768,1152]{1,0:T(8,128)(2,1)}, bf16[768,1152]{1,0:T(8,128)(2,1)}, u32[]{:S(2)}, u32[]{:S(2)}) collective-permute-start(bf16[768,1152]{1,0:T(8,128)(2,1)} %fusion.43), channel_id=1, source_target_pairs={{0,2},{1,3},{2,0},{3,1},{4,6},{5,7},{6,4},{7,5},{8,10},{9,11},{10,... | collective-permute-start | bytes 5308424 | tf_op jit(solution)/shard_map/ppermute | solution.py:465
  504.5 227.4 %collective-permute-start.52 = (bf16[2,2,2,2,64,1152]{5,4,0,1,3,2:T(8,128)(2,1)}, bf16[2,2,2,2,64,1152]{5,4,0,1,3,2:T(8,128)(2,1)}, u32[]{:S(2)}, u32[]{:S(2)}) collective-permute-start(bf16[2,2,2,2,64,1152]{5,4,0,1,3,2:T(8,128)(2,1)} %bitcast.329), channel_id=1, source_target_pairs={{0,2},{1,3},{2,0},{3,1},{4,6},{5,7},{6,4},{7,5},{8,10},{9,11},{10,... | collective-permute-start | bytes 7077896 | tf_op jit(solution)/shard_map/ppermute | solution.py:465
  511.5 267.4 %collective-permute-start.43 = (bf16[2,2,2,72,2304]{4,3,0,1,2:T(8,128)(2,1)}, bf16[2,2,2,72,2304]{4,3,0,1,2:T(8,128)(2,1)}, u32[]{:S(2)}, u32[]{:S(2)}) collective-permute-start(bf16[2,2,2,72,2304]{4,3,0,1,2:T(8,128)(2,1)} %bitcast.327), channel_id=1, source_target_pairs={{1,2},{2,1},{5,6},{6,5},{9,10},{10,9},{13,14},{14,13},{17,18},{18,... | collective-permute-start | bytes 7962632 | tf_op jit(solution)/shard_map/ppermute | solution.py:465
  528.4 254.2 %collective-permute-start.48 = (bf16[2,2,2,72,2304]{4,3,0,1,2:T(8,128)(2,1)}, bf16[2,2,2,72,2304]{4,3,0,1,2:T(8,128)(2,1)}, u32[]{:S(2)}, u32[]{:S(2)}) collective-permute-start(bf16[2,2,2,72,2304]{4,3,0,1,2:T(8,128)(2,1)} %bitcast.369), channel_id=1, source_target_pairs={{1,2},{2,1},{5,6},{6,5},{9,10},{10,9},{13,14},{14,13},{17,18},{18,... | collective-permute-start | bytes 7962632 | tf_op jit(solution)/shard_map/ppermute | solution.py:465
  681.2 98.2 %collective-permute-start.42 = (bf16[2,2,2,72,2304]{4,3,0,1,2:T(8,128)(2,1)}, bf16[2,2,2,72,2304]{4,3,0,1,2:T(8,128)(2,1)}, u32[]{:S(2)}, u32[]{:S(2)}) collective-permute-start(bf16[2,2,2,72,2304]{4,3,0,1,2:T(8,128)(2,1)} %bitcast.328), channel_id=1, source_target_pairs={{0,2},{1,0},{2,3},{3,1},{4,6},{5,4},{6,7},{7,5},{8,10},{9,8},{10,1... | collective-permute-start | bytes 7962632 | tf_op jit(solution)/shard_map/ppermute | solution.py:465
  727.3 57.1 %collective-permute-start.47 = (bf16[2,2,2,72,2304]{4,3,0,1,2:T(8,128)(2,1)}, bf16[2,2,2,72,2304]{4,3,0,1,2:T(8,128)(2,1)}, u32[]{:S(2)}, u32[]{:S(2)}) collective-permute-start(bf16[2,2,2,72,2304]{4,3,0,1,2:T(8,128)(2,1)} %bitcast.368), channel_id=1, source_target_pairs={{0,2},{1,0},{2,3},{3,1},{4,6},{5,4},{6,7},{7,5},{8,10},{9,8},{10,1... | collective-permute-start | bytes 7962632 | tf_op jit(solution)/shard_map/ppermute | solution.py:465
  770.6 149.5 %collective-permute-start.57 = (bf16[2,2,2,2,64,2048]{5,4,0,1,3,2:T(8,128)(2,1)}, bf16[2,2,2,2,64,2048]{5,4,0,1,3,2:T(8,128)(2,1)}, u32[]{:S(2)}, u32[]{:S(2)}) collective-permute-start(bf16[2,2,2,2,64,2048]{5,4,0,1,3,2:T(8,128)(2,1)} %bitcast.324), channel_id=1, source_target_pairs={{0,2},{1,3},{2,0},{3,1},{4,6},{5,7},{6,4},{7,5},{8,10},{9,11},{10,... | collective-permute-start | bytes 12582920 | tf_op jit(solution)/shard_map/ppermute | solution.py:465
  778.9 48.7 %collective-permute-start.15 = (bf16[768,1152]{1,0:T(8,128)(2,1)}, bf16[768,1152]{1,0:T(8,128)(2,1)}, u32[]{:S(2)}, u32[]{:S(2)}) collective-permute-start(bf16[768,1152]{1,0:T(8,128)(2,1)} %fusion.49), channel_id=1, source_target_pairs={{0,2},{1,3},{2,0},{3,1},{4,6},{5,7},{6,4},{7,5},{8,10},{9,11},{10,... | collective-permute-start | bytes 5308424 | tf_op jit(solution)/shard_map/ppermute | solution.py:465
  779.4 92.5 %collective-permute-start.27 = (bf16[2,2,2,72,1728]{4,3,2,1,0:T(8,128)(2,1)}, bf16[2,2,2,72,1728]{4,3,2,1,0:T(8,128)(2,1)}, u32[]{:S(2)}, u32[]{:S(2)}) collective-permute-start(bf16[2,2,2,72,1728]{4,3,2,1,0:T(8,128)(2,1)} %dynamic-slice_bitcast_fusion.1), channel_id=1, source_target_pairs={{0,4},{1,5},{2,6},{3,7},{4,0},{5,1},{6,2},{7,3},{8,12},{9,13},{10,... | collective-permute-start | bytes 5971976 | tf_op jit(solution)/shard_map/ppermute | solution.py:465
  826.6 54.6 %collective-permute-start.44 = (bf16[2,2,72,2304]{3,2,0,1:T(8,128)(2,1)}, bf16[2,2,72,2304]{3,2,0,1:T(8,128)(2,1)}, u32[]{:S(2)}, u32[]{:S(2)}) collective-permute-start(bf16[2,2,72,2304]{3,2,0,1:T(8,128)(2,1)} %dynamic-slice_bitcast_fusion.3), channel_id=1, source_target_pairs={{0,4},{1,5},{2,6},{3,7},{4,0},{5,1},{6,2},{7,3},{8,12},{9,13},{10,... | collective-permute-start | bytes 3981320 | tf_op jit(solution)/shard_map/ppermute | solution.py:465
  827.6 81.2 %collective-permute-start.49 = (bf16[2,2,72,2304]{3,2,0,1:T(8,128)(2,1)}, bf16[2,2,72,2304]{3,2,0,1:T(8,128)(2,1)}, u32[]{:S(2)}, u32[]{:S(2)}) collective-permute-start(bf16[2,2,72,2304]{3,2,0,1:T(8,128)(2,1)} %dynamic-slice_bitcast_fusion.2), channel_id=1, source_target_pairs={{0,4},{1,5},{2,6},{3,7},{4,0},{5,1},{6,2},{7,3},{8,12},{9,13},{10,... | collective-permute-start | bytes 3981320 | tf_op jit(solution)/shard_map/ppermute | solution.py:465
  870.3 183.6 %collective-permute-start.16 = (bf16[768,1152]{1,0:T(8,128)(2,1)S(1)}, bf16[768,1152]{1,0:T(8,128)(2,1)S(1)}, u32[]{:S(2)}, u32[]{:S(2)}) collective-permute-start(bf16[768,1152]{1,0:T(8,128)(2,1)S(1)} %add_convert_fusion.3), channel_id=1, source_target_pairs={{1,2},{2,1},{5,6},{6,5},{9,10},{10,9},{13,14},{14,13},{17,18},{18,... | collective-permute-start | bytes 5308424 | tf_op jit(solution)/shard_map/ppermute | solution.py:465
  871.9 45.9 %collective-permute-start.54 = (bf16[2,2,64,1152]{3,2,0,1:T(8,128)(2,1)}, bf16[2,2,64,1152]{3,2,0,1:T(8,128)(2,1)S(1)}, u32[]{:S(2)}, u32[]{:S(2)}) collective-permute-start(bf16[2,2,64,1152]{3,2,0,1:T(8,128)(2,1)} %dynamic-slice_bitcast_fusion.10), channel_id=1, source_target_pairs={{0,1},{1,0},{2,3},{3,2},{4,5},{5,4},{6,7},{7,6},{8,9},{9,8},{10,11... | collective-permute-start | bytes 1769480 | tf_op jit(solution)/shard_map/ppermute | solution.py:465
  908.8 108.0 %collective-permute-start.28 = (bf16[2,2,72,1728]{3,2,1,0:T(8,128)(2,1)S(1)}, bf16[2,2,72,1728]{3,2,1,0:T(8,128)(2,1)S(1)}, u32[]{:S(2)}, u32[]{:S(2)}) collective-permute-start(bf16[2,2,72,1728]{3,2,1,0:T(8,128)(2,1)S(1)} %dynamic-slice_bitcast_fusion.6), channel_id=1, source_target_pairs={{0,8},{1,9},{2,10},{3,11},{4,12},{5,13},{6,14},{7,15},{8,0},{9,1},... | collective-permute-start | bytes 2985992 | tf_op jit(solution)/shard_map/ppermute | solution.py:465
  917.7 93.5 %collective-permute-start.45 = (bf16[2,72,2304]{2,1,0:T(8,128)(2,1)}, bf16[2,72,2304]{2,1,0:T(8,128)(2,1)}, u32[]{:S(2)}, u32[]{:S(2)}) collective-permute-start(bf16[2,72,2304]{2,1,0:T(8,128)(2,1)} %dynamic-slice_bitcast_fusion.9), channel_id=1, source_target_pairs={{0,8},{1,9},{2,10},{3,11},{4,12},{5,13},{6,14},{7,15},{8,0},{9,1},... | collective-permute-start | bytes 1990664 | tf_op jit(solution)/shard_map/ppermute | solution.py:465
  917.8 94.8 %collective-permute-start.50 = (bf16[2,72,2304]{2,1,0:T(8,128)(2,1)}, bf16[2,72,2304]{2,1,0:T(8,128)(2,1)}, u32[]{:S(2)}, u32[]{:S(2)}) collective-permute-start(bf16[2,72,2304]{2,1,0:T(8,128)(2,1)} %dynamic-slice_bitcast_fusion.8), channel_id=1, source_target_pairs={{0,8},{1,9},{2,10},{3,11},{4,12},{5,13},{6,14},{7,15},{8,0},{9,1},... | collective-permute-start | bytes 1990664 | tf_op jit(solution)/shard_map/ppermute | solution.py:465
  (167 other events, 4501.6 us)

commit v2 on v1

--- a/solution.py
+++ b/solution.py
@@ -447,6 +447,8 @@
 
 LANES = 128
 MESH = pl.DeviceIdType.MESH
+TILE = 256
+LOG2_E = 1.4426950408889634
 bf16 = jnp.bfloat16
 f32 = jnp.float32
 
@@ -495,12 +497,6 @@
 
 def pick(array, index, axis):
     return lax.dynamic_index_in_dim(array, index, axis=axis, keepdims=False)
-
-
-def halve(array, axis, bit, move):
-    got = send(pick(array, 1 - bit, axis), move)
-    kept = pick(array, bit, axis)
-    return (kept.astype(f32) + got.astype(f32)).astype(bf16)
 
 
 def gather_kernel(own_ref, out_ref, local_sem, send_sem, recv_sem):
@@ -540,141 +536,860 @@
     )(own).reshape(2 * rows, width)
 
 
-def attend_kernel(factor, starts, counts, q_ref, k_ref, v_ref, o_ref):
-    def unit(index, carry):
-        rows = pl.ds(pl.multiple_of(index * SHORT, SHORT), SHORT)
-
-        def run(length):
-            cols = pl.ds(pl.multiple_of(starts[index] * SHORT, SHORT), length)
-            scores = dot_nt(k_ref[cols, :], q_ref[rows, :])
-            top = jnp.max(scores, axis=0, keepdims=True)
-            exponent = jnp.exp((scores - top) * factor)
-            total = jnp.sum(exponent, axis=0, keepdims=True)
-            prob_low = (exponent * (1.0 / total)).astype(bf16)
-            summed = dot_tn(v_ref[cols, :], prob_low)
-            o_ref[rows, :] = summed.T.astype(bf16)
-
-        @pl.when(counts[index] == 1)
-        def _():
-            run(SHORT)
-
-        @pl.when(counts[index] != 1)
-        def _():
-            run(4 * SHORT)
-
-        return carry
-
-    lax.fori_loop(0, q_ref.shape[0] // SHORT, unit, 0)
-
-
-def attend(starts, counts, qkv, heads, factor):
+def split_heads(flat_ref, heads_ref, parts, heads):
+    heads_ref[...] = jnp.zeros_like(heads_ref)
+    for part in range(parts):
+        for head in range(heads):
+            begin = (part * heads + head) * HEAD_DIM
+            heads_ref[part * heads + head, :, 0:HEAD_DIM] = flat_ref[:, begin : begin + HEAD_DIM]
+
+
+def join_heads(heads_ref, flat_ref, count):
+    rows, columns = flat_ref.shape
+    for block in range(rows // LANES):
+        span = slice(block * LANES, (block + 1) * LANES)
+        pieces = [heads_ref[head, span, 0:HEAD_DIM] for head in range(count)]
+        if columns > count * HEAD_DIM:
+            pieces.append(jnp.zeros((LANES, columns - count * HEAD_DIM), flat_ref.dtype))
+        flat_ref[span, :] = jnp.concatenate(pieces, axis=1)
+
+
+def per_image(count, run):
+    @pl.when(count == 1)
+    def _():
+        run(SHORT)
+
+    @pl.when(count != 1)
+    def _():
+        run(4 * SHORT)
+
+
+def attend_kernel(heads, together, factor, starts, counts, qkv_ref, o_ref, log_ref, part_ref, o_heads):
+    split_heads(qkv_ref, part_ref, 3, heads)
+    unit_count = o_ref.shape[0] // SHORT
+
+    def some_heads(step, carry):
+        def unit(index, carry):
+            rows = pl.ds(pl.multiple_of(index * SHORT, SHORT), SHORT)
+
+            def run(length):
+                cols = pl.ds(pl.multiple_of(starts[index] * SHORT, SHORT), length)
+                for ahead in range(together):
+                    head = step * together + ahead
+                    scores = dot_nt(part_ref[heads + head, cols, :], part_ref[head, rows, :])
+                    top = jnp.max(scores, axis=0, keepdims=True)
+                    exponent = jnp.exp2((scores - top) * factor)
+                    total = jnp.sum(exponent, axis=0, keepdims=True)
+                    summed = dot_tn(part_ref[2 * heads + head, cols, :], exponent.astype(bf16))
+                    o_heads[head, rows, :] = (summed * (1.0 / total)).T.astype(bf16)
+                    log_ref[head * unit_count + index] = top * factor + jnp.log2(total)
+
+            per_image(counts[index], run)
+            return carry
+
+        return lax.fori_loop(0, unit_count, unit, carry)
+
+    lax.fori_loop(0, heads // together, some_heads, 0)
+    join_heads(o_heads, o_ref, heads)
+
+
+def whole_spec(space=pltpu.VMEM):
+    return pl.BlockSpec(memory_space=space)
+
+
+def attend(starts, counts, qkv, heads, out_cols):
     rows = qkv.shape[0]
-
-    def spec(part):
-        return pl.BlockSpec((rows, LANES), lambda h, *_: (0, part * heads + h))
-
+    factor = HEAD_DIM ** (-0.5) * LOG2_E
     return pl.pallas_call(
-        functools.partial(attend_kernel, factor),
-        out_shape=jax.ShapeDtypeStruct((rows, heads * LANES), bf16),
-        grid_spec=pltpu.PrefetchScalarGridSpec(
-            num_scalar_prefetch=2,
-            grid=(heads,),
-            in_specs=[spec(0), spec(1), spec(2)],
-            out_specs=spec(0),
+        functools.partial(attend_kernel, heads, 2, factor),
+        out_shape=(
+            jax.ShapeDtypeStruct((rows, out_cols), bf16),
+            jax.ShapeDtypeStruct((heads * (rows // SHORT), 1, SHORT), f32),
         ),
-        compiler_params=pltpu.CompilerParams(vmem_limit_bytes=48 << 20),
+        in_specs=[whole_spec(pltpu.SMEM), whole_spec(pltpu.SMEM), whole_spec()],
+        out_specs=(whole_spec(), whole_spec()),
+        scratch_shapes=[
+            pltpu.VMEM((3 * heads, rows, LANES), bf16),
+            pltpu.VMEM((heads, rows, LANES), bf16),
+        ],
+        compiler_params=pltpu.CompilerParams(vmem_limit_bytes=40 << 20),
         cost_estimate=pl.CostEstimate(flops=20 * 10**9, bytes_accessed=13 * 10**6, transcendentals=10**7),
         name="attend",
-    )(starts, counts, qkv, qkv, qkv)
+    )(starts, counts, qkv)
 
 
 def attend_back_kernel(
-    factor, starts, counts, q_ref, k_ref, v_ref, g_ref, out_ref, bias_ref, key_acc, value_acc, query_low
+    heads,
+    together,
+    factor,
+    starts,
+    counts,
+    qkv_ref,
+    log_ref,
+    grad_ref,
+    out_ref,
+    bias_ref,
+    part_ref,
+    grad_heads,
+    key_acc,
+    value_acc,
+    sums,
 ):
-    part = pl.program_id(1)
-    rows_all = q_ref.shape[0]
-
-    @pl.when(part == 0)
-    def _():
+    split_heads(qkv_ref, part_ref, 3, heads)
+    split_heads(grad_ref, grad_heads, 1, heads)
+    unit_count = out_ref.shape[0] // SHORT
+
+    def some_heads(step, carry):
         key_acc[...] = jnp.zeros_like(key_acc)
         value_acc[...] = jnp.zeros_like(value_acc)
-        bias_ref[...] = jnp.zeros_like(bias_ref)
+        for ahead in range(together):
+            sums[step * together + ahead] = jnp.zeros((8, LANES), f32)
 
         def unit(index, carry):
             rows = pl.ds(pl.multiple_of(index * SHORT, SHORT), SHORT)
 
             def run(length):
                 cols = pl.ds(pl.multiple_of(starts[index] * SHORT, SHORT), length)
-                queries = q_ref[rows, :]
-                grads = g_ref[rows, :]
-                keys = k_ref[cols, :]
-                scores = dot_nt(keys, queries)
-                top = jnp.max(scores, axis=0, keepdims=True)
-                exponent = jnp.exp((scores - top) * factor)
-                total = jnp.sum(exponent, axis=0, keepdims=True)
-                soft = exponent * (1.0 / total)
-                grad_soft = dot_nt(v_ref[cols, :], grads)
-                inner = jnp.sum(soft * grad_soft, axis=0, keepdims=True)
-                grad_scores = (soft * (grad_soft - inner)).astype(bf16)
-                value_acc[cols, :] += jnp.dot(soft.astype(bf16), grads, preferred_element_type=f32)
-                key_acc[cols, :] += jnp.dot(grad_scores, queries, preferred_element_type=f32)
-                grad_query = dot_tn(keys, grad_scores).T * factor
-                query_low[rows, :] = grad_query.astype(bf16)
-                bias_ref[0:1, :] += jnp.sum(grad_query, axis=0, keepdims=True)
-
-            @pl.when(counts[index] == 1)
-            def _():
-                run(SHORT)
-
-            @pl.when(counts[index] != 1)
-            def _():
-                run(4 * SHORT)
-
+                for ahead in range(together):
+                    head = step * together + ahead
+                    queries = part_ref[head, rows, :]
+                    grads = grad_heads[head, rows, :]
+                    keys = part_ref[heads + head, cols, :]
+                    scores = dot_nt(keys, queries)
+                    soft = jnp.exp2(scores * (factor * LOG2_E) - log_ref[head * unit_count + index])
+                    grad_soft = dot_nt(part_ref[2 * heads + head, cols, :], grads)
+                    product = soft * grad_soft
+                    inner = jnp.sum(product, axis=0, keepdims=True)
+                    grad_scores = (product - soft * inner).astype(bf16)
+                    value_acc[ahead, cols, :] += jnp.dot(soft.astype(bf16), grads, preferred_element_type=f32)
+                    key_acc[ahead, cols, :] += jnp.dot(grad_scores, queries, preferred_element_type=f32)
+                    grad_query = dot_tn(keys, grad_scores).T * factor
+                    sums[head, 0:1, :] += jnp.sum(grad_query, axis=0, keepdims=True)
+                    part_ref[head, rows, :] = grad_query.astype(bf16)
+
+            per_image(counts[index], run)
             return carry
 
-        lax.fori_loop(0, rows_all // SHORT, unit, 0)
-        bias_ref[1:2, :] = jnp.sum(value_acc[...], axis=0, keepdims=True)
-        out_ref[...] = query_low[...]
-
-    @pl.when(part == 1)
-    def _():
-        out_ref[...] = (key_acc[...] * factor).astype(bf16)
-
-    @pl.when(part == 2)
-    def _():
-        out_ref[...] = value_acc[...].astype(bf16)
-
-
-def attend_back(starts, counts, qkv, grad_heads, heads, factor):
-    rows = qkv.shape[0]
-
-    def spec(part):
-        return pl.BlockSpec((rows, LANES), lambda h, p, *_: (0, part * heads + h))
-
+        lax.fori_loop(0, unit_count, unit, 0)
+        for ahead in range(together):
+            head = step * together + ahead
+            sums[head, 1:2, :] = jnp.sum(value_acc[ahead], axis=0, keepdims=True)
+            part_ref[heads + head] = (key_acc[ahead] * factor).astype(bf16)
+            part_ref[2 * heads + head] = value_acc[ahead].astype(bf16)
+        return carry
+
+    lax.fori_loop(0, heads // together, some_heads, 0)
+    join_heads(part_ref, out_ref, 3 * heads)
+    bias_ref[...] = jnp.concatenate([sums[head, :, 0:HEAD_DIM] for head in range(heads)], axis=1)
+
+
+def attend_back(starts, counts, qkv, log_sums, grad_heads, heads):
+    rows, columns = qkv.shape
+    factor = HEAD_DIM ** (-0.5)
+    together = 2
     return pl.pallas_call(
-        functools.partial(attend_back_kernel, factor),
+        functools.partial(attend_back_kernel, heads, together, factor),
         out_shape=(
-            jax.ShapeDtypeStruct((rows, 3 * heads * LANES), bf16),
-            jax.ShapeDtypeStruct((8, heads * LANES), f32),
+            jax.ShapeDtypeStruct((rows, columns), bf16),
+            jax.ShapeDtypeStruct((8, heads * HEAD_DIM), f32),
         ),
-        grid_spec=pltpu.PrefetchScalarGridSpec(
-            num_scalar_prefetch=2,
-            grid=(heads, 3),
-            in_specs=[spec(0), spec(1), spec(2), spec(0)],
-            out_specs=(
-                pl.BlockSpec((rows, LANES), lambda h, p, *_: (0, p * heads + h)),
-                pl.BlockSpec((8, LANES), lambda h, p, *_: (0, h)),
-            ),
-            scratch_shapes=[
-                pltpu.VMEM((rows, LANES), f32),
-                pltpu.VMEM((rows, LANES), f32),
-                pltpu.VMEM((rows, LANES), bf16),
-            ],
-        ),
+        in_specs=[whole_spec(pltpu.SMEM), whole_spec(pltpu.SMEM)] + [whole_spec()] * 3,
+        out_specs=(whole_spec(), whole_spec()),
+        scratch_shapes=[
+            pltpu.VMEM((3 * heads, rows, LANES), bf16),
+            pltpu.VMEM((heads, rows, LANES), bf16),
+            pltpu.VMEM((together, rows, LANES), f32),
+            pltpu.VMEM((together, rows, LANES), f32),
+            pltpu.VMEM((heads, 8, LANES), f32),
+        ],
         compiler_params=pltpu.CompilerParams(vmem_limit_bytes=48 << 20),
         cost_estimate=pl.CostEstimate(flops=40 * 10**9, bytes_accessed=25 * 10**6, transcendentals=10**7),
         name="attend_back",
-    )(starts, counts, qkv, qkv, qkv, grad_heads)
+    )(starts, counts, qkv, log_sums, grad_heads)
+
+
+def reduce_kernel(
+    grid_rows,
+    first_jobs,
+    second_jobs,
+    proj_jobs,
+    one_left,
+    one_right,
+    two_left,
+    two_right,
+    three_left,
+    three_right,
+    four_left,
+    four_right,
+    mid_left,
+    mid_right,
+    in_left,
+    in_right,
+    last_left,
+    last_right,
+    bias_ref,
+    slot_ref,
+    first_out,
+    second_out,
+    proj_out,
+    bias_out,
+    slot_out,
+    stage,
+    first_left,
+    second_left,
+    first_right,
+    second_right,
+    proj_stage,
+    proj_left,
+    proj_right,
+    p0,
+    p0_got,
+    p1,
+    p1_got,
+    p2,
+    p2_got,
+    p3,
+    p3_got,
+    f0,
+    f0_turn,
+    f0_swap,
+    f1,
+    f1_got,
+    f2,
+    f2_got,
+    s0,
+    s0_got,
+    s1,
+    s1_got,
+    s2,
+    s2_turn,
+    s2_swap,
+    bias_got,
+    slot_x,
+    slot_y,
+    slot_y_got,
+    slot_z,
+    slot_z_got,
+    load_sem,
+    first_load,
+    second_load,
+    proj_load,
+    p0_sems,
+    p1_sems,
+    p2_sems,
+    p3_sems,
+    f0_sems,
+    f1_sems,
+    f2_sems,
+    s0_sems,
+    s1_sems,
+    s2_sems,
+    bias_sems,
+    slot_sems,
+    slot_z_sems,
+    first_free,
+    second_free,
+):
+    dp = lax.axis_index("dp")
+    x = lax.axis_index("tensor")
+    core = dp % 2
+    y = (dp // 2) % 2
+    z = dp // 4
+    home = core == x
+    away = core != x
+
+    def device(z_at, y_at, core_at, x_at):
+        return ((z_at * 2 + y_at) * 2 + core_at, x_at)
+
+    turn_to = device(z, y, core + (1 - 2 * core) * (1 - jnp.abs(core - x)), x + (core - x))
+    turn_from = device(z, y, x + 0 * core, x + (1 - 2 * x) * (1 - jnp.abs(core - x)))
+    swap_peer = device(z, y, x, core)
+    y_peer = device(z, 1 - y, core, x)
+
+    def z_peer(ahead):
+        return device(lax.rem(z + ahead, 4), y, core, x)
+
+    barrier = pltpu.get_barrier_semaphore()
+    near = [device(z, y, 1 - core, x), device(z, y, core, 1 - x), device(z, y, 1 - core, 1 - x), y_peer]
+    for peer in near + [z_peer(1), z_peer(2), z_peer(3)]:
+        pl.semaphore_signal(barrier, inc=1, device_id=peer, device_id_type=MESH)
+    pl.semaphore_wait(barrier, 7)
+
+    def remote(source, target, sems, index, peer):
+        return pltpu.make_async_remote_copy(
+            src_ref=source,
+            dst_ref=target,
+            send_sem=sems.at[(0,) + index],
+            recv_sem=sems.at[(1,) + index],
+            device_id=peer,
+            device_id_type=MESH,
+        )
+
+    def added(*terms):
+        total = terms[0].astype(f32)
+        for term in terms[1:]:
+            total = total + term.astype(f32)
+        return total
+
+    def load_left(source, through, target):
+        height = source.shape[1]
+        through = through if height == through.shape[1] else through.at[:, 0:height]
+        copy = pltpu.make_async_copy(source, through, load_sem)
+        copy.start()
+        copy.wait()
+
+        def block(index, carry):
+            rows = pl.ds(pl.multiple_of(index * LANES, LANES), LANES)
+            target[0:height, rows] = through[rows, :].T
+            return carry
+
+        lax.fori_loop(0, source.shape[0] // LANES, block, 0)
+
+    def right_copy(source, tile, target, sems, slot):
+        columns = pl.ds(pl.multiple_of(tile * TILE, TILE), TILE)
+        return pltpu.make_async_copy(source.at[:, columns], target.at[slot], sems.at[slot])
+
+    first_split = one_right.shape[1] // TILE
+    second_split = three_right.shape[1] // TILE
+
+    def first_right_do(job, slot, action):
+        @pl.when(job < first_split)
+        def _():
+            action(right_copy(one_right, job, first_right, first_load, slot))
+
+        @pl.when(job >= first_split)
+        def _():
+            action(right_copy(two_right, job - first_split, first_right, first_load, slot))
+
+    def second_right_do(job, slot, action):
+        @pl.when(job < second_split)
+        def _():
+            action(right_copy(three_right, job, second_right, second_load, slot))
+
+        @pl.when(job >= second_split)
+        def _():
+            action(right_copy(four_right, job - second_split, second_right, second_load, slot))
+
+    def begin(copy):
+        copy.start()
+
+    def finish(copy):
+        copy.wait()
+
+    def multiply(left, right, slot, keep):
+        def block(at_z, carry):
+            height = 4 * grid_rows
+            span = pl.ds(pl.multiple_of(at_z * height, 32), height)
+            product = jnp.dot(left[span, :], right[slot], preferred_element_type=f32)
+            for at_y in range(2):
+                for at_core in range(2):
+                    low = (at_y * 2 + at_core) * grid_rows
+                    keep(at_z, at_y, at_core, product[low : low + grid_rows, :].astype(bf16))
+            return carry
+
+        lax.fori_loop(0, 4, block, 0)
+
+    def f0_copies(slot):
+        turn = remote(f0.at[slot, 1 - x], f0_turn.at[slot], f0_sems, (0, slot), turn_to)
+        swap = remote(f0.at[slot, x], f0_swap.at[slot], f0_sems, (1, slot), swap_peer)
+        return turn, swap
+
+    def f1_copy(slot):
+        return remote(f1.at[slot, 1 - y], f1_got.at[slot], f1_sems, (slot,), y_peer)
+
+    def f2_copy(slot, ahead):
+        return remote(
+            f2.at[slot, lax.rem(z + ahead, 4)], f2_got.at[slot, ahead - 1], f2_sems, (slot, ahead - 1), z_peer(ahead)
+        )
+
+    def s0_copy(slot):
+        return remote(s0.at[slot, 1 - y], s0_got.at[slot], s0_sems, (slot,), y_peer)
+
+    def s1_copy(slot, ahead):
+        return remote(
+            s1.at[slot, lax.rem(z + ahead, 4)], s1_got.at[slot, ahead - 1], s1_sems, (slot, ahead - 1), z_peer(ahead)
+        )
+
+    def s2_copies(slot):
+        turn = remote(s2.at[slot, 1 - x], s2_turn.at[slot], s2_sems, (0, slot), turn_to)
+        swap = remote(s2.at[slot, x], s2_swap.at[slot], s2_sems, (1, slot), swap_peer)
+        return turn, swap
+
+    def inside(job, count):
+        return jnp.logical_and(job >= 0, job < count)
+
+    first_right_do(0, 0, begin)
+    second_right_do(0, 0, begin)
+
+    def first_tick(tick):
+        @pl.when(tick < first_jobs)
+        def _():
+            slot = lax.rem(tick, 2)
+            first_right_do(tick, slot, finish)
+
+            @pl.when(tick + 1 < first_jobs)
+            def _():
+                first_right_do(tick + 1, 1 - slot, begin)
+
+            @pl.when(tick == 0)
+            def _():
+                load_left(one_left, stage, first_left)
+
+            @pl.when(tick == first_split)
+            def _():
+                load_left(two_left, stage, first_left)
+
+            def keep(at_z, at_y, at_core, value):
+                f0[slot, at_core, at_y, at_z] = value
+
+            multiply(first_left, first_right, slot, keep)
+
+        last = tick - 3
+
+        @pl.when(inside(last, first_jobs))
+        def _():
+            slot = lax.rem(last, 2)
+            for ahead in (1, 2, 3):
+                f2_copy(slot, ahead).wait()
+            first_out[last] = added(f2[slot, z], f2_got[slot, 0], f2_got[slot, 1], f2_got[slot, 2])
+
+        third = tick - 2
+
+        @pl.when(inside(third, first_jobs))
+        def _():
+            slot = lax.rem(third, 2)
+            f1_copy(slot).wait()
+            f2[slot] = added(f1[slot, y], f1_got[slot]).astype(bf16)
+            for ahead in (1, 2, 3):
+                f2_copy(slot, ahead).start()
+
+        second = tick - 1
+
+        @pl.when(inside(second, first_jobs))
+        def _():
+            slot = lax.rem(second, 2)
+            turn, swap = f0_copies(slot)
+            turn.wait()
+
+            @pl.when(home)
+            def _():
+                f1[slot] = added(f0_turn[slot], f0[slot, x]).astype(bf16)
+
+            @pl.when(away)
+            def _():
+                swap.wait()
+                f1[slot] = added(f0_turn[slot], f0_swap[slot]).astype(bf16)
+
+            @pl.when(second + 2 < first_jobs)
+            def _():
+                pl.semaphore_signal(first_free, inc=1, device_id=turn_from, device_id_type=MESH)
+
+            f1_copy(slot).start()
+
+        @pl.when(tick < first_jobs)
+        def _():
+            slot = lax.rem(tick, 2)
+            turn, swap = f0_copies(slot)
+
+            @pl.when(tick >= 2)
+            def _():
+                pl.semaphore_wait(first_free, 1)
+
+            turn.start()
+
+            @pl.when(away)
+            def _():
+                swap.start()
+
+    def second_tick(tick):
+        @pl.when(tick < second_jobs)
+        def _():
+            slot = lax.rem(tick, 2)
+            second_right_do(tick, slot, finish)
+
+            @pl.when(tick + 1 < second_jobs)
+            def _():
+                second_right_do(tick + 1, 1 - slot, begin)
+
+            @pl.when(tick == 0)
+            def _():
+                load_left(three_left, stage, second_left)
+
+            @pl.when(tick == second_split)
+            def _():
+                load_left(four_left, stage, second_left)
+
+            def keep(at_z, at_y, at_core, value):
+                s0[slot, at_y, at_z, at_core] = value
+
+            multiply(second_left, second_right, slot, keep)
+
+        last = tick - 3
+
+        @pl.when(inside(last, second_jobs))
+        def _():
+            slot = lax.rem(last, 2)
+            turn, swap = s2_copies(slot)
+            turn.wait()
+
+            @pl.when(home)
+            def _():
+                second_out[last] = added(s2_turn[slot], s2[slot, x])
+
+            @pl.when(away)
+            def _():
+                swap.wait()
+                second_out[last] = added(s2_turn[slot], s2_swap[slot])
+
+            @pl.when(last + 2 < second_jobs)
+            def _():
+                pl.semaphore_signal(second_free, inc=1, device_id=turn_from, device_id_type=MESH)
+
+        third = tick - 2
+
+        @pl.when(inside(third, second_jobs))
+        def _():
+            slot = lax.rem(third, 2)
+            for ahead in (1, 2, 3):
+                s1_copy(slot, ahead).wait()
+            s2[slot] = added(s1[slot, z], s1_got[slot, 0], s1_got[slot, 1], s1_got[slot, 2]).astype(bf16)
+            turn, swap = s2_copies(slot)
+
+            @pl.when(third >= 2)
+            def _():
+                pl.semaphore_wait(second_free, 1)
+
+            turn.start()
+
+            @pl.when(away)
+            def _():
+                swap.start()
+
+        second = tick - 1
+
+        @pl.when(inside(second, second_jobs))
+        def _():
+            slot = lax.rem(second, 2)
+            s0_copy(slot).wait()
+            s1[slot] = added(s0[slot, y], s0_got[slot]).astype(bf16)
+            for ahead in (1, 2, 3):
+                s1_copy(slot, ahead).start()
+
+        @pl.when(tick < second_jobs)
+        def _():
+            s0_copy(lax.rem(tick, 2)).start()
+
+    mid_jobs = mid_right.shape[1] // TILE
+    in_jobs = -(-in_right.shape[1] // TILE)
+    in_left_over = in_right.shape[1] % TILE
+    proj_rows = mid_left.shape[1] // 32
+    last_rows = last_left.shape[1] // 32
+
+    def proj_right_do(job, slot, action):
+        def copy(source, tile, columns):
+            start = pl.multiple_of(tile * columns, LANES)
+            return pltpu.make_async_copy(
+                source.at[:, pl.ds(start, columns)], proj_right.at[slot, :, pl.ds(0, columns)], proj_load.at[slot]
+            )
+
+        @pl.when(job < mid_jobs)
+        def _():
+            action(copy(mid_right, job, TILE))
+
+        full = in_jobs - (1 if in_left_over else 0)
+
+        @pl.when(inside(job - mid_jobs, full))
+        def _():
+            action(copy(in_right, job - mid_jobs, TILE))
+
+        if in_left_over:
+
+            @pl.when(job == mid_jobs + full)
+            def _():
+                rest = pltpu.make_async_copy(
+                    in_right.at[:, pl.ds(full * TILE, in_left_over)],
+                    proj_right.at[slot, :, pl.ds(0, in_left_over)],
+                    proj_load.at[slot],
+                )
+                action(rest)
+
+        @pl.when(job >= mid_jobs + in_jobs)
+        def _():
+            action(copy(last_right, job - mid_jobs - in_jobs, 2 * TILE))
+
+    def p0_copy(slot):
+        return remote(p0.at[slot, 1 - core], p0_got.at[slot], p0_sems, (slot,), device(z, y, 1 - core, x))
+
+    def p1_copy(slot):
+        return remote(p1.at[slot, 1 - x], p1_got.at[slot], p1_sems, (slot,), device(z, y, core, 1 - x))
+
+    def p2_copy(slot):
+        return remote(p2.at[slot, 1 - y], p2_got.at[slot], p2_sems, (slot,), y_peer)
+
+    def p3_copy(slot, ahead):
+        return remote(
+            p3.at[slot, lax.rem(z + ahead, 4)], p3_got.at[slot, ahead - 1], p3_sems, (slot, ahead - 1), z_peer(ahead)
+        )
+
+    pltpu.make_async_copy(mid_right.at[:, pl.ds(0, TILE)], proj_right.at[0, :, pl.ds(0, TILE)], proj_load.at[0]).start()
+
+    def proj_tick(tick):
+        @pl.when(tick < proj_jobs)
+        def _():
+            slot = lax.rem(tick, 2)
+            proj_right_do(tick, slot, finish)
+
+            @pl.when(tick + 1 < proj_jobs)
+            def _():
+                proj_right_do(tick + 1, 1 - slot, begin)
+
+            for at, source in ((0, mid_left), (mid_jobs, in_left), (mid_jobs + in_jobs, last_left)):
+
+                @pl.when(tick == at)
+                def _(source=source):
+                    load_left(source, proj_stage, proj_left)
+
+            shares = [(at_y, at_core, at_x) for at_y in range(2) for at_core in range(2) for at_x in range(2)]
+
+            @pl.when(tick < mid_jobs + in_jobs)
+            def _():
+                def block(at_z, carry):
+                    span = pl.ds(pl.multiple_of(at_z * 8 * proj_rows, 32), 8 * proj_rows)
+                    right = proj_right[slot, :, 0:TILE]
+                    product = jnp.dot(proj_left[span, :], right, preferred_element_type=f32).astype(bf16)
+                    for low, (at_y, at_core, at_x) in enumerate(shares):
+                        p0[slot, at_core, at_x, at_y, at_z] = product[low * proj_rows : (low + 1) * proj_rows, :]
+                    return carry
+
+                lax.fori_loop(0, 4, block, 0)
+
+            @pl.when(tick >= mid_jobs + in_jobs)
+            def _():
+                def block(at_z, carry):
+                    span = pl.ds(pl.multiple_of(at_z * 8 * last_rows, 32), 8 * last_rows)
+                    for half in range(2):
+                        right = proj_right[slot, :, half * TILE : (half + 1) * TILE]
+                        product = jnp.dot(proj_left[span, :], right, preferred_element_type=f32)
+                        begin_row = half * proj_rows // 2
+                        for low, (at_y, at_core, at_x) in enumerate(shares):
+                            p0[slot, at_core, at_x, at_y, at_z, begin_row : begin_row + last_rows, :] = product[
+                                low * last_rows : (low + 1) * last_rows, :
+                            ].astype(bf16)
+                    return carry
+
+                lax.fori_loop(0, 4, block, 0)
+
+        fifth = tick - 4
+
+        @pl.when(inside(fifth, proj_jobs))
+        def _():
+            slot = lax.rem(fifth, 2)
+            for ahead in (1, 2, 3):
+                p3_copy(slot, ahead).wait()
+            proj_out[fifth] = added(p3[slot, z], p3_got[slot, 0], p3_got[slot, 1], p3_got[slot, 2])
+
+        fourth = tick - 3
+
+        @pl.when(inside(fourth, proj_jobs))
+        def _():
+            slot = lax.rem(fourth, 2)
+            p2_copy(slot).wait()
+            p3[slot] = added(p2[slot, y], p2_got[slot]).astype(bf16)
+            for ahead in (1, 2, 3):
+                p3_copy(slot, ahead).start()
+
+        third = tick - 2
+
+        @pl.when(inside(third, proj_jobs))
+        def _():
+            slot = lax.rem(third, 2)
+            p1_copy(slot).wait()
+            p2[slot] = added(p1[slot, x], p1_got[slot]).astype(bf16)
+            p2_copy(slot).start()
+
+        second = tick - 1
+
+        @pl.when(inside(second, proj_jobs))
+        def _():
+            slot = lax.rem(second, 2)
+            p0_copy(slot).wait()
+            p1[slot] = added(p0[slot, core], p0_got[slot]).astype(bf16)
+            p1_copy(slot).start()
+
+        @pl.when(tick < proj_jobs)
+        def _():
+            p0_copy(lax.rem(tick, 2)).start()
+
+    bias_peers = [
+        device(z, y, 1 - core, x),
+        device(z, y, core, 1 - x),
+        y_peer,
+        device(z + 1 - 2 * lax.rem(z, 2), y, core, x),
+        device(lax.rem(z + 2, 4), y, core, x),
+    ]
+
+    def bias_copy(step):
+        return remote(bias_out, bias_got.at[step], bias_sems, (step,), bias_peers[step])
+
+    def slot_x_copy():
+        return remote(slot_ref.at[1 - x], slot_x, slot_sems, (0,), device(z, y, core, 1 - x))
+
+    def slot_y_copy():
+        return remote(slot_y.at[1 - y], slot_y_got, slot_sems, (1,), y_peer)
+
+    def slot_z_copy(ahead):
+        return remote(
+            slot_z.at[lax.rem(z + ahead, 4)], slot_z_got.at[ahead - 1], slot_z_sems, (ahead - 1,), z_peer(ahead)
+        )
+
+    def small_tick(tick):
+        @pl.when(tick == 0)
+        def _():
+            bias_out[...] = bias_ref[...]
+            slot_x_copy().start()
+
+        for step in range(5):
+
+            @pl.when(tick == step + 1)
+            def _(step=step):
+                bias_copy(step).wait()
+                bias_out[...] = bias_out[...] + bias_got[step]
+
+        for step in range(5):
+
+            @pl.when(tick == step)
+            def _(step=step):
+                bias_copy(step).start()
+
+        @pl.when(tick == 1)
+        def _():
+            slot_x_copy().wait()
+            for at_y in range(2):
+                slot_y[at_y, x] = slot_ref[x, at_y]
+                slot_y[at_y, 1 - x] = slot_x[at_y]
+            slot_y_copy().start()
+
+        @pl.when(tick == 2)
+        def _():
+            slot_y_copy().wait()
+            for at_z in range(4):
+                slot_z[at_z, y] = slot_y[y, :, at_z]
+                slot_z[at_z, 1 - y] = slot_y_got[:, at_z]
+            for ahead in (1, 2, 3):
+                slot_z_copy(ahead).start()
+
+        @pl.when(tick == 3)
+        def _():
+            slot_out[z] = slot_z[z]
+            for ahead in (1, 2, 3):
+                slot_z_copy(ahead).wait()
+                slot_out[lax.rem(z + 4 - ahead, 4)] = slot_z_got[ahead - 1]
+
+    def tick_body(tick, carry):
+        small_tick(tick)
+        second_tick(tick)
+        proj_tick(tick)
+
+        @pl.when(lax.rem(tick, 4) != 3)
+        def _():
+            first_tick(tick // 4 * 3 + lax.rem(tick, 4))
+
+        return carry
+
+    ticks = max(second_jobs + 3, proj_jobs + 4, -(-4 * (first_jobs + 3) // 3))
+    lax.fori_loop(0, ticks, tick_body, 0)
+
+
+def reduce_grads(one, two, three, four, mid, first, last, bias, slots):
+    tokens, width = one[0].shape
+    grid_rows = width // 16
+    first_jobs = (one[1].shape[1] + two[1].shape[1]) // TILE
+    second_jobs = (three[1].shape[1] + four[1].shape[1]) // TILE
+    proj_jobs = mid[1].shape[1] // TILE + -(-first[1].shape[1] // TILE) + last[1].shape[1] // (2 * TILE)
+    proj_tokens, proj_hidden = mid[0].shape
+    proj_tile = (proj_hidden // 32, TILE)
+    tile = (grid_rows, TILE)
+    dma = pltpu.SemaphoreType.DMA
+    slot_tail = slots.shape[-2:]
+
+    def low(*lead):
+        return pltpu.VMEM(lead + tile, bf16)
+
+    scratch = [
+        pltpu.VMEM((tokens, width), bf16),
+        pltpu.VMEM((width, tokens), bf16),
+        pltpu.VMEM((width, tokens), bf16),
+        pltpu.VMEM((2, tokens, TILE), bf16),
+        pltpu.VMEM((2, tokens, TILE), bf16),
+        pltpu.VMEM((proj_tokens, proj_hidden), bf16),
+        pltpu.VMEM((proj_hidden, proj_tokens), bf16),
+        pltpu.VMEM((2, proj_tokens, 2 * TILE), bf16),
+        pltpu.VMEM((2, 2, 2, 2, 4) + proj_tile, bf16),
+        pltpu.VMEM((2, 2, 2, 4) + proj_tile, bf16),
+        pltpu.VMEM((2, 2, 2, 4) + proj_tile, bf16),
+        pltpu.VMEM((2, 2, 4) + proj_tile, bf16),
+        pltpu.VMEM((2, 2, 4) + proj_tile, bf16),
+        pltpu.VMEM((2, 4) + proj_tile, bf16),
+        pltpu.VMEM((2, 4) + proj_tile, bf16),
+        pltpu.VMEM((2, 3) + proj_tile, bf16),
+        low(2, 2, 2, 4),
+        low(2, 2, 4),
+        low(2, 2, 4),
+        low(2, 2, 4),
+        low(2, 4),
+        low(2, 4),
+        low(2, 3),
+        low(2, 2, 4, 2),
+        low(2, 4, 2),
+        low(2, 4, 2),
+        low(2, 3, 2),
+        low(2, 2),
+        low(2),
+        low(2),
+        pltpu.VMEM((5,) + bias.shape, f32),
+        pltpu.VMEM((2, 4) + slot_tail, f32),
+        pltpu.VMEM((2, 2, 4) + slot_tail, f32),
+        pltpu.VMEM((2, 4) + slot_tail, f32),
+        pltpu.VMEM((4, 2, 2) + slot_tail, f32),
+        pltpu.VMEM((3, 2, 2) + slot_tail, f32),
+        dma,
+        dma((2,)),
+        dma((2,)),
+        dma((2,)),
+        dma((2, 2)),
+        dma((2, 2)),
+        dma((2, 2)),
+        dma((2, 2, 3)),
+        dma((2, 2, 2)),
+        dma((2, 2)),
+        dma((2, 2, 3)),
+        dma((2, 2)),
+        dma((2, 2, 3)),
+        dma((2, 2, 2)),
+        dma((2, 5)),
+        dma((2, 2)),
+        dma((2, 3)),
+        pltpu.SemaphoreType.REGULAR,
+        pltpu.SemaphoreType.REGULAR,
+    ]
+    return pl.pallas_call(
+        functools.partial(reduce_kernel, grid_rows, first_jobs, second_jobs, proj_jobs),
+        out_shape=(
+            jax.ShapeDtypeStruct((first_jobs,) + tile, f32),
+            jax.ShapeDtypeStruct((second_jobs,) + tile, f32),
+            jax.ShapeDtypeStruct((proj_jobs,) + proj_tile, f32),
+            jax.ShapeDtypeStruct(bias.shape, f32),
+            jax.ShapeDtypeStruct((4, 2, 2) + slot_tail, f32),
+        ),
+        in_specs=[whole_spec(pl.ANY)] * 14 + [whole_spec()] * 2,
+        out_specs=(whole_spec(),) * 5,
+        scratch_shapes=scratch,
+        compiler_params=pltpu.CompilerParams(
+            collective_id=1, has_side_effects=True, vmem_limit_bytes=52 << 20
+        ),
+        cost_estimate=pl.CostEstimate(flops=10**11, bytes_accessed=10**8, transcendentals=0),
+        name="reduce_grads",
+    )(*one, *two, *three, *four, *mid, *first, *last, bias, slots)
 
 
 def after(value, earlier):
@@ -722,8 +1437,8 @@
     local_cols = qkv_weight.shape[2]
     local_hidden = up_weight.shape[1]
     heads = local_cols // HEAD_DIM
-    padded = heads * LANES
-    factor = HEAD_DIM ** (-0.5)
+    qkv_cols = -(-3 * local_cols // TILE) * TILE
+    out_cols = -(-local_cols // TILE) * TILE
 
     def swap(value):
         return jnp.where(home, value, send(value, to_diag))
@@ -753,9 +1468,6 @@
 
     silu_cond, silu_back = jax.vjp(jax.nn.silu, cond_low.astype(f32))
     silu_low = silu_cond.astype(bf16)
-    silu_all = lax.dynamic_update_index_in_dim(jnp.zeros((16, slots, width), bf16), silu_low, group, axis=0)
-    for move in (to_x, to_y, to_z_near, to_z_far):
-        silu_all = silu_all + send(silu_all, move)
     modulation = jnp.dot(silu_low, ada_weight, preferred_element_type=f32) + ada_bias.astype(f32)
     per_unit = jnp.dot(one_hot, modulation, precision=highest, preferred_element_type=f32)
     shift_one, scale_one, gate_one, shift_two, scale_two, gate_two = [
@@ -782,19 +1494,13 @@
     attn_in = flat((normed_one * (1.0 + scale_one) + shift_one).astype(bf16))
     attn_all = gather_cores(attn_in)
 
-    def pad_heads(array):
-        lead = array.shape[:-1]
-        shaped = array.reshape(lead + (-1, HEAD_DIM))
-        widths = [(0, 0)] * (len(lead) + 1) + [(0, LANES - HEAD_DIM)]
-        return jnp.pad(shaped, widths).reshape(lead + (-1,))
-
-    qkv_pad = pad_heads(qkv_half)
-    out_pad = jnp.pad(
-        out_half.reshape(heads, HEAD_DIM, width), ((0, 0), (0, LANES - HEAD_DIM), (0, 0))
-    ).reshape(padded, width)
-    qkv_bias = pad_heads(jnp.concatenate([qv_half[0], jnp.zeros_like(qv_half[0]), qv_half[1]]))
+    qkv_pad = jnp.pad(qkv_half, ((0, 0), (0, qkv_cols - 3 * local_cols)))
+    out_pad = jnp.pad(out_half, ((0, out_cols - local_cols), (0, 0)))
+    qkv_bias = jnp.concatenate(
+        [qv_half[0], jnp.zeros_like(qv_half[0]), qv_half[1], jnp.zeros((qkv_cols - 3 * local_cols,), f32)]
+    )
     qkv = (dot_nn(attn_all, qkv_pad) + qkv_bias).astype(bf16)
-    attended = attend(starts, counts, qkv, heads, factor)
+    attended, log_sums = attend(starts, counts, qkv, heads, out_cols)
     attn_branch = by_unit(reduce_cores(attended, out_pad, dot_nn) + out_bias.astype(f32))
     mid = resid + gate_one * attn_branch
 
@@ -825,6 +1531,12 @@
     grad_first_low = grad_first.astype(bf16)
     grad_block = by_unit(grad_out.astype(f32) + dot_nt(grad_first_low, proj_in))
 
+    silu_all = lax.dynamic_update_index_in_dim(
+        jnp.zeros((16, slots, width), bf16), after(silu_low, first_low), group, axis=0
+    )
+    for move in (to_x, to_y, to_z_near, to_z_far):
+        silu_all = silu_all + send(silu_all, move)
+
     grad_mlp_branch = gate_two * grad_block
     grad_mlp_all = gather_cores(flat(grad_mlp_branch.astype(bf16)))
     grad_pre = act_back(dot_nt(grad_mlp_all, down_half))[0]
@@ -835,55 +1547,9 @@
     grad_attn_branch = gate_one * grad_mid
     grad_attn_all = gather_cores(flat(grad_attn_branch.astype(bf16)))
     grad_heads = dot_nt(grad_attn_all, out_pad).astype(bf16)
-    grad_qkv, qkv_bias_sums = attend_back(starts, counts, qkv, grad_heads, heads, factor)
+    grad_qkv, qkv_bias_sums = attend_back(starts, counts, qkv, log_sums, grad_heads, heads)
     grad_attn_in = by_unit(reduce_cores(grad_qkv, qkv_pad, dot_nt))
     grad_tokens = grad_mid + norm_back(normed_one, inv_one, grad_attn_in * (1.0 + scale_one))
-
-    def spread(array, rows):
-        return array.reshape(2, 2, 2, 2, rows, array.shape[-1])
-
-    def over_zy(array):
-        array = halve(array, 2, y, to_y)
-        array = halve(array, 1, z_near, to_z_near)
-        return halve(array, 0, z_far, to_z_far)
-
-    def over_pair(array, axis):
-        turned = send(pick(array, 1 - x, axis), to_cycle)
-        straight = swap(pick(array, x, axis))
-        return (turned.astype(f32) + straight.astype(f32)).astype(bf16)
-
-    proj_rows = proj_in.shape[1] // 32
-    grads_in = dot_tn(grad_first_low, block_low).astype(bf16)
-    grads_mid = dot_tn(grad_second_low, first_low).astype(bf16)
-    grads_last = dot_tn(grad_last_low, second_low).astype(bf16)
-
-    def over_all(array):
-        rows = array.shape[0] // 32
-        array = array.reshape(2, 2, 2, 2, 2, rows, array.shape[1])
-        array = halve(array, 3, core, to_core)
-        array = halve(array, 2, y, to_y)
-        array = halve(array, 2, x, to_x)
-        array = halve(array, 1, z_near, to_z_near)
-        return halve(array, 0, z_far, to_z_far)
-
-    near_in = over_all(grads_in)
-    near_mid = over_all(grads_mid)
-    last = over_all(grads_last)
-
-    grads_down = dot_tn(grad_mlp_all, hidden).astype(bf16)
-    grads_up = dot_tn(mlp_all, grad_pre_low).astype(bf16)
-    row_count = width // 16
-    up_sum = over_zy(over_pair(spread(grads_up, row_count), 3))
-    down_sum = over_zy(over_pair(spread(grads_down, row_count), 3))
-
-    grads_out = dot_tn(grad_attn_all, attended).astype(bf16)
-    grads_qkv = dot_tn(attn_all, grad_qkv).astype(bf16)
-
-    def trim(array):
-        return array.reshape(array.shape[:-1] + (-1, LANES))[..., :HEAD_DIM].reshape(array.shape[:-1] + (-1,))
-
-    qkv_sum = over_pair(over_zy(spread(trim(grads_qkv), row_count)), 0)
-    out_sum = over_pair(over_zy(spread(trim(grads_out), row_count)), 0)
 
     def unit_sum(array):
         return jnp.sum(array, axis=1)
@@ -904,18 +1570,10 @@
     slot_low = slot_grad.astype(bf16)
     grad_condition = swap(silu_back(dot_nt(slot_low, ada_weight))[0])
     mod_cols = slot_low.shape[1] // 32
-    slot_cols = slot_low.reshape(slots, 2, 2, 2, 2, 2, mod_cols)
-    slot_cols = pick(slot_cols, core, 4)
-    slot_mine = lax.dynamic_update_index_in_dim(
-        jnp.zeros((16,) + slot_cols.shape, bf16), slot_cols, group, axis=0
-    )
-    for axis, bit, move in ((5, x, to_x), (4, y, to_y), (3, z_near, to_z_near), (2, z_far, to_z_far)):
-        slot_mine = pick(slot_mine, bit, axis) + send(pick(slot_mine, 1 - bit, axis), move)
-    slot_mine = slot_mine.reshape(16 * slots, mod_cols)
-    grad_ada = dot_tn(silu_all.reshape(16 * slots, width), slot_mine)
-    ada_bias_grad = jnp.sum(slot_mine.astype(f32), axis=0)
-
-    qv_sums = trim(qkv_bias_sums[:2])
+    slot_cols = pick(slot_grad.reshape(slots, 4, 2, 2, 2, mod_cols), core, 3).transpose(3, 2, 1, 0, 4)
+    slot_cols = jnp.pad(slot_cols, ((0, 0),) * 3 + ((0, 8 - slots), (0, -mod_cols % LANES)))
+
+    qv_sums = qkv_bias_sums[:2]
     qv_full = lax.dynamic_update_slice_in_dim(jnp.zeros((2, width), f32), qv_sums, core * local_cols, axis=1)
     up_full = lax.dynamic_update_slice_in_dim(
         jnp.zeros((2 * local_hidden,), f32), jnp.sum(grad_pre, axis=0), core * local_hidden, axis=0
@@ -929,9 +1587,44 @@
         jnp.sum(grad_second, axis=0),
         jnp.sum(grad_projected, axis=0),
     ]
-    sums = jnp.concatenate(pieces)
-    for move in (to_core, to_x, to_y, to_z_near, to_z_far):
-        sums = sums + send(sums, move)
+    packed = jnp.concatenate(pieces)
+    packed = jnp.pad(packed, (0, -packed.shape[0] % (8 * LANES))).reshape(-1, LANES)
+    first_sum, second_sum, proj_sum, sums, slot_sum = reduce_grads(
+        (grad_mlp_all, hidden),
+        (grad_attn_all, attended),
+        (mlp_all, grad_pre_low),
+        (attn_all, grad_qkv),
+        (grad_second_low, first_low),
+        (grad_first_low, block_low),
+        (grad_last_low, second_low),
+        packed,
+        slot_cols,
+    )
+    sums = sums.reshape(-1)
+    slot_mine = slot_sum.reshape(16, 8, -1)[:, :slots, :mod_cols].astype(bf16).reshape(16 * slots, mod_cols)
+    grad_ada = dot_tn(silu_all.reshape(16 * slots, width), slot_mine)
+    ada_bias_grad = jnp.sum(slot_mine.astype(f32), axis=0)
+    row_count = width // 16
+
+    def columns(tiles):
+        return tiles.transpose(1, 0, 2).reshape(tiles.shape[1], -1)
+
+    def rows(tiles):
+        return tiles.transpose(0, 2, 1).reshape(-1, tiles.shape[1])
+
+    down_tiles = local_hidden // TILE
+    sum_down = rows(first_sum[:down_tiles])
+    sum_out = rows(first_sum[down_tiles:])[:local_cols]
+    sum_up = columns(second_sum[:down_tiles])
+    sum_qkv = columns(second_sum[down_tiles:])[:, : 3 * local_cols].reshape(row_count, 3, local_cols)
+    mid_tiles = proj_mid.shape[0] // TILE
+    in_tiles = -(-width // TILE)
+    sum_mid = rows(proj_sum[:mid_tiles])
+    sum_in = rows(proj_sum[mid_tiles : mid_tiles + in_tiles])[:width]
+    last_share = proj_last.shape[1] // 32
+    last_tiles = proj_sum[mid_tiles + in_tiles :]
+    last_tiles = last_tiles.reshape(last_tiles.shape[0] * 2, -1, TILE)[:, :last_share]
+    sum_last = rows(last_tiles)
     found = []
     offset = 0
     for piece in pieces:
@@ -948,19 +1641,19 @@
         grad_condition,
         grad_ada,
         ada_bias_grad,
-        qkv_sum.astype(f32).reshape(row_count, 3, local_cols),
+        sum_qkv,
         qv_grad,
-        out_sum.astype(f32).T,
+        sum_out,
         found[2],
-        up_sum.astype(f32),
+        sum_up,
         up_bias_grad,
-        down_sum.astype(f32).T,
+        sum_down,
         found[3],
-        near_in.astype(f32).T,
+        sum_in,
         found[4],
-        near_mid.astype(f32).T,
+        sum_mid,
         found[5],
-        last.astype(f32).T,
+        sum_last,
         found[6],
     )
 

time: 1090 us -> 763 us (0.70)
  waiting for transfers between devices: 288 us -> 18.7 us
  Pallas kernels: 194 us -> 395 us
  local copies, waits for them, and re-layouts: 136 us -> 25.1 us
  matrix products: 258 us -> 172 us
  other arithmetic: 98.6 us -> 56.2 us
  starting transfers between devices: 99.8 us -> 87 us
    ppermute x67 -> x23, waiting for transfers between devices: 288 us -> 18.7 us  [send(): return lax.ppermute(value, ('dp', 'tensor'), pairs_of(move))]
    pallas_call x2 -> x3, Pallas kernels: 120 us -> 326 us  [the longest x1 231 us: reduce_grads(): pl.pallas_call(functools.partial(reduce_kernel, grid_rows, first_jobs, se...]
    dot_general x9 -> x2, matrix products: 67.5 us -> 1.65 us  [dot_tn(): lax.dot_general(left_arg, right_arg, (((0,), (0,)), ((), ())), precision=...]
    dynamic_slice x18 -> x1, local copies, waits for them, and re-layouts: 40.2 us -> 0.03 us  [pick(): return lax.dynamic_index_in_dim(array, index, axis=axis, keepdims=False)]
    convert_element_type x26 -> x1, other arithmetic: 30.7 us -> 0.02 us  [paired_shards(): silu_low = silu_cond.astype(bf16)]
    another operation x2 -> x0, local copies, waits for them, and re-layouts: 22.3 us -> none  [spread(): return array.reshape(2, 2, 2, 2, rows, array.shape[-1])]
    unnamed x264 -> x213, local copies, waits for them, and re-layouts: 24.1 us -> 7.91 us
    squeeze x27 -> x0, local copies, waits for them, and re-layouts: 14.1 us -> none  [pick(): return lax.dynamic_index_in_dim(array, index, axis=axis, keepdims=False)]
  transfers between devices with their start and end apart: 67 -> 23, of which waited for: 25 -> 3; matrix products, arithmetic and copies ran while one was open for 44% -> 26% of each run, Pallas kernels for 18% -> 51%
where the time goes in v2:
time: 763 us; the launch traced here: 757 us
  Pallas kernels  395 us (52%)
  matrix products  172 us (23%)
  starting transfers between devices  87 us (11%)
  other arithmetic  56.2 us (7%)
  local copies, waits for them, and re-layouts  25.1 us (3%)
  waiting for transfers between devices  18.7 us (2%)
    pallas_call x1, Pallas kernels, reduce_grads(): pl.pallas_call(functools.partial(reduce_kernel, grid_rows, first_jobs, se...  231 us
    dot_general x10, matrix products, dot_nt(): lax.dot_general(left_arg, right_arg, (((1,), (1,)), ((), ())), preferred_...  94.4 us
    ppermute x23, starting transfers between devices, send(): return lax.ppermute(value, ('dp', 'tensor'), pairs_of(move))  87 us
    pallas_call x4, Pallas kernels, gather_cores(): pl.pallas_call(gather_kernel, out_shape=jax.ShapeDtypeStruct((2, rows, wi...  68.4 us
    dot_general x9, matrix products, dot_nn(): return jnp.dot(left, right, preferred_element_type=f32)  67.5 us
    pallas_call x1, Pallas kernels, attend_back(): pl.pallas_call(functools.partial(attend_back_kernel, heads, together, fac...  55.6 us
    pallas_call x1, Pallas kernels, attend(): pl.pallas_call(functools.partial(attend_kernel, heads, 2, factor), out_sh...  39.5 us
    ppermute x23, waiting for transfers between devices, send(): return lax.ppermute(value, ('dp', 'tensor'), pairs_of(move))  18.7 us
  transfers between devices with their start and end apart: 23, of which 3 were waited for; matrix products, arithmetic and copies ran while one was open for 26% of the time, Pallas kernels for 51%

profile of v2, /device:TPU:0, one launch (start us, length us, event | category | flops | bytes accessed | tf_op | source)
XLA Modules:
  0.0 757.2 jit_solution(3521532603402105191)
XLA Ops:
  8.6 24.8 %collective-permute-start.1 = (s32[1536]{0:T(1024)S(1)}, s32[1536]{0:T(1024)S(1)}, u32[]{:S(2)}, u32[]{:S(2)}) collective-permute-start(s32[1536]{0:T(1024)S(1)} %copy-done.63), channel_id=1, source_target_pairs={{0,2},{1,3},{2,0},{3,1},{4,6},{5,7},{6,4},{7,5},{8,10},{9,11},{10,... | collective-permute-start | bytes 18440 | tf_op jit(solution)/shard_map/ppermute | solution.py:467
  40.3 8.6 %convolution_add_fusion.1 = f32[6,6912]{1,0:T(8,128)S(1)} fusion(bf16[6,1152]{1,0:T(8,128)(2,1)S(1)} %fusion.62, bf16[1152,6912]{1,0:T(8,128)(2,1)} %param.24, f32[6912]{0:T(1024)S(1)} %convert_element_type.160), kind=kOutput, calls=%fused_computation.14 | convolution fusion | flops 95592960 | bytes 16132608 | tf_op jit(solution)/shard_map/dot_general | solution.py:1471
  54.4 54.4 %gather_cores.4 = bf16[2,768,1152]{2,1,0:T(8,128)(2,1)S(1)} custom-call(bf16[768,1152]{1,0:T(8,128)(2,1)S(1)} %fusion.12.own_ref), custom_call_target="tpu_custom_call" | custom-call | bytes 12000000 | tf_op jit(solution)/shard_map/gather_cores/pallas_call | solution.py:527
  108.8 7.6 %add_convert_fusion.qkv_ref = bf16[1536,1792]{1,0:T(8,128)(2,1)S(1)} fusion(bf16[1536,1152]{1,0:T(8,128)(2,1)S(1)} %bitcast.149, f32[1792]{0:T(1024)S(1)} %concatenate.13, bf16[1152,1728]{0,1:T(8,128)(2,1)S(1)} %broadcast_select_fusion.2), kind=kOutput, calls=%fused_computation.11 | convolution fusion | flops 6347292672 | bytes 13032448 | tf_op jit(solution)/shard_map/dot_general | solution.py:1490
  116.5 39.5 %attend.1 = (bf16[1536,768]{1,0:T(8,128)(2,1)S(1)}, f32[48,1,256]{2,1,0:T(1,128)S(1)}) custom-call(s32[6]{0:T(128)S(1)} %get-tuple-element.36.starts, s32[6]{0:T(128)S(1)} %fusion.69.counts, bf16[1536,1792]{1,0:T(8,128)(2,1)S(1)} %add_convert_fusion.qkv_ref), custom_call_target="tpu_custom_call" | custom-call | flops 20000000000 | bytes 13000000 | tf_op jit(solution)/shard_map/attend/pallas_call | solution.py:603
  156.0 6.3 broadcast_select_fusion.1
  187.9 15.8 %multiply_convert_fusion = (bf16[1536,2304]{1,0:T(8,128)(2,1)}, f32[1536,2304]{1,0:T(8,128)}) fusion(f32[2304]{0:T(1024)S(1)} %slice.132, bf16[1536,1152]{1,0:T(8,128)(2,1)S(1)} %bitcast.151, bf16[1152,2304]{1,0:T(8,128)(2,1)S(1)} %bitcast.160), kind=kOutput, calls=%fused_computation.9 | convolution fusion | flops 8189116416 | bytes 30090240 | tf_op jit(solution)/shard_map/dot_general | solution.py:1490
  204.3 9.9 %fusion.28 = bf16[768,1152]{1,0:T(8,128)(2,1)} fusion(bf16[2304,1152]{1,0:T(8,128)(2,1)S(1)} %broadcast_select_fusion, bf16[1536,2304]{1,0:T(8,128)(2,1)} %get-tuple-element.162.one_right, s32[]{:T(128)S(6)} %select_n.172), kind=kOutput, calls=%fused_computation.69 | convolution fusion | flops 4077748224 | bytes 10616836 | tf_op jit(solution)/shard_map/dot_general | solution.py:1490
  214.2 28.1 %collective-permute-start.9 = (bf16[768,1152]{1,0:T(8,128)(2,1)}, bf16[768,1152]{1,0:T(8,128)(2,1)}, u32[]{:S(2)}, u32[]{:S(2)}) collective-permute-start(bf16[768,1152]{1,0:T(8,128)(2,1)} %fusion.28), channel_id=1, source_target_pairs={{0,2},{1,3},{2,0},{3,1},{4,6},{5,7},{6,4},{7,5},{8,10},{9,11},{10,... | collective-permute-start | bytes 5308424 | tf_op jit(solution)/shard_map/ppermute | solution.py:467
  266.1 9.7 %multiply_convert_fusion.2 = (bf16[768,2048]{1,0:T(8,128)(2,1)S(1)}, f32[768,2048]{1,0:T(8,128)}) fusion(f32[2048]{0:T(1024)S(1)} %convert_element_type.179, bf16[768,1152]{1,0:T(8,128)(2,1)S(1)} %get-tuple-element.135.in_right, bf16[1152,2048]{1,0:T(8,128)(2,1)} %param.34), kind=kOutput, calls=%fused_computation.21 | convolution fusion | flops 3633315840 | bytes 15933440 | tf_op jit(solution)/shard_map/dot_general | solution.py:1490
  275.9 9.3 %multiply_convert_fusion.1 = (bf16[768,2048]{1,0:T(8,128)(2,1)S(1)}, f32[768,2048]{1,0:T(8,128)}) fusion(f32[2048]{0:T(1024)S(1)} %convert_element_type.181, bf16[768,2048]{1,0:T(8,128)(2,1)S(1)} %get-tuple-element.164.mid_right, bf16[2048,2048]{1,0:T(8,128)(2,1)S(1)} %bitcast.185), kind=kOutput, calls=%fused_computation.19 | convolution fusion | flops 6451888128 | bytes 20979712 | tf_op jit(solution)/shard_map/dot_general | solution.py:1490
  294.9 14.9 %fusion.95 = (f32[2048]{0:T(1024)}, bf16[768,2048]{1,0:T(8,128)(2,1)S(1)}) fusion(f32[768,2048]{1,0:T(8,128)} %get-tuple-element.165, f32[2048]{0:T(1024)S(1)} %convert_element_type.179, bf16[768,2048]{1,0:T(8,128)(2,1)S(1)} %get-tuple-element.124.mid_left, bf16[2048,2048]{1,0:T(8,128)(2,1)} %param.36), kind=kOutput, calls=%fused_computation.205 | convolution fusion | flops 6461323264 | bytes 20987904 | tf_op jit(solution)/shard_map/dot_general | solution.py:21
  309.8 7.7 %fusion.102 = f32[768,1152]{1,0:T(8,128)S(1)} fusion(bf16[768,2048]{1,0:T(8,128)(2,1)S(1)} %get-tuple-element.126.in_left, bf16[1152,2048]{1,0:T(8,128)(2,1)} %param.34), kind=kOutput, calls=%fused_computation.209 | convolution fusion | flops 3623878656 | bytes 11403264 | tf_op jit(solution)/shard_map/dot_general | solution.py:21
  320.1 6.4 gather_cores.6
  326.6 20.7 %fusion.97 = (f32[2304]{0:T(1024)S(1)}, bf16[1536,2304]{1,0:T(8,128)(2,1)}) fusion(f32[1536,2304]{1,0:T(8,128)} %get-tuple-element.163, bf16[1536,1152]{1,0:T(8,128)(2,1)S(1)} %bitcast.153, bf16[2304,1152]{1,0:T(8,128)(2,1)S(1)} %bitcast.172), kind=kOutput, calls=%fused_computation.206 | convolution fusion | flops 8228042752 | bytes 30090240 | tf_op jit(solution)/shard_map/dot_general | solution.py:21
  347.3 8.0 %fusion.34 = bf16[768,1152]{1,0:T(8,128)(2,1)} fusion(bf16[1152,2304]{1,0:T(8,128)(2,1)S(1)} %bitcast.162, bf16[1536,2304]{1,0:T(8,128)(2,1)} %get-tuple-element.132.three_right, s32[]{:T(128)S(6)} %select_n.172), kind=kOutput, calls=%fused_computation.71 | convolution fusion | flops 4077748224 | bytes 10616836 | tf_op jit(solution)/shard_map/dot_general | solution.py:21
  357.6 7.5 collective-permute-done.19
  366.7 7.0 collective-permute-done.20
  384.2 11.4 %fusion.45 = (f32[768]{0:T(1024)S(1)}, f32[768]{0:T(1024)S(1)}, f32[768,1152]{1,0:T(8,128)}, bf16[768,1152]{1,0:T(8,128)(2,1)S(1)}) fusion(f32[3,1152]{1,0:T(4,128)S(1)} %copy-done.42, bf16[768,1152]{1,0:T(8,128)(2,1)S(1)} %collective-permute-done.14, f32[768]{0:T(1024)S(1)} %copy-done.54, f32[768,1152]{1,0:T(8,128)} %copy-done.12, f32[768]{0:T(1024)S(1)} %copy-done.50, ...), kind=kOutput, calls=%fused_computation.88 | convolution fusion | flops 4085709312 | bytes 19490308 | tf_op jit(solution)/shard_map/dot_general | solution.py:21
  405.0 55.6 %attend_back.1 = (bf16[1536,1792]{1,0:T(8,128)(2,1)}, f32[8,576]{1,0:T(8,128)S(1)}) custom-call(s32[6]{0:T(128)S(1)} %copy-done.7, s32[6]{0:T(128)S(1)} %copy-done.9, bf16[1536,1792]{1,0:T(8,128)(2,1)} %copy-done.11, f32[48,1,256]{2,1,0:T(1,128)S(1)} %get-tuple-element.44.log_ref, bf16[1536,768]{1,0:T(8,128)(2,1)S(1)} %convolution_convert_fusion.2.grad_ref), custom_call_target="tpu_custom_call" | custom-call | flops 40000000000 | bytes 25000000 | tf_op jit(solution)/shard_map/attend_back/pallas_call | solution.py:690
  460.7 6.7 convolution_convert_fusion
  473.3 6.6 fusion.44
  493.1 231.4 %reduce_grads.1 = (f32[12,72,256]{2,1,0:T(8,128)S(1)}, f32[16,72,256]{2,1,0:T(8,128)}, f32[17,64,256]{2,1,0:T(8,128)}, f32[112,128]{1,0:T(8,128)S(1)}, f32[4,2,2,8,256]{4,3,2,1,0:T(8,128)S(1)}) custom-call(bf16[1536,1152]{1,0:T(8,128)(2,1)} %bitcast.154, bf16[1536,2304]{1,0:T(8,128)(2,1)} %get-tuple-element.162.one_right, bf16[1536,1152]{1,0:T(8,128)(2,1)} %bitcast.156, ...), custom_call_target="tpu_custom_call" | custom-call | flops 99999997952 | bytes 100000000 | tf_op jit(solution)/shard_map/reduce_grads/pallas_call | solution.py:1375
  731.1 9.8 %fusion.64 = f32[6,1152]{1,0:T(8,128)S(1)} fusion(bf16[1152,6912]{1,0:T(8,128)(2,1)} %param.24, f32[6,6912]{1,0:T(8,128)S(1)} %add.310, bf16[6,1152]{1,0:T(8,128)(2,1)S(1)} %copy-done.58, bf16[6,1152]{1,0:T(8,128)(2,1)S(1)} %copy-done.60, pred[]{:T(512)S(6)} %eq.37), kind=kOutput, calls=%fused_computation.129 | convolution fusion | flops 95668992 | bytes 16146433 | tf_op jit(solution)/shard_map/dot_general | solution.py:21
  (376 shorter events, 146.6 us)
Async XLA Ops:
  0.7 284.5 %copy-start = (bf16[2048,768]{1,0:T(8,128)(2,1)S(1)}, bf16[2048,768]{1,0:T(8,128)(2,1)}, u32[]{:S(2)}) copy-start(bf16[2048,768]{1,0:T(8,128)(2,1)} %param.38) | copy-start | bytes 9437188
  0.7 2.0 collective-permute-start
  6.1 30.1 %collective-permute-start.3 = (bf16[1152,1728]{0,1:T(8,128)(2,1)}, bf16[1152,1728]{0,1:T(8,128)(2,1)}, u32[]{:S(2)}, u32[]{:S(2)}) collective-permute-start(bf16[1152,1728]{0,1:T(8,128)(2,1)} %bitcast.4), channel_id=1, source_target_pairs={{1,2},{2,1},{5,6},{6,5},{9,10},{10,9},{13,14},{14,13},{17,18},{18,... | collective-permute-start | bytes 11943944 | tf_op jit(solution)/shard_map/ppermute | solution.py:467
  8.6 26.2 %collective-permute-start.1 = (s32[1536]{0:T(1024)S(1)}, s32[1536]{0:T(1024)S(1)}, u32[]{:S(2)}, u32[]{:S(2)}) collective-permute-start(s32[1536]{0:T(1024)S(1)} %copy-done.63), channel_id=1, source_target_pairs={{0,2},{1,3},{2,0},{3,1},{4,6},{5,7},{6,4},{7,5},{8,10},{9,11},{10,... | collective-permute-start | bytes 18440 | tf_op jit(solution)/shard_map/ppermute | solution.py:467
  33.5 6.2 collective-permute-start.2
  34.1 1.9 collective-permute-start.4
  38.9 10.4 %collective-permute-start.5 = (bf16[576,1152]{1,0:T(8,128)(2,1)S(1)}, bf16[576,1152]{1,0:T(8,128)(2,1)S(1)}, u32[]{:S(2)}, u32[]{:S(2)}) collective-permute-start(bf16[576,1152]{1,0:T(8,128)(2,1)S(1)} %copy-done.33), channel_id=1, source_target_pairs={{1,2},{2,1},{5,6},{6,5},{9,10},{10,9},{13,14},{14,13},{17,18},{18,... | collective-permute-start | bytes 3981320 | tf_op jit(solution)/shard_map/ppermute | solution.py:467
  49.6 106.4 %collective-permute-start.7 = (bf16[1152,2304]{1,0:T(8,128)(2,1)S(1)}, bf16[1152,2304]{1,0:T(8,128)(2,1)}, u32[]{:S(2)}, u32[]{:S(2)}) collective-permute-start(bf16[1152,2304]{1,0:T(8,128)(2,1)S(1)} %bitcast.168), channel_id=1, source_target_pairs={{1,2},{2,1},{5,6},{6,5},{9,10},{10,9},{13,14},{14,13},{17,18},{18,... | collective-permute-start | bytes 15925256 | tf_op jit(solution)/shard_map/ppermute | solution.py:467
  162.3 41.4 %collective-permute-start.8 = (bf16[2304,1152]{1,0:T(8,128)(2,1)}, bf16[2304,1152]{1,0:T(8,128)(2,1)}, u32[]{:S(2)}, u32[]{:S(2)}) collective-permute-start(bf16[2304,1152]{1,0:T(8,128)(2,1)} %param.32), channel_id=1, source_target_pairs={{1,2},{2,1},{5,6},{6,5},{9,10},{10,9},{13,14},{14,13},{17,18},{18,... | collective-permute-start | bytes 15925256 | tf_op jit(solution)/shard_map/ppermute | solution.py:467
  168.6 9.3 %collective-permute-start.6 = (bf16[768,1152]{1,0:T(8,128)(2,1)}, bf16[768,1152]{1,0:T(8,128)(2,1)}, u32[]{:S(2)}, u32[]{:S(2)}) collective-permute-start(bf16[768,1152]{1,0:T(8,128)(2,1)} %convolution_convert_fusion.3), channel_id=1, source_target_pairs={{0,2},{1,3},{2,0},{3,1},{4,6},{5,7},{6,4},{7,5},{8,10},{9,11},{10,... | collective-permute-start | bytes 5308424 | tf_op jit(solution)/shard_map/ppermute | solution.py:467
  174.3 68.0 %collective-permute-start.13 = (bf16[1536,768]{1,0:T(8,128)(2,1)}, bf16[1536,768]{1,0:T(8,128)(2,1)}, u32[]{:S(2)}, u32[]{:S(2)}) collective-permute-start(bf16[1536,768]{1,0:T(8,128)(2,1)} %param.40), channel_id=1, source_target_pairs={{0,2},{1,3},{2,0},{3,1},{4,6},{5,7},{6,4},{7,5},{8,10},{9,11},{10,... | collective-permute-start | bytes 7077896 | tf_op jit(solution)/shard_map/ppermute | solution.py:467
  214.2 46.1 %collective-permute-start.9 = (bf16[768,1152]{1,0:T(8,128)(2,1)}, bf16[768,1152]{1,0:T(8,128)(2,1)}, u32[]{:S(2)}, u32[]{:S(2)}) collective-permute-start(bf16[768,1152]{1,0:T(8,128)(2,1)} %fusion.28), channel_id=1, source_target_pairs={{0,2},{1,3},{2,0},{3,1},{4,6},{5,7},{6,4},{7,5},{8,10},{9,11},{10,... | collective-permute-start | bytes 5308424 | tf_op jit(solution)/shard_map/ppermute | solution.py:467
  245.6 8.4 %collective-permute-start.12 = (s32[768]{0:T(1024)S(1)}, s32[768]{0:T(1024)S(1)}, u32[]{:S(2)}, u32[]{:S(2)}) collective-permute-start(s32[768]{0:T(1024)S(1)} %copy-done.73), channel_id=1, source_target_pairs={{1,2},{2,1},{5,6},{6,5},{9,10},{10,9},{13,14},{14,13},{17,18},{18,... | collective-permute-start | bytes 9224 | tf_op jit(solution)/shard_map/ppermute | solution.py:467
  252.2 65.4 %collective-permute-start.11 = (bf16[768,1152]{1,0:T(8,128)(2,1)}, bf16[768,1152]{1,0:T(8,128)(2,1)}, u32[]{:S(2)}, u32[]{:S(2)}) collective-permute-start(bf16[768,1152]{1,0:T(8,128)(2,1)} %param.43), channel_id=1, source_target_pairs={{1,2},{2,1},{5,6},{6,5},{9,10},{10,9},{13,14},{14,13},{17,18},{18,... | collective-permute-start | bytes 5308424 | tf_op jit(solution)/shard_map/ppermute | solution.py:467
  355.3 28.9 %collective-permute-start.14 = (bf16[768,1152]{1,0:T(8,128)(2,1)}, bf16[768,1152]{1,0:T(8,128)(2,1)S(1)}, u32[]{:S(2)}, u32[]{:S(2)}) collective-permute-start(bf16[768,1152]{1,0:T(8,128)(2,1)} %fusion.34), channel_id=1, source_target_pairs={{0,2},{1,3},{2,0},{3,1},{4,6},{5,7},{6,4},{7,5},{8,10},{9,11},{10,... | collective-permute-start | bytes 5308424 | tf_op jit(solution)/shard_map/ppermute | solution.py:467
  355.7 9.4 %collective-permute-start.19 = (bf16[16,6,1152]{2,1,0:T(8,128)(2,1)S(1)}, bf16[16,6,1152]{2,1,0:T(8,128)(2,1)S(1)}, u32[]{:S(2)}, u32[]{:S(2)}) collective-permute-start(bf16[16,6,1152]{2,1,0:T(8,128)(2,1)S(1)} %bitcast_dynamic-update-slice_fusion), channel_id=1, source_target_pairs={{0,1},{1,0},{2,3},{3,2},{4,5},{5,4},{6,7},{7,6},{8,9},{9,8},{10,11... | collective-permute-start | bytes 663560 | tf_op jit(solution)/shard_map/ppermute | solution.py:467
  365.1 8.6 %collective-permute-start.20 = (bf16[16,6,1152]{2,1,0:T(8,128)(2,1)S(1)}, bf16[16,6,1152]{2,1,0:T(8,128)(2,1)S(1)}, u32[]{:S(2)}, u32[]{:S(2)}) collective-permute-start(bf16[16,6,1152]{2,1,0:T(8,128)(2,1)S(1)} %fusion.68), channel_id=1, source_target_pairs={{0,4},{1,5},{2,6},{3,7},{4,0},{5,1},{6,2},{7,3},{8,12},{9,13},{10,... | collective-permute-start | bytes 663560 | tf_op jit(solution)/shard_map/ppermute | solution.py:467
  373.8 7.7 %collective-permute-start.21 = (bf16[16,6,1152]{2,1,0:T(8,128)(2,1)S(1)}, bf16[16,6,1152]{2,1,0:T(8,128)(2,1)S(1)}, u32[]{:S(2)}, u32[]{:S(2)}) collective-permute-start(bf16[16,6,1152]{2,1,0:T(8,128)(2,1)S(1)} %add.313), channel_id=1, source_target_pairs={{0,8},{1,9},{2,10},{3,11},{4,12},{5,13},{6,14},{7,15},{8,0},{9,1},... | collective-permute-start | bytes 663560 | tf_op jit(solution)/shard_map/ppermute | solution.py:467
  375.4 94.8 %collective-permute-start.10 = (bf16[768,1152]{1,0:T(8,128)(2,1)}, bf16[768,1152]{1,0:T(8,128)(2,1)}, u32[]{:S(2)}, u32[]{:S(2)}) collective-permute-start(bf16[768,1152]{1,0:T(8,128)(2,1)} %copy-done.28), channel_id=1, source_target_pairs={{1,2},{2,1},{5,6},{6,5},{9,10},{10,9},{13,14},{14,13},{17,18},{18,... | collective-permute-start | bytes 5308424 | tf_op jit(solution)/shard_map/ppermute | solution.py:467
  381.5 86.4 %collective-permute-start.22 = (bf16[16,6,1152]{2,1,0:T(8,128)(2,1)S(1)}, bf16[16,6,1152]{2,1,0:T(8,128)(2,1)}, u32[]{:S(2)}, u32[]{:S(2)}) collective-permute-start(bf16[16,6,1152]{2,1,0:T(8,128)(2,1)S(1)} %add.314), channel_id=1, source_target_pairs={{0,16},{1,17},{2,18},{3,19},{4,20},{5,21},{6,22},{7,23},{8,24},{9,... | collective-permute-start | bytes 663560 | tf_op jit(solution)/shard_map/ppermute | solution.py:467
  467.4 5.8 collective-permute-start.15
  485.9 6.7 collective-permute-start.17
  490.7 262.3 %collective-permute-start.16 = (bf16[768,1152]{1,0:T(8,128)(2,1)}, bf16[768,1152]{1,0:T(8,128)(2,1)}, u32[]{:S(2)}, u32[]{:S(2)}) collective-permute-start(bf16[768,1152]{1,0:T(8,128)(2,1)} %add_convert_fusion.1), channel_id=1, source_target_pairs={{1,2},{2,1},{5,6},{6,5},{9,10},{10,9},{13,14},{14,13},{17,18},{18,... | collective-permute-start | bytes 5308424 | tf_op jit(solution)/shard_map/ppermute | solution.py:467
  740.9 11.4 %collective-permute-start.18 = (f32[6,1152]{1,0:T(8,128)S(1)}, f32[6,1152]{1,0:T(8,128)S(1)}, u32[]{:S(2)}, u32[]{:S(2)}) collective-permute-start(f32[6,1152]{1,0:T(8,128)S(1)} %fusion.64), channel_id=1, source_target_pairs={{1,2},{2,1},{5,6},{6,5},{9,10},{10,9},{13,14},{14,13},{17,18},{18,... | collective-permute-start | bytes 82952 | tf_op jit(solution)/shard_map/ppermute | solution.py:467
  (95 other events, 2139.8 us)

commit v3 on v2

--- a/solution.py
+++ b/solution.py
@@ -487,6 +487,10 @@
     return (z, 1 - y, c, x)
 
 
+def to_swapped_y(z, y, c, x):
+    return (z, 1 - y, c, x) if c != x else (z, y, c, x)
+
+
 def to_z_near(z, y, c, x):
     return (z ^ 1, y, c, x)
 
@@ -729,11 +733,16 @@
     last_right,
     bias_ref,
     slot_ref,
+    silu_ref,
+    slot_low_ref,
+    ada_ref,
     first_out,
     second_out,
     proj_out,
     bias_out,
     slot_out,
+    silu_out,
+    cond_out,
     stage,
     first_left,
     second_left,
@@ -770,6 +779,13 @@
     slot_y_got,
     slot_z,
     slot_z_got,
+    silu_x,
+    silu_y,
+    silu_y_got,
+    silu_z,
+    silu_z_got,
+    ada_tile,
+    cond_acc,
     load_sem,
     first_load,
     second_load,
@@ -787,6 +803,10 @@
     bias_sems,
     slot_sems,
     slot_z_sems,
+    silu_sems,
+    silu_z_sems,
+    ada_sems,
+    cond_sems,
     first_free,
     second_free,
 ):
@@ -1242,11 +1262,21 @@
             slot_z.at[lax.rem(z + ahead, 4)], slot_z_got.at[ahead - 1], slot_z_sems, (ahead - 1,), z_peer(ahead)
         )
 
+    def silu_x_copy():
+        return remote(silu_ref, silu_x, silu_sems, (0,), device(z, y, core, 1 - x))
+
+    def silu_y_copy():
+        return remote(silu_y, silu_y_got, silu_sems, (1,), y_peer)
+
+    def silu_z_copy(ahead):
+        return remote(silu_z, silu_z_got.at[ahead - 1], silu_z_sems, (ahead - 1,), z_peer(ahead))
+
     def small_tick(tick):
         @pl.when(tick == 0)
         def _():
             bias_out[...] = bias_ref[...]
             slot_x_copy().start()
+            silu_x_copy().start()
 
         for step in range(5):
 
@@ -1268,6 +1298,10 @@
                 slot_y[at_y, x] = slot_ref[x, at_y]
                 slot_y[at_y, 1 - x] = slot_x[at_y]
             slot_y_copy().start()
+            silu_x_copy().wait()
+            silu_y[x] = silu_ref[...]
+            silu_y[1 - x] = silu_x[...]
+            silu_y_copy().start()
 
         @pl.when(tick == 2)
         def _():
@@ -1275,18 +1309,66 @@
             for at_z in range(4):
                 slot_z[at_z, y] = slot_y[y, :, at_z]
                 slot_z[at_z, 1 - y] = slot_y_got[:, at_z]
+            silu_y_copy().wait()
+            silu_z[y] = silu_y[...]
+            silu_z[1 - y] = silu_y_got[...]
             for ahead in (1, 2, 3):
                 slot_z_copy(ahead).start()
+                silu_z_copy(ahead).start()
 
         @pl.when(tick == 3)
         def _():
             slot_out[z] = slot_z[z]
+            silu_out[z] = silu_z[...]
             for ahead in (1, 2, 3):
                 slot_z_copy(ahead).wait()
                 slot_out[lax.rem(z + 4 - ahead, 4)] = slot_z_got[ahead - 1]
+                silu_z_copy(ahead).wait()
+                silu_out[lax.rem(z + 4 - ahead, 4)] = silu_z_got[ahead - 1]
+
+    ada_cols = ada_tile.shape[2]
+    ada_tiles = ada_ref.shape[1] // ada_cols
+    cond_copy = remote(cond_acc, cond_out, cond_sems, (), swap_peer)
+
+    def ada_copy(tile, slot):
+        columns = pl.ds(pl.multiple_of(tile * ada_cols, LANES), ada_cols)
+        return pltpu.make_async_copy(ada_ref.at[:, columns], ada_tile.at[slot], ada_sems.at[slot])
+
+    def cond_tick(tick):
+        tile = tick - 4
+
+        @pl.when(tile == -1)
+        def _():
+            cond_acc[...] = jnp.zeros_like(cond_acc)
+
+        @pl.when(inside(tile + 1, ada_tiles))
+        def _():
+            ada_copy(tile + 1, lax.rem(tile + 1, 2)).start()
+
+        @pl.when(inside(tile, ada_tiles))
+        def _():
+            slot = lax.rem(tile, 2)
+            ada_copy(tile, slot).wait()
+            columns = pl.ds(pl.multiple_of(tile * ada_cols, LANES), ada_cols)
+            cond_acc[...] += dot_nt(slot_low_ref[:, columns], ada_tile[slot])
+
+        @pl.when(tile == ada_tiles)
+        def _():
+            @pl.when(home)
+            def _():
+                cond_out[...] = cond_acc[...]
+
+            @pl.when(away)
+            def _():
+                cond_copy.start()
+
+        @pl.when(jnp.logical_and(tile == ada_tiles + 1, away))
+        def _():
+            cond_copy.wait()
 
     def tick_body(tick, carry):
         small_tick(tick)
+        cond_tick(tick)
         second_tick(tick)
         proj_tick(tick)
 
@@ -1296,11 +1378,11 @@
 
         return carry
 
-    ticks = max(second_jobs + 3, proj_jobs + 4, -(-4 * (first_jobs + 3) // 3))
+    ticks = max(second_jobs + 3, proj_jobs + 4, ada_tiles + 6, -(-4 * (first_jobs + 3) // 3))
     lax.fori_loop(0, ticks, tick_body, 0)
 
 
-def reduce_grads(one, two, three, four, mid, first, last, bias, slots):
+def reduce_grads(one, two, three, four, mid, first, last, bias, slots, silu, slot_low, ada_weight):
     tokens, width = one[0].shape
     grid_rows = width // 16
     first_jobs = (one[1].shape[1] + two[1].shape[1]) // TILE
@@ -1352,6 +1434,13 @@
         pltpu.VMEM((2, 4) + slot_tail, f32),
         pltpu.VMEM((4, 2, 2) + slot_tail, f32),
         pltpu.VMEM((3, 2, 2) + slot_tail, f32),
+        pltpu.VMEM(silu.shape, bf16),
+        pltpu.VMEM((2,) + silu.shape, bf16),
+        pltpu.VMEM((2,) + silu.shape, bf16),
+        pltpu.VMEM((2, 2) + silu.shape, bf16),
+        pltpu.VMEM((3, 2, 2) + silu.shape, bf16),
+        pltpu.VMEM((2, ada_weight.shape[0], ada_weight.shape[1] // 9), bf16),
+        pltpu.VMEM((8, ada_weight.shape[0]), f32),
         dma,
         dma((2,)),
         dma((2,)),
@@ -1369,6 +1458,10 @@
         dma((2, 5)),
         dma((2, 2)),
         dma((2, 3)),
+        dma((2, 2)),
+        dma((2, 3)),
+        dma((2,)),
+        dma((2,)),
         pltpu.SemaphoreType.REGULAR,
         pltpu.SemaphoreType.REGULAR,
     ]
@@ -1380,16 +1473,202 @@
             jax.ShapeDtypeStruct((proj_jobs,) + proj_tile, f32),
             jax.ShapeDtypeStruct(bias.shape, f32),
             jax.ShapeDtypeStruct((4, 2, 2) + slot_tail, f32),
+            jax.ShapeDtypeStruct((4, 2, 2) + silu.shape, bf16),
+            jax.ShapeDtypeStruct((8, ada_weight.shape[0]), f32),
         ),
-        in_specs=[whole_spec(pl.ANY)] * 14 + [whole_spec()] * 2,
-        out_specs=(whole_spec(),) * 5,
+        in_specs=[whole_spec(pl.ANY)] * 14 + [whole_spec()] * 4 + [whole_spec(pl.ANY)],
+        out_specs=(whole_spec(),) * 7,
         scratch_shapes=scratch,
         compiler_params=pltpu.CompilerParams(
             collective_id=1, has_side_effects=True, vmem_limit_bytes=52 << 20
         ),
         cost_estimate=pl.CostEstimate(flops=10**11, bytes_accessed=10**8, transcendentals=0),
         name="reduce_grads",
-    )(*one, *two, *three, *four, *mid, *first, *last, bias, slots)
+    )(*one, *two, *three, *four, *mid, *first, *last, bias, slots, silu, slot_low, ada_weight)
+
+
+def fetch_kernel(
+    tokens_ref,
+    qkv_ref,
+    cond_ref,
+    ada_ref,
+    ada_bias_ref,
+    tokens_out,
+    qkv_out,
+    cond_out,
+    mod_out,
+    ada_tile,
+    token_hold,
+    qkv_hold,
+    token_sems,
+    cond_sems,
+    x_sems,
+    y_sems,
+    z_sems,
+    local_sems,
+    ada_sems,
+):
+    dp = lax.axis_index("dp")
+    x = lax.axis_index("tensor")
+    core = dp % 2
+    y = (dp // 2) % 2
+    z = dp // 4
+    z_near = lax.rem(z, 2)
+    home = core == x
+    away = core != x
+    pieces = x_sems.shape[1]
+    quarter = qkv_ref.shape[0] // 4
+    height = quarter // pieces
+
+    def device(z_at, y_at, core_at, x_at):
+        return ((z_at * 2 + y_at) * 2 + core_at, x_at)
+
+    core_peer = device(z, y, 1 - core, x)
+    swap_peer = device(z, y, x, core)
+    y_peer = device(z, 1 - y, core, x)
+    z_peer = device(z + 1 - 2 * z_near, y, core, x)
+    barrier = pltpu.get_barrier_semaphore()
+    peers = [core_peer, device(z, y, core, 1 - x), device(z, y, 1 - core, 1 - x), y_peer, z_peer]
+    for peer in peers:
+        pl.semaphore_signal(barrier, inc=1, device_id=peer, device_id_type=MESH)
+    pl.semaphore_wait(barrier, len(peers))
+
+    def remote(source, target, sems, index, peer):
+        return pltpu.make_async_remote_copy(
+            src_ref=source,
+            dst_ref=target,
+            send_sem=sems.at[(0,) + index],
+            recv_sem=sems.at[(1,) + index],
+            device_id=peer,
+            device_id_type=MESH,
+        )
+
+    def span(y_at, piece):
+        return pl.ds(pl.multiple_of((y_at * 2 + z_near) * quarter + piece * height, 32), height)
+
+    def x_copy(piece):
+        return remote(qkv_ref.at[span(y, piece), :], qkv_out.at[span(y, piece), :], x_sems, (piece,), swap_peer)
+
+    def y_copy(piece):
+        return remote(qkv_out.at[span(y, piece), :], qkv_out.at[span(y, piece), :], y_sems, (piece,), y_peer)
+
+    def z_copy(piece, other):
+        y_at = 1 - y if other else y
+        rows = span(y_at, piece)
+        return remote(qkv_out.at[rows, :], qkv_out.at[rows, :], z_sems, (int(other), piece), z_peer)
+
+    token_copy = remote(tokens_ref, tokens_out, token_sems, (), swap_peer)
+    cond_copy = remote(cond_ref, cond_out, cond_sems, (), core_peer)
+    local_in = [
+        pltpu.make_async_copy(tokens_ref, token_hold, local_sems.at[0]),
+        pltpu.make_async_copy(qkv_ref, qkv_hold, local_sems.at[1]),
+    ]
+    local_out = [
+        pltpu.make_async_copy(token_hold, tokens_out, local_sems.at[2]),
+        pltpu.make_async_copy(qkv_hold, qkv_out, local_sems.at[3]),
+    ]
+
+    @pl.when(away)
+    def _():
+        for piece in range(pieces):
+            x_copy(piece).start()
+        token_copy.start()
+
+    @pl.when(home)
+    def _():
+        cond_copy.start()
+        for copy in local_in:
+            copy.start()
+        cond_out[...] = cond_ref[...]
+
+    tile_cols = ada_tile.shape[2]
+    tiles = ada_ref.shape[1] // tile_cols
+
+    def ada_copy(tile, slot):
+        columns = pl.ds(pl.multiple_of(tile * tile_cols, LANES), tile_cols)
+        return pltpu.make_async_copy(ada_ref.at[:, columns], ada_tile.at[slot], ada_sems.at[slot])
+
+    ada_copy(0, 0).start()
+
+    @pl.when(away)
+    def _():
+        cond_copy.wait_recv()
+
+    cond = cond_out[...].astype(f32)
+    low = (cond / (1.0 + jnp.exp(-cond))).astype(bf16)
+
+    def modulate(tile, carry):
+        slot = lax.rem(tile, 2)
+        ada_copy(tile, slot).wait()
+
+        @pl.when(tile + 1 < tiles)
+        def _():
+            ada_copy(tile + 1, 1 - slot).start()
+
+        columns = pl.ds(pl.multiple_of(tile * tile_cols, LANES), tile_cols)
+        product = jnp.dot(low, ada_tile[slot], preferred_element_type=f32)
+        mod_out[:, columns] = product + ada_bias_ref[:, columns].astype(f32)
+        return carry
+
+    lax.fori_loop(0, tiles, modulate, 0)
+
+    @pl.when(away)
+    def _():
+        for piece in range(pieces):
+            x_copy(piece).wait_recv()
+            y_copy(piece).start()
+            z_copy(piece, False).start()
+        for piece in range(pieces):
+            y_copy(piece).wait_recv()
+            z_copy(piece, True).start()
+        token_copy.wait()
+        for piece in range(pieces):
+            x_copy(piece).wait_send()
+            y_copy(piece).wait_send()
+            z_copy(piece, False).wait()
+            z_copy(piece, True).wait()
+
+    @pl.when(home)
+    def _():
+        cond_copy.wait_send()
+        for copy, onward in zip(local_in, local_out):
+            copy.wait()
+            onward.start()
+        for copy in local_out:
+            copy.wait()
+
+
+def fetch(tokens, qkv, condition, ada_weight, ada_bias):
+    pieces = 3
+    dma = pltpu.SemaphoreType.DMA
+    return pl.pallas_call(
+        fetch_kernel,
+        out_shape=(
+            jax.ShapeDtypeStruct(tokens.shape, bf16),
+            jax.ShapeDtypeStruct(qkv.shape, bf16),
+            jax.ShapeDtypeStruct(condition.shape, bf16),
+            jax.ShapeDtypeStruct((condition.shape[0], ada_weight.shape[1]), f32),
+        ),
+        in_specs=[whole_spec(pl.ANY), whole_spec(pl.ANY), whole_spec(), whole_spec(pl.ANY), whole_spec()],
+        out_specs=(whole_spec(pl.ANY), whole_spec(pl.ANY), whole_spec(), whole_spec()),
+        scratch_shapes=[
+            pltpu.VMEM((2, ada_weight.shape[0], ada_weight.shape[1] // 9), bf16),
+            pltpu.VMEM(tokens.shape, bf16),
+            pltpu.VMEM(qkv.shape, bf16),
+            dma((2,)),
+            dma((2,)),
+            dma((2, pieces)),
+            dma((2, pieces)),
+            dma((2, 2, pieces)),
+            dma((4,)),
+            dma((2,)),
+        ],
+        compiler_params=pltpu.CompilerParams(
+            collective_id=2, has_side_effects=True, vmem_limit_bytes=56 << 20
+        ),
+        cost_estimate=pl.CostEstimate(flops=10**10, bytes_accessed=3 * 10**7, transcendentals=0),
+        name="fetch",
+    )(tokens, qkv, condition, ada_weight, ada_bias.reshape(1, -1))
 
 
 def after(value, earlier):
@@ -1443,17 +1722,31 @@
     def swap(value):
         return jnp.where(home, value, send(value, to_diag))
 
-    tokens = swap(tokens_in)
+    tokens, qkv_half, cond_low, modulation = fetch(
+        tokens_in, qkv_weight.reshape(width, 3 * local_cols), condition, ada_weight, ada_bias
+    )
     packed_ids = send(image_ids, to_core)
     ids = jnp.where(home, image_ids, packed_ids)
-    cond_low = jnp.where(home, condition, send(condition, to_core))
-    qkv_half = swap(after(qkv_weight.reshape(width, 3 * local_cols), tokens))
-    out_half = swap(after(out_weight, qkv_half))
-    up_half = swap(after(up_weight, out_half))
-    down_half = swap(after(down_weight, up_half))
+
+    def over_x(weight, earlier):
+        own = lax.dynamic_slice_in_dim(weight, y * (weight.shape[0] // 2), weight.shape[0] // 2)
+        return send(after(own, earlier), to_diag)
+
+    def over_y(weight, first):
+        second = send(first, to_swapped_y)
+        first, second, whole = lax.optimization_barrier((first, second, weight))
+        halves = whole.reshape((2,) + first.shape)
+        mine = jnp.arange(2).reshape(2, 1, 1) == y
+        return jnp.where(home, halves, jnp.where(mine, first[None], second[None])).reshape(weight.shape)
+
+    out_first = over_x(out_weight, tokens)
+    up_first = over_x(up_weight, tokens)
+    down_first = over_x(down_weight, up_first)
+    out_half = over_y(out_weight, out_first)
+    up_half = over_y(up_weight, up_first)
     features = jnp.where(home, enc_features, send(enc_features, to_core))
-    rows_low = swap(after(target_rows, down_half))
-    grad_out = swap(after(out_grad, down_half))
+    rows_low = swap(after(target_rows, up_first))
+    grad_out = swap(after(out_grad, down_first))
     bias_pack = jnp.concatenate([qv_bias.reshape(-1), up_bias])
     bias_half = swap(bias_pack).astype(f32)
     qv_half = bias_half[: 2 * local_cols].reshape(2, local_cols)
@@ -1466,9 +1759,7 @@
     my_units = lax.dynamic_slice_in_dim(unit_ids, core * units, units)
     one_hot = (my_units[:, None] == jnp.arange(slots, dtype=jnp.int32)[None, :]).astype(f32)
 
-    silu_cond, silu_back = jax.vjp(jax.nn.silu, cond_low.astype(f32))
-    silu_low = silu_cond.astype(bf16)
-    modulation = jnp.dot(silu_low, ada_weight, preferred_element_type=f32) + ada_bias.astype(f32)
+    silu_low = jax.nn.silu(cond_low.astype(f32)).astype(bf16)
     per_unit = jnp.dot(one_hot, modulation, precision=highest, preferred_element_type=f32)
     shift_one, scale_one, gate_one, shift_two, scale_two, gate_two = [
         piece[:, None, :] for piece in jnp.split(per_unit, 6, axis=1)
@@ -1500,7 +1791,10 @@
         [qv_half[0], jnp.zeros_like(qv_half[0]), qv_half[1], jnp.zeros((qkv_cols - 3 * local_cols,), f32)]
     )
     qkv = (dot_nn(attn_all, qkv_pad) + qkv_bias).astype(bf16)
+    qkv = after(qkv, (out_first, up_first))
     attended, log_sums = attend(starts, counts, qkv, heads, out_cols)
+    attended, down_first = lax.optimization_barrier((attended, down_first))
+    down_half = over_y(down_weight, down_first)
     attn_branch = by_unit(reduce_cores(attended, out_pad, dot_nn) + out_bias.astype(f32))
     mid = resid + gate_one * attn_branch
 
@@ -1531,12 +1825,6 @@
     grad_first_low = grad_first.astype(bf16)
     grad_block = by_unit(grad_out.astype(f32) + dot_nt(grad_first_low, proj_in))
 
-    silu_all = lax.dynamic_update_index_in_dim(
-        jnp.zeros((16, slots, width), bf16), after(silu_low, first_low), group, axis=0
-    )
-    for move in (to_x, to_y, to_z_near, to_z_far):
-        silu_all = silu_all + send(silu_all, move)
-
     grad_mlp_branch = gate_two * grad_block
     grad_mlp_all = gather_cores(flat(grad_mlp_branch.astype(bf16)))
     grad_pre = act_back(dot_nt(grad_mlp_all, down_half))[0]
@@ -1568,7 +1856,6 @@
     slot_part = dot_tn(one_hot, mod_units, precision=highest)
     slot_grad = slot_part + send(slot_part, to_core)
     slot_low = slot_grad.astype(bf16)
-    grad_condition = swap(silu_back(dot_nt(slot_low, ada_weight))[0])
     mod_cols = slot_low.shape[1] // 32
     slot_cols = pick(slot_grad.reshape(slots, 4, 2, 2, 2, mod_cols), core, 3).transpose(3, 2, 1, 0, 4)
     slot_cols = jnp.pad(slot_cols, ((0, 0),) * 3 + ((0, 8 - slots), (0, -mod_cols % LANES)))
@@ -1589,7 +1876,7 @@
     ]
     packed = jnp.concatenate(pieces)
     packed = jnp.pad(packed, (0, -packed.shape[0] % (8 * LANES))).reshape(-1, LANES)
-    first_sum, second_sum, proj_sum, sums, slot_sum = reduce_grads(
+    first_sum, second_sum, proj_sum, sums, slot_sum, silu_sum, cond_sum = reduce_grads(
         (grad_mlp_all, hidden),
         (grad_attn_all, attended),
         (mlp_all, grad_pre_low),
@@ -1599,10 +1886,14 @@
         (grad_last_low, second_low),
         packed,
         slot_cols,
-    )
+        jnp.pad(silu_low, ((0, 8 - slots), (0, 0))),
+        jnp.pad(slot_low, ((0, 8 - slots), (0, 0))),
+        ada_weight,
+    )
+    grad_condition = jax.vjp(jax.nn.silu, condition.astype(f32))[1](cond_sum[:slots])[0]
     sums = sums.reshape(-1)
     slot_mine = slot_sum.reshape(16, 8, -1)[:, :slots, :mod_cols].astype(bf16).reshape(16 * slots, mod_cols)
-    grad_ada = dot_tn(silu_all.reshape(16 * slots, width), slot_mine)
+    grad_ada = dot_tn(silu_sum.reshape(16, 8, width)[:, :slots].reshape(16 * slots, width), slot_mine)
     ada_bias_grad = jnp.sum(slot_mine.astype(f32), axis=0)
     row_count = width // 16
 

time: 763 us -> 702 us (0.920)
  starting transfers between devices: 87 us -> 58.1 us
  local copies, waits for them, and re-layouts: 25.1 us -> 44.6 us
  Pallas kernels: 395 us -> 377 us
  waiting for transfers between devices: 18.7 us -> 1.48 us
  matrix products: 172 us -> 161 us
    pallas_call x4, Pallas kernels: 68.4 us -> 34.4 us  [gather_cores(): pl.pallas_call(gather_kernel, out_shape=jax.ShapeDtypeStruct((2, rows, wi...]
    ppermute x23 -> x18, starting transfers between devices: 87 us -> 58.1 us  [send(): return lax.ppermute(value, ('dp', 'tensor'), pairs_of(move))]
    pallas_call x0 -> x1, Pallas kernels: none -> 22.7 us  [fetch(): pl.pallas_call(fetch_kernel, out_shape=(jax.ShapeDtypeStruct(tokens.shape...]
    pallas_call x1, Pallas kernels: 231 us -> 252 us  [reduce_grads(): pl.pallas_call(functools.partial(reduce_kernel, grid_rows, first_jobs, se...]
    ppermute x23 -> x18, waiting for transfers between devices: 18.7 us -> 1.48 us  [send(): return lax.ppermute(value, ('dp', 'tensor'), pairs_of(move))]
    select_n x0 -> x3, other arithmetic: none -> 16.8 us  [over_y(): jnp.where(home, halves, jnp.where(mine, first[None], second[None]))]
    pallas_call x1, Pallas kernels: 55.6 us -> 41.8 us  [attend_back(): pl.pallas_call(functools.partial(attend_back_kernel, heads, together, fac...]
    dot_general x10 -> x9, matrix products: 94.4 us -> 80.9 us  [dot_nt(): lax.dot_general(left_arg, right_arg, (((1,), (1,)), ((), ())), preferred_...]
  transfers between devices with their start and end apart: 23 -> 18, of which waited for: 3 -> 1; matrix products, arithmetic and copies ran while one was open for 26% -> 28% of each run, Pallas kernels for 51% -> 48%
where the time goes in v3:
time: 702 us; the launch traced here: 694 us
  Pallas kernels  377 us (54%)
  matrix products  161 us (23%)
  starting transfers between devices  58.1 us (8%)
  other arithmetic  49 us (7%)
  local copies, waits for them, and re-layouts  44.6 us (6%)
    pallas_call x1, Pallas kernels, reduce_grads(): pl.pallas_call(functools.partial(reduce_kernel, grid_rows, first_jobs, se...  252 us
    dot_general x9, matrix products, dot_nt(): lax.dot_general(left_arg, right_arg, (((1,), (1,)), ((), ())), preferred_...  80.9 us
    dot_general x9, matrix products, dot_nn(): return jnp.dot(left, right, preferred_element_type=f32)  78.3 us
    ppermute x18, starting transfers between devices, send(): return lax.ppermute(value, ('dp', 'tensor'), pairs_of(move))  58.1 us
    pallas_call x1, Pallas kernels, attend_back(): pl.pallas_call(functools.partial(attend_back_kernel, heads, together, fac...  41.8 us
    pallas_call x4, Pallas kernels, gather_cores(): pl.pallas_call(gather_kernel, out_shape=jax.ShapeDtypeStruct((2, rows, wi...  34.4 us
    pallas_call x1, Pallas kernels, attend(): pl.pallas_call(functools.partial(attend_kernel, heads, 2, factor), out_sh...  26.4 us
    pallas_call x1, Pallas kernels, fetch(): pl.pallas_call(fetch_kernel, out_shape=(jax.ShapeDtypeStruct(tokens.shape...  22.7 us
  transfers between devices with their start and end apart: 18, of which 1 were waited for; matrix products, arithmetic and copies ran while one was open for 28% of the time, Pallas kernels for 48%

profile of v3, /device:TPU:0, one launch (start us, length us, event | category | flops | bytes accessed | tf_op | source)
XLA Modules:
  0.0 694.2 jit_solution(6894531649203264048)
XLA Ops:
  0.7 6.6 copy.73.qkv_ref
  11.4 22.7 %fetch.1 = (bf16[768,1152]{1,0:T(8,128)(2,1)}, bf16[1152,1728]{1,0:T(8,128)(2,1)}, bf16[6,1152]{1,0:T(8,128)(2,1)}, f32[6,6912]{1,0:T(8,128)}) custom-call(bf16[768,1152]{1,0:T(8,128)(2,1)} %tokens_ref.1, bf16[1152,1728]{1,0:T(8,128)(2,1)} %copy.73.qkv_ref, bf16[6,1152]{1,0:T(8,128)(2,1)} %cond_ref.1, bf16[1152,6912]{1,0:T(8,128)(2,1)} %ada_ref.3, ...), custom_call_target="tpu_custom_call" | custom-call | flops 10000000000 | bytes 30000000 | tf_op jit(solution)/shard_map/fetch/pallas_call | solution.py:1644
  36.4 22.6 %collective-permute-start = (s32[1536]{0:T(1024)S(1)}, s32[1536]{0:T(1024)S(1)}, u32[]{:S(2)}, u32[]{:S(2)}) collective-permute-start(s32[1536]{0:T(1024)S(1)} %copy-done.48), channel_id=1, source_target_pairs={{0,2},{1,3},{2,0},{3,1},{4,6},{5,7},{6,4},{7,5},{8,10},{9,11},{10,... | collective-permute-start | bytes 18440 | tf_op jit(solution)/shard_map/ppermute | solution.py:467
  75.4 6.8 gather_cores.4
  85.8 10.3 %add_convert_fusion.qkv_ref = bf16[1536,1792]{1,0:T(8,128)(2,1)S(1)} fusion(f32[1792]{0:T(1024)S(1)} %concatenate.13, bf16[1536,1152]{1,0:T(8,128)(2,1)} %bitcast.161, bf16[1152,1728]{1,0:T(8,128)(2,1)} %get-tuple-element.55), kind=kOutput, calls=%fused_computation.11 | convolution fusion | flops 6347292672 | bytes 13032448 | tf_op jit(solution)/shard_map/dot_general | solution.py:1781
  100.4 26.4 %attend.1 = (bf16[1536,768]{1,0:T(8,128)(2,1)S(1)}, f32[48,1,256]{2,1,0:T(1,128)S(1)}) custom-call(s32[6]{0:T(128)S(1)} %get-tuple-element.54.starts, s32[6]{0:T(128)S(1)} %fusion.77.counts, bf16[1536,1792]{1,0:T(8,128)(2,1)S(1)} %add_convert_fusion.qkv_ref), custom_call_target="tpu_custom_call" | custom-call | flops 20000000000 | bytes 13000000 | tf_op jit(solution)/shard_map/attend/pallas_call | solution.py:607
  129.8 17.4 %collective-permute-start.6 = (bf16[768,1152]{1,0:T(8,128)(2,1)}, bf16[768,1152]{1,0:T(8,128)(2,1)}, u32[]{:S(2)}, u32[]{:S(2)}) collective-permute-start(bf16[768,1152]{1,0:T(8,128)(2,1)} %convolution_convert_fusion.3), channel_id=1, source_target_pairs={{0,2},{1,3},{2,0},{3,1},{4,6},{5,7},{6,4},{7,5},{8,10},{9,11},{10,... | collective-permute-start | bytes 5308424 | tf_op jit(solution)/shard_map/ppermute | solution.py:467
  149.7 7.2 %fusion.11 = bf16[1152,2304]{1,0:T(8,128)(2,1)} fusion(bf16[1152,2304]{1,0:T(8,128)(2,1)} %param.30, pred[1152]{0:T(1024)(128)(4,1)S(1)} %broadcast_in_dim.171, pred[]{:T(512)S(6)} %eq.53, bf16[576,2304]{1,0:T(8,128)(2,1)} %collective-permute-done.7, bf16[576,2304]{1,0:T(8,128)(2,1)} %collective-permute-done.3), kind=kLoop, calls=%fused_computation.25 | loop fusion | flops 5308416 | bytes 15926401 | tf_op jit(solution)/shard_map/jit(_where)/select_n | solution.py:1740
  168.8 15.6 %multiply_convert_fusion = (bf16[1536,2304]{1,0:T(8,128)(2,1)}, f32[1536,2304]{1,0:T(8,128)}) fusion(f32[2304]{0:T(1024)S(1)} %slice.140, bf16[1536,1152]{1,0:T(8,128)(2,1)S(1)} %bitcast.163, bf16[1152,2304]{1,0:T(8,128)(2,1)S(1)} %bitcast.175), kind=kOutput, calls=%fused_computation.9 | convolution fusion | flops 8189116416 | bytes 30090240 | tf_op jit(solution)/shard_map/dot_general | solution.py:1781
  184.5 7.7 %fusion.10 = bf16[2304,1152]{1,0:T(8,128)(2,1)} fusion(bf16[2304,1152]{1,0:T(8,128)(2,1)} %param.32, pred[2304]{0:T(1024)(128)(4,1)S(1)} %broadcast_in_dim.178, pred[]{:T(512)S(6)} %eq.53, bf16[1152,1152]{1,0:T(8,128)(2,1)} %collective-permute-done.8, bf16[1152,1152]{1,0:T(8,128)(2,1)} %copy-done.24), kind=kLoop, calls=%fused_computation.23 | loop fusion | flops 5308416 | bytes 15927553 | tf_op jit(solution)/shard_map/jit(_where)/select_n | solution.py:1740
  192.2 9.6 %fusion.32 = bf16[768,1152]{1,0:T(8,128)(2,1)} fusion(bf16[2304,1152]{1,0:T(8,128)(2,1)} %fusion.10, bf16[1536,2304]{1,0:T(8,128)(2,1)} %get-tuple-element.190.one_right, s32[]{:T(128)S(6)} %select_n.175), kind=kOutput, calls=%fused_computation.69 | convolution fusion | flops 4077748224 | bytes 10616836 | tf_op jit(solution)/shard_map/dot_general | solution.py:1781
  213.9 12.4 %fusion.16 = (bf16[768,1152]{1,0:T(8,128)(2,1)}, f32[768,1152]{1,0:T(8,128)}) fusion(f32[768,1152]{1,0:T(8,128)} %copy-done.8, f32[3,1152]{1,0:T(4,128)S(1)} %get-tuple-element.173, f32[1152]{0:T(1024)S(1)} %convert_element_type.177, bf16[768,1152]{1,0:T(8,128)(2,1)} %collective-permute-done.9, bf16[2304,1152]{1,0:T(8,128)(2,1)} %fusion.10, ...), kind=kOutput, calls=%fused_computation.38 | convolution fusion | flops 4083941376 | bytes 19482628 | tf_op jit(solution)/shard_map/dot_general | solution.py:1781
  226.3 10.5 %multiply_convert_fusion.2 = (bf16[768,2048]{1,0:T(8,128)(2,1)S(1)}, f32[768,2048]{1,0:T(8,128)}) fusion(f32[2048]{0:T(1024)S(1)} %convert_element_type.180, bf16[768,1152]{1,0:T(8,128)(2,1)} %get-tuple-element.192.in_right, bf16[1152,2048]{1,0:T(8,128)(2,1)} %param.34), kind=kOutput, calls=%fused_computation.20 | convolution fusion | flops 3633315840 | bytes 15933440 | tf_op jit(solution)/shard_map/dot_general | solution.py:1781
  236.9 7.4 %multiply_convert_fusion.1 = (bf16[768,2048]{1,0:T(8,128)(2,1)S(1)}, f32[768,2048]{1,0:T(8,128)S(1)}) fusion(f32[2048]{0:T(1024)S(1)} %convert_element_type.182, bf16[768,2048]{1,0:T(8,128)(2,1)S(1)} %get-tuple-element.194.mid_right, bf16[2048,2048]{1,0:T(8,128)(2,1)S(1)} %bitcast.195), kind=kOutput, calls=%fused_computation.18 | convolution fusion | flops 6451888128 | bytes 20979712 | tf_op jit(solution)/shard_map/dot_general | solution.py:1781
  253.7 14.0 %fusion.104 = (f32[2048]{0:T(1024)S(1)}, bf16[768,2048]{1,0:T(8,128)(2,1)S(1)}) fusion(f32[768,2048]{1,0:T(8,128)} %get-tuple-element.195, f32[2048]{0:T(1024)S(1)} %convert_element_type.180, bf16[768,2048]{1,0:T(8,128)(2,1)S(1)} %get-tuple-element.158.mid_left, bf16[2048,2048]{1,0:T(8,128)(2,1)} %param.36), kind=kOutput, calls=%fused_computation.208 | convolution fusion | flops 6461323264 | bytes 20987904 | tf_op jit(solution)/shard_map/dot_general | solution.py:21
  267.7 7.8 %fusion.113 = f32[768,1152]{1,0:T(8,128)S(1)} fusion(bf16[768,2048]{1,0:T(8,128)(2,1)S(1)} %get-tuple-element.160.in_left, bf16[1152,2048]{1,0:T(8,128)(2,1)} %param.34), kind=kOutput, calls=%fused_computation.214 | convolution fusion | flops 3623878656 | bytes 11403264 | tf_op jit(solution)/shard_map/dot_general | solution.py:21
  276.6 20.0 %gather_cores.6 = bf16[2,768,1152]{2,1,0:T(8,128)(2,1)S(1)} custom-call(bf16[768,1152]{1,0:T(8,128)(2,1)S(1)} %fusion.46.own_ref), custom_call_target="tpu_custom_call" | custom-call | bytes 12000000 | tf_op jit(solution)/shard_map/gather_cores/pallas_call | solution.py:531
  296.7 20.8 %fusion.106 = (f32[2304]{0:T(1024)S(1)}, bf16[1536,2304]{1,0:T(8,128)(2,1)}) fusion(f32[1536,2304]{1,0:T(8,128)} %get-tuple-element.191, bf16[1536,1152]{1,0:T(8,128)(2,1)S(1)} %bitcast.165, bf16[2304,1152]{1,0:T(8,128)(2,1)S(1)} %bitcast.179), kind=kOutput, calls=%fused_computation.209 | convolution fusion | flops 8228042752 | bytes 30090240 | tf_op jit(solution)/shard_map/dot_general | solution.py:21
  317.6 6.9 fusion.38
  328.3 8.8 %fusion.54 = (f32[768]{0:T(1024)S(1)}, f32[768]{0:T(1024)S(1)}, f32[768,1152]{1,0:T(8,128)S(1)}) fusion(f32[3,1152]{1,0:T(4,128)S(1)} %copy-done.32, f32[768]{0:T(1024)S(1)} %copy-done.43, f32[768,1152]{1,0:T(8,128)S(1)} %copy-done.9, f32[768]{0:T(1024)S(1)} %copy-done.39, bf16[768,1152]{1,0:T(8,128)(2,1)S(1)} %collective-permute-done.14, ...), kind=kOutput, calls=%fused_computation.89 | convolution fusion | flops 4085709312 | bytes 17720836 | tf_op jit(solution)/shard_map/dot_general | solution.py:21
  346.6 41.8 %attend_back.1 = (bf16[1536,1792]{1,0:T(8,128)(2,1)}, f32[8,576]{1,0:T(8,128)S(1)}) custom-call(s32[6]{0:T(128)S(1)} %get-tuple-element.54.starts, s32[6]{0:T(128)S(1)} %fusion.77.counts, bf16[1536,1792]{1,0:T(8,128)(2,1)} %copy-done.7, f32[48,1,256]{2,1,0:T(1,128)S(1)} %get-tuple-element.74.log_ref, bf16[1536,768]{1,0:T(8,128)(2,1)S(1)} %convolution_convert_fusion.2.grad_ref), custom_call_target="tpu_custom_call" | custom-call | flops 40000000000 | bytes 25000000 | tf_op jit(solution)/shard_map/attend_back/pallas_call | solution.py:694
  388.5 6.9 convolution_convert_fusion
  399.8 7.8 %fusion.53 = (f32[768]{0:T(1024)S(1)}, f32[768]{0:T(1024)S(1)}, f32[768,1152]{1,0:T(8,128)S(1)}) fusion(f32[3,1152]{1,0:T(4,128)S(1)} %copy-done.34, f32[768]{0:T(1024)S(1)} %copy-done.41, f32[768]{0:T(1024)S(1)} %copy-done.37, bf16[768,1152]{1,0:T(8,128)(2,1)S(1)} %copy-done.10, bf16[768,1152]{1,0:T(8,128)(2,1)} %collective-permute-done.15, ...), kind=kOutput, calls=%fused_computation.88 | convolution fusion | flops 3180624384 | bytes 13985284 | tf_op jit(solution)/shard_map/dot_general | solution.py:21
  418.6 251.8 %reduce_grads.1 = (f32[12,72,256]{2,1,0:T(8,128)S(1)}, f32[16,72,256]{2,1,0:T(8,128)}, f32[17,64,256]{2,1,0:T(8,128)}, f32[112,128]{1,0:T(8,128)S(1)}, f32[4,2,2...) custom-call(bf16[1536,1152]{1,0:T(8,128)(2,1)} %bitcast.166, ...), custom_call_target="tpu_custom_call" | custom-call | flops 99999997952 | bytes 100000000 | tf_op jit(solution)/shard_map/reduce_grads/pallas_call | solution.py:1468
  (315 shorter events, 121.6 us)
Async XLA Ops:
  0.7 243.6 %copy-start = (bf16[2048,768]{1,0:T(8,128)(2,1)S(1)}, bf16[2048,768]{1,0:T(8,128)(2,1)}, u32[]{:S(2)}) copy-start(bf16[2048,768]{1,0:T(8,128)(2,1)} %param.38) | copy-start | bytes 9437188
  11.4 47.6 %copy-start.57 = (bf16[2,576]{1,0:T(2,128)(2,1)S(1)}, bf16[2,576]{1,0:T(2,128)(2,1)}, u32[]{:S(2)}) copy-start(bf16[2,576]{1,0:T(2,128)(2,1)} %param.27) | copy-start | bytes 6916
  11.4 47.9 %copy-start.49 = (bf16[2304]{0:T(1024)(128)(2,1)S(1)}, bf16[2304]{0:T(1024)(128)(2,1)}, u32[]{:S(2)}) copy-start(bf16[2304]{0:T(1024)(128)(2,1)} %param.31) | copy-start | bytes 13828
  34.2 50.7 %collective-permute-start.3 = (bf16[576,2304]{1,0:T(8,128)(2,1)}, bf16[576,2304]{1,0:T(8,128)(2,1)}, u32[]{:S(2)}, u32[]{:S(2)}) collective-permute-start(bf16[576,2304]{1,0:T(8,128)(2,1)} %constant_dynamic-slice_fusion.3), channel_id=1, source_target_pairs={{1,2},{2,1},{5,6},{6,5},{9,10},{10,9},{13,14},{14,13},{17,18},{18,... | collective-permute-start | bytes 7962632 | tf_op jit(solution)/shard_map/ppermute | solution.py:467
  36.4 35.0 %collective-permute-start = (s32[1536]{0:T(1024)S(1)}, s32[1536]{0:T(1024)S(1)}, u32[]{:S(2)}, u32[]{:S(2)}) collective-permute-start(s32[1536]{0:T(1024)S(1)} %copy-done.48), channel_id=1, source_target_pairs={{0,2},{1,3},{2,0},{3,1},{4,6},{5,7},{6,4},{7,5},{8,10},{9,11},{10,... | collective-permute-start | bytes 18440 | tf_op jit(solution)/shard_map/ppermute | solution.py:467
  59.6 24.4 %collective-permute-start.1 = (bf16[3456]{0:T(1024)(128)(2,1)S(1)}, bf16[3456]{0:T(1024)(128)(2,1)S(1)}, u32[]{:S(2)}, u32[]{:S(2)}) collective-permute-start(bf16[3456]{0:T(1024)(128)(2,1)S(1)} %dynamic-update-slice.14), channel_id=1, source_target_pairs={{1,2},{2,1},{5,6},{6,5},{9,10},{10,9},{13,14},{14,13},{17,18},{18,... | collective-permute-start | bytes 20744 | tf_op jit(solution)/shard_map/ppermute | solution.py:467
  62.3 21.9 %collective-permute-start.2 = (bf16[288,1152]{1,0:T(8,128)(2,1)}, bf16[288,1152]{1,0:T(8,128)(2,1)}, u32[]{:S(2)}, u32[]{:S(2)}) collective-permute-start(bf16[288,1152]{1,0:T(8,128)(2,1)} %constant_dynamic-slice_fusion.4), channel_id=1, source_target_pairs={{1,2},{2,1},{5,6},{6,5},{9,10},{10,9},{13,14},{14,13},{17,18},{18,... | collective-permute-start | bytes 1990664 | tf_op jit(solution)/shard_map/ppermute | solution.py:467
  72.1 84.9 %copy-start.29 = (f32[3,1152]{1,0:T(4,128)}, f32[3,1152]{1,0:T(4,128)S(1)}, u32[]{:S(2)}) copy-start(f32[3,1152]{1,0:T(4,128)S(1)} %get-tuple-element.178) | copy-start | bytes 41476
  72.1 91.7 %copy-start.31 = (f32[3,1152]{1,0:T(4,128)}, f32[3,1152]{1,0:T(4,128)S(1)}, u32[]{:S(2)}) copy-start(f32[3,1152]{1,0:T(4,128)S(1)} %get-tuple-element.175) | copy-start | bytes 41476
  84.2 11.9 %collective-permute-start.5 = (bf16[288,1152]{1,0:T(8,128)(2,1)}, bf16[288,1152]{1,0:T(8,128)(2,1)S(1)}, u32[]{:S(2)}, u32[]{:S(2)}) collective-permute-start(bf16[288,1152]{1,0:T(8,128)(2,1)} %collective-permute-done.2), channel_id=1, source_target_pairs={{1,5},{2,6},{5,1},{6,2},{9,13},{10,14},{13,9},{14,10},{17,21},{18,... | collective-permute-start | bytes 1990664 | tf_op jit(solution)/shard_map/ppermute | solution.py:467
  84.9 41.9 %collective-permute-start.4 = (bf16[1152,1152]{1,0:T(8,128)(2,1)}, bf16[1152,1152]{1,0:T(8,128)(2,1)S(1)}, u32[]{:S(2)}, u32[]{:S(2)}) collective-permute-start(bf16[1152,1152]{1,0:T(8,128)(2,1)} %constant_dynamic-slice_fusion.2), channel_id=1, source_target_pairs={{1,2},{2,1},{5,6},{6,5},{9,10},{10,9},{13,14},{14,13},{17,18},{18,... | collective-permute-start | bytes 7962632 | tf_op jit(solution)/shard_map/ppermute | solution.py:467
  98.0 49.6 %collective-permute-start.7 = (bf16[576,2304]{1,0:T(8,128)(2,1)}, bf16[576,2304]{1,0:T(8,128)(2,1)}, u32[]{:S(2)}, u32[]{:S(2)}) collective-permute-start(bf16[576,2304]{1,0:T(8,128)(2,1)} %collective-permute-done.3), channel_id=1, source_target_pairs={{1,5},{2,6},{5,1},{6,2},{9,13},{10,14},{13,9},{14,10},{17,21},{18,... | collective-permute-start | bytes 7962632 | tf_op jit(solution)/shard_map/ppermute | solution.py:467
  129.8 27.1 %collective-permute-start.6 = (bf16[768,1152]{1,0:T(8,128)(2,1)}, bf16[768,1152]{1,0:T(8,128)(2,1)}, u32[]{:S(2)}, u32[]{:S(2)}) collective-permute-start(bf16[768,1152]{1,0:T(8,128)(2,1)} %convolution_convert_fusion.3), channel_id=1, source_target_pairs={{0,2},{1,3},{2,0},{3,1},{4,6},{5,7},{6,4},{7,5},{8,10},{9,11},{10,... | collective-permute-start | bytes 5308424 | tf_op jit(solution)/shard_map/ppermute | solution.py:467
  147.2 55.3 %collective-permute-start.13 = (bf16[1536,768]{1,0:T(8,128)(2,1)}, bf16[1536,768]{1,0:T(8,128)(2,1)}, u32[]{:S(2)}, u32[]{:S(2)}) collective-permute-start(bf16[1536,768]{1,0:T(8,128)(2,1)} %param.40), channel_id=1, source_target_pairs={{0,2},{1,3},{2,0},{3,1},{4,6},{5,7},{6,4},{7,5},{8,10},{9,11},{10,... | collective-permute-start | bytes 7077896 | tf_op jit(solution)/shard_map/ppermute | solution.py:467
  147.6 36.9 %collective-permute-start.8 = (bf16[1152,1152]{1,0:T(8,128)(2,1)}, bf16[1152,1152]{1,0:T(8,128)(2,1)}, u32[]{:S(2)}, u32[]{:S(2)}) collective-permute-start(bf16[1152,1152]{1,0:T(8,128)(2,1)} %copy-done.24), channel_id=1, source_target_pairs={{1,5},{2,6},{5,1},{6,2},{9,13},{10,14},{13,9},{14,10},{17,21},{18,... | collective-permute-start | bytes 7962632 | tf_op jit(solution)/shard_map/ppermute | solution.py:467
  201.8 12.1 %collective-permute-start.9 = (bf16[768,1152]{1,0:T(8,128)(2,1)}, bf16[768,1152]{1,0:T(8,128)(2,1)}, u32[]{:S(2)}, u32[]{:S(2)}) collective-permute-start(bf16[768,1152]{1,0:T(8,128)(2,1)} %fusion.32), channel_id=1, source_target_pairs={{0,2},{1,3},{2,0},{3,1},{4,6},{5,7},{6,4},{7,5},{8,10},{9,11},{10,... | collective-permute-start | bytes 5308424 | tf_op jit(solution)/shard_map/ppermute | solution.py:467
  201.8 4.0 collective-permute-start.12
  211.9 63.7 %collective-permute-start.11 = (bf16[768,1152]{1,0:T(8,128)(2,1)}, bf16[768,1152]{1,0:T(8,128)(2,1)}, u32[]{:S(2)}, u32[]{:S(2)}) collective-permute-start(bf16[768,1152]{1,0:T(8,128)(2,1)} %param.43), channel_id=1, source_target_pairs={{1,2},{2,1},{5,6},{6,5},{9,10},{10,9},{13,14},{14,13},{17,18},{18,... | collective-permute-start | bytes 5308424 | tf_op jit(solution)/shard_map/ppermute | solution.py:467
  276.3 60.8 %copy-start.11 = (f32[768,1152]{1,0:T(8,128)}, f32[768,1152]{1,0:T(8,128)S(1)}, u32[]{:S(2)}) copy-start(f32[768,1152]{1,0:T(8,128)S(1)} %get-tuple-element.162) | copy-start | bytes 10616836
  324.5 3.8 collective-permute-start.14
  325.0 71.7 %collective-permute-start.10 = (bf16[768,1152]{1,0:T(8,128)(2,1)}, bf16[768,1152]{1,0:T(8,128)(2,1)}, u32[]{:S(2)}, u32[]{:S(2)}) collective-permute-start(bf16[768,1152]{1,0:T(8,128)(2,1)} %get-tuple-element.192.in_right), channel_id=1, source_target_pairs={{1,2},{2,1},{5,6},{6,5},{9,10},{10,9},{13,14},{14,13},{17,18},{18,... | collective-permute-start | bytes 5308424 | tf_op jit(solution)/shard_map/ppermute | solution.py:467
  395.4 4.4 collective-permute-start.15
  413.3 4.7 collective-permute-start.17
  416.1 273.8 %collective-permute-start.16 = (bf16[768,1152]{1,0:T(8,128)(2,1)}, bf16[768,1152]{1,0:T(8,128)(2,1)}, u32[]{:S(2)}, u32[]{:S(2)}) collective-permute-start(bf16[768,1152]{1,0:T(8,128)(2,1)} %add_convert_fusion.1), channel_id=1, source_target_pairs={{1,2},{2,1},{5,6},{6,5},{9,10},{10,9},{13,14},{14,13},{17,18},{18,... | collective-permute-start | bytes 5308424 | tf_op jit(solution)/shard_map/ppermute | solution.py:467
  (65 other events, 733.1 us)

commit v4 on v3

--- a/solution.py
+++ b/solution.py
@@ -448,7 +448,11 @@
 LANES = 128
 MESH = pl.DeviceIdType.MESH
 TILE = 256
+GAP = 2
+SLOTS = 2 * GAP
 LOG2_E = 1.4426950408889634
+GELU_SCALE = 0.7978845608028654
+GELU_CUBE = 0.044715
 bf16 = jnp.bfloat16
 f32 = jnp.float32
 
@@ -605,7 +609,7 @@
     rows = qkv.shape[0]
     factor = HEAD_DIM ** (-0.5) * LOG2_E
     return pl.pallas_call(
-        functools.partial(attend_kernel, heads, 2, factor),
+        functools.partial(attend_kernel, heads, 4, factor),
         out_shape=(
             jax.ShapeDtypeStruct((rows, out_cols), bf16),
             jax.ShapeDtypeStruct((heads * (rows // SHORT), 1, SHORT), f32),
@@ -690,7 +694,7 @@
 def attend_back(starts, counts, qkv, log_sums, grad_heads, heads):
     rows, columns = qkv.shape
     factor = HEAD_DIM ** (-0.5)
-    together = 2
+    together = 4
     return pl.pallas_call(
         functools.partial(attend_back_kernel, heads, together, factor),
         out_shape=(
@@ -716,7 +720,6 @@
     grid_rows,
     first_jobs,
     second_jobs,
-    proj_jobs,
     one_left,
     one_right,
     two_left,
@@ -725,12 +728,6 @@
     three_right,
     four_left,
     four_right,
-    mid_left,
-    mid_right,
-    in_left,
-    in_right,
-    last_left,
-    last_right,
     bias_ref,
     slot_ref,
     silu_ref,
@@ -738,7 +735,6 @@
     ada_ref,
     first_out,
     second_out,
-    proj_out,
     bias_out,
     slot_out,
     silu_out,
@@ -748,17 +744,6 @@
     second_left,
     first_right,
     second_right,
-    proj_stage,
-    proj_left,
-    proj_right,
-    p0,
-    p0_got,
-    p1,
-    p1_got,
-    p2,
-    p2_got,
-    p3,
-    p3_got,
     f0,
     f0_turn,
     f0_swap,
@@ -789,11 +774,6 @@
     load_sem,
     first_load,
     second_load,
-    proj_load,
-    p0_sems,
-    p1_sems,
-    p2_sems,
-    p3_sems,
     f0_sems,
     f1_sems,
     f2_sems,
@@ -904,7 +884,9 @@
             for at_y in range(2):
                 for at_core in range(2):
                     low = (at_y * 2 + at_core) * grid_rows
-                    keep(at_z, at_y, at_core, product[low : low + grid_rows, :].astype(bf16))
+                    part = product[low : low + grid_rows, :]
+                    stacked = jnp.concatenate([part[:, :LANES], part[:, LANES:]], axis=0)
+                    keep(at_z, at_y, at_core, stacked.astype(bf16))
             return carry
 
         lax.fori_loop(0, 4, block, 0)
@@ -960,34 +942,34 @@
                 load_left(two_left, stage, first_left)
 
             def keep(at_z, at_y, at_core, value):
-                f0[slot, at_core, at_y, at_z] = value
+                f0[lax.rem(tick, SLOTS), at_core, at_y, at_z] = value
 
             multiply(first_left, first_right, slot, keep)
 
-        last = tick - 3
+        last = tick - 3 * GAP
 
         @pl.when(inside(last, first_jobs))
         def _():
-            slot = lax.rem(last, 2)
+            slot = lax.rem(last, SLOTS)
             for ahead in (1, 2, 3):
                 f2_copy(slot, ahead).wait()
             first_out[last] = added(f2[slot, z], f2_got[slot, 0], f2_got[slot, 1], f2_got[slot, 2])
 
-        third = tick - 2
+        third = tick - 2 * GAP
 
         @pl.when(inside(third, first_jobs))
         def _():
-            slot = lax.rem(third, 2)
+            slot = lax.rem(third, SLOTS)
             f1_copy(slot).wait()
             f2[slot] = added(f1[slot, y], f1_got[slot]).astype(bf16)
             for ahead in (1, 2, 3):
                 f2_copy(slot, ahead).start()
 
-        second = tick - 1
+        second = tick - GAP
 
         @pl.when(inside(second, first_jobs))
         def _():
-            slot = lax.rem(second, 2)
+            slot = lax.rem(second, SLOTS)
             turn, swap = f0_copies(slot)
             turn.wait()
 
@@ -1000,7 +982,7 @@
                 swap.wait()
                 f1[slot] = added(f0_turn[slot], f0_swap[slot]).astype(bf16)
 
-            @pl.when(second + 2 < first_jobs)
+            @pl.when(second + SLOTS < first_jobs)
             def _():
                 pl.semaphore_signal(first_free, inc=1, device_id=turn_from, device_id_type=MESH)
 
@@ -1008,10 +990,10 @@
 
         @pl.when(tick < first_jobs)
         def _():
-            slot = lax.rem(tick, 2)
+            slot = lax.rem(tick, SLOTS)
             turn, swap = f0_copies(slot)
 
-            @pl.when(tick >= 2)
+            @pl.when(tick >= SLOTS)
             def _():
                 pl.semaphore_wait(first_free, 1)
 
@@ -1040,15 +1022,15 @@
                 load_left(four_left, stage, second_left)
 
             def keep(at_z, at_y, at_core, value):
-                s0[slot, at_y, at_z, at_core] = value
+                s0[lax.rem(tick, SLOTS), at_y, at_z, at_core] = value
 
             multiply(second_left, second_right, slot, keep)
 
-        last = tick - 3
+        last = tick - 3 * GAP
 
         @pl.when(inside(last, second_jobs))
         def _():
-            slot = lax.rem(last, 2)
+            slot = lax.rem(last, SLOTS)
             turn, swap = s2_copies(slot)
             turn.wait()
 
@@ -1061,21 +1043,21 @@
                 swap.wait()
                 second_out[last] = added(s2_turn[slot], s2_swap[slot])
 
-            @pl.when(last + 2 < second_jobs)
+            @pl.when(last + SLOTS < second_jobs)
             def _():
                 pl.semaphore_signal(second_free, inc=1, device_id=turn_from, device_id_type=MESH)
 
-        third = tick - 2
+        third = tick - 2 * GAP
 
         @pl.when(inside(third, second_jobs))
         def _():
-            slot = lax.rem(third, 2)
+            slot = lax.rem(third, SLOTS)
             for ahead in (1, 2, 3):
                 s1_copy(slot, ahead).wait()
             s2[slot] = added(s1[slot, z], s1_got[slot, 0], s1_got[slot, 1], s1_got[slot, 2]).astype(bf16)
             turn, swap = s2_copies(slot)
 
-            @pl.when(third >= 2)
+            @pl.when(third >= SLOTS)
             def _():
                 pl.semaphore_wait(second_free, 1)
 
@@ -1085,11 +1067,11 @@
             def _():
                 swap.start()
 
-        second = tick - 1
+        second = tick - GAP
 
         @pl.when(inside(second, second_jobs))
         def _():
-            slot = lax.rem(second, 2)
+            slot = lax.rem(second, SLOTS)
             s0_copy(slot).wait()
             s1[slot] = added(s0[slot, y], s0_got[slot]).astype(bf16)
             for ahead in (1, 2, 3):
@@ -1097,148 +1079,7 @@
 
         @pl.when(tick < second_jobs)
         def _():
-            s0_copy(lax.rem(tick, 2)).start()
-
-    mid_jobs = mid_right.shape[1] // TILE
-    in_jobs = -(-in_right.shape[1] // TILE)
-    in_left_over = in_right.shape[1] % TILE
-    proj_rows = mid_left.shape[1] // 32
-    last_rows = last_left.shape[1] // 32
-
-    def proj_right_do(job, slot, action):
-        def copy(source, tile, columns):
-            start = pl.multiple_of(tile * columns, LANES)
-            return pltpu.make_async_copy(
-                source.at[:, pl.ds(start, columns)], proj_right.at[slot, :, pl.ds(0, columns)], proj_load.at[slot]
-            )
-
-        @pl.when(job < mid_jobs)
-        def _():
-            action(copy(mid_right, job, TILE))
-
-        full = in_jobs - (1 if in_left_over else 0)
-
-        @pl.when(inside(job - mid_jobs, full))
-        def _():
-            action(copy(in_right, job - mid_jobs, TILE))
-
-        if in_left_over:
-
-            @pl.when(job == mid_jobs + full)
-            def _():
-                rest = pltpu.make_async_copy(
-                    in_right.at[:, pl.ds(full * TILE, in_left_over)],
-                    proj_right.at[slot, :, pl.ds(0, in_left_over)],
-                    proj_load.at[slot],
-                )
-                action(rest)
-
-        @pl.when(job >= mid_jobs + in_jobs)
-        def _():
-            action(copy(last_right, job - mid_jobs - in_jobs, 2 * TILE))
-
-    def p0_copy(slot):
-        return remote(p0.at[slot, 1 - core], p0_got.at[slot], p0_sems, (slot,), device(z, y, 1 - core, x))
-
-    def p1_copy(slot):
-        return remote(p1.at[slot, 1 - x], p1_got.at[slot], p1_sems, (slot,), device(z, y, core, 1 - x))
-
-    def p2_copy(slot):
-        return remote(p2.at[slot, 1 - y], p2_got.at[slot], p2_sems, (slot,), y_peer)
-
-    def p3_copy(slot, ahead):
-        return remote(
-            p3.at[slot, lax.rem(z + ahead, 4)], p3_got.at[slot, ahead - 1], p3_sems, (slot, ahead - 1), z_peer(ahead)
-        )
-
-    pltpu.make_async_copy(mid_right.at[:, pl.ds(0, TILE)], proj_right.at[0, :, pl.ds(0, TILE)], proj_load.at[0]).start()
-
-    def proj_tick(tick):
-        @pl.when(tick < proj_jobs)
-        def _():
-            slot = lax.rem(tick, 2)
-            proj_right_do(tick, slot, finish)
-
-            @pl.when(tick + 1 < proj_jobs)
-            def _():
-                proj_right_do(tick + 1, 1 - slot, begin)
-
-            for at, source in ((0, mid_left), (mid_jobs, in_left), (mid_jobs + in_jobs, last_left)):
-
-                @pl.when(tick == at)
-                def _(source=source):
-                    load_left(source, proj_stage, proj_left)
-
-            shares = [(at_y, at_core, at_x) for at_y in range(2) for at_core in range(2) for at_x in range(2)]
-
-            @pl.when(tick < mid_jobs + in_jobs)
-            def _():
-                def block(at_z, carry):
-                    span = pl.ds(pl.multiple_of(at_z * 8 * proj_rows, 32), 8 * proj_rows)
-                    right = proj_right[slot, :, 0:TILE]
-                    product = jnp.dot(proj_left[span, :], right, preferred_element_type=f32).astype(bf16)
-                    for low, (at_y, at_core, at_x) in enumerate(shares):
-                        p0[slot, at_core, at_x, at_y, at_z] = product[low * proj_rows : (low + 1) * proj_rows, :]
-                    return carry
-
-                lax.fori_loop(0, 4, block, 0)
-
-            @pl.when(tick >= mid_jobs + in_jobs)
-            def _():
-                def block(at_z, carry):
-                    span = pl.ds(pl.multiple_of(at_z * 8 * last_rows, 32), 8 * last_rows)
-                    for half in range(2):
-                        right = proj_right[slot, :, half * TILE : (half + 1) * TILE]
-                        product = jnp.dot(proj_left[span, :], right, preferred_element_type=f32)
-                        begin_row = half * proj_rows // 2
-                        for low, (at_y, at_core, at_x) in enumerate(shares):
-                            p0[slot, at_core, at_x, at_y, at_z, begin_row : begin_row + last_rows, :] = product[
-                                low * last_rows : (low + 1) * last_rows, :
-                            ].astype(bf16)
-                    return carry
-
-                lax.fori_loop(0, 4, block, 0)
-
-        fifth = tick - 4
-
-        @pl.when(inside(fifth, proj_jobs))
-        def _():
-            slot = lax.rem(fifth, 2)
-            for ahead in (1, 2, 3):
-                p3_copy(slot, ahead).wait()
-            proj_out[fifth] = added(p3[slot, z], p3_got[slot, 0], p3_got[slot, 1], p3_got[slot, 2])
-
-        fourth = tick - 3
-
-        @pl.when(inside(fourth, proj_jobs))
-        def _():
-            slot = lax.rem(fourth, 2)
-            p2_copy(slot).wait()
-            p3[slot] = added(p2[slot, y], p2_got[slot]).astype(bf16)
-            for ahead in (1, 2, 3):
-                p3_copy(slot, ahead).start()
-
-        third = tick - 2
-
-        @pl.when(inside(third, proj_jobs))
-        def _():
-            slot = lax.rem(third, 2)
-            p1_copy(slot).wait()
-            p2[slot] = added(p1[slot, x], p1_got[slot]).astype(bf16)
-            p2_copy(slot).start()
-
-        second = tick - 1
-
-        @pl.when(inside(second, proj_jobs))
-        def _():
-            slot = lax.rem(second, 2)
-            p0_copy(slot).wait()
-            p1[slot] = added(p0[slot, core], p0_got[slot]).astype(bf16)
-            p1_copy(slot).start()
-
-        @pl.when(tick < proj_jobs)
-        def _():
-            p0_copy(lax.rem(tick, 2)).start()
+            s0_copy(lax.rem(tick, SLOTS)).start()
 
     bias_peers = [
         device(z, y, 1 - core, x),
@@ -1369,28 +1210,24 @@
     def tick_body(tick, carry):
         small_tick(tick)
         cond_tick(tick)
-        second_tick(tick)
-        proj_tick(tick)
-
-        @pl.when(lax.rem(tick, 4) != 3)
-        def _():
-            first_tick(tick // 4 * 3 + lax.rem(tick, 4))
+        first_tick(tick)
+
+        @pl.when(lax.rem(tick, 3) != 2)
+        def _():
+            second_tick(tick // 3 * 2 + lax.rem(tick, 3))
 
         return carry
 
-    ticks = max(second_jobs + 3, proj_jobs + 4, ada_tiles + 6, -(-4 * (first_jobs + 3) // 3))
+    ticks = max(first_jobs + 3 * GAP, ada_tiles + 6, -(-3 * (second_jobs + 3 * GAP) // 2))
     lax.fori_loop(0, ticks, tick_body, 0)
 
 
-def reduce_grads(one, two, three, four, mid, first, last, bias, slots, silu, slot_low, ada_weight):
+def reduce_grads(one, two, three, four, bias, slots, silu, slot_low, ada_weight):
     tokens, width = one[0].shape
     grid_rows = width // 16
     first_jobs = (one[1].shape[1] + two[1].shape[1]) // TILE
     second_jobs = (three[1].shape[1] + four[1].shape[1]) // TILE
-    proj_jobs = mid[1].shape[1] // TILE + -(-first[1].shape[1] // TILE) + last[1].shape[1] // (2 * TILE)
-    proj_tokens, proj_hidden = mid[0].shape
-    proj_tile = (proj_hidden // 32, TILE)
-    tile = (grid_rows, TILE)
+    tile = (grid_rows * TILE // LANES, LANES)
     dma = pltpu.SemaphoreType.DMA
     slot_tail = slots.shape[-2:]
 
@@ -1403,31 +1240,20 @@
         pltpu.VMEM((width, tokens), bf16),
         pltpu.VMEM((2, tokens, TILE), bf16),
         pltpu.VMEM((2, tokens, TILE), bf16),
-        pltpu.VMEM((proj_tokens, proj_hidden), bf16),
-        pltpu.VMEM((proj_hidden, proj_tokens), bf16),
-        pltpu.VMEM((2, proj_tokens, 2 * TILE), bf16),
-        pltpu.VMEM((2, 2, 2, 2, 4) + proj_tile, bf16),
-        pltpu.VMEM((2, 2, 2, 4) + proj_tile, bf16),
-        pltpu.VMEM((2, 2, 2, 4) + proj_tile, bf16),
-        pltpu.VMEM((2, 2, 4) + proj_tile, bf16),
-        pltpu.VMEM((2, 2, 4) + proj_tile, bf16),
-        pltpu.VMEM((2, 4) + proj_tile, bf16),
-        pltpu.VMEM((2, 4) + proj_tile, bf16),
-        pltpu.VMEM((2, 3) + proj_tile, bf16),
-        low(2, 2, 2, 4),
-        low(2, 2, 4),
-        low(2, 2, 4),
-        low(2, 2, 4),
-        low(2, 4),
-        low(2, 4),
-        low(2, 3),
-        low(2, 2, 4, 2),
-        low(2, 4, 2),
-        low(2, 4, 2),
-        low(2, 3, 2),
-        low(2, 2),
-        low(2),
-        low(2),
+        low(SLOTS, 2, 2, 4),
+        low(SLOTS, 2, 4),
+        low(SLOTS, 2, 4),
+        low(SLOTS, 2, 4),
+        low(SLOTS, 4),
+        low(SLOTS, 4),
+        low(SLOTS, 3),
+        low(SLOTS, 2, 4, 2),
+        low(SLOTS, 4, 2),
+        low(SLOTS, 4, 2),
+        low(SLOTS, 3, 2),
+        low(SLOTS, 2),
+        low(SLOTS),
+        low(SLOTS),
         pltpu.VMEM((5,) + bias.shape, f32),
         pltpu.VMEM((2, 4) + slot_tail, f32),
         pltpu.VMEM((2, 2, 4) + slot_tail, f32),
@@ -1444,17 +1270,12 @@
         dma,
         dma((2,)),
         dma((2,)),
-        dma((2,)),
-        dma((2, 2)),
-        dma((2, 2)),
-        dma((2, 2)),
-        dma((2, 2, 3)),
-        dma((2, 2, 2)),
-        dma((2, 2)),
-        dma((2, 2, 3)),
-        dma((2, 2)),
-        dma((2, 2, 3)),
-        dma((2, 2, 2)),
+        dma((2, 2, SLOTS)),
+        dma((2, SLOTS)),
+        dma((2, SLOTS, 3)),
+        dma((2, SLOTS)),
+        dma((2, SLOTS, 3)),
+        dma((2, 2, SLOTS)),
         dma((2, 5)),
         dma((2, 2)),
         dma((2, 3)),
@@ -1466,40 +1287,455 @@
         pltpu.SemaphoreType.REGULAR,
     ]
     return pl.pallas_call(
-        functools.partial(reduce_kernel, grid_rows, first_jobs, second_jobs, proj_jobs),
+        functools.partial(reduce_kernel, grid_rows, first_jobs, second_jobs),
         out_shape=(
             jax.ShapeDtypeStruct((first_jobs,) + tile, f32),
             jax.ShapeDtypeStruct((second_jobs,) + tile, f32),
-            jax.ShapeDtypeStruct((proj_jobs,) + proj_tile, f32),
             jax.ShapeDtypeStruct(bias.shape, f32),
             jax.ShapeDtypeStruct((4, 2, 2) + slot_tail, f32),
             jax.ShapeDtypeStruct((4, 2, 2) + silu.shape, bf16),
             jax.ShapeDtypeStruct((8, ada_weight.shape[0]), f32),
         ),
-        in_specs=[whole_spec(pl.ANY)] * 14 + [whole_spec()] * 4 + [whole_spec(pl.ANY)],
-        out_specs=(whole_spec(),) * 7,
+        in_specs=[whole_spec(pl.ANY)] * 8 + [whole_spec()] * 4 + [whole_spec(pl.ANY)],
+        out_specs=(whole_spec(),) * 6,
         scratch_shapes=scratch,
         compiler_params=pltpu.CompilerParams(
             collective_id=1, has_side_effects=True, vmem_limit_bytes=52 << 20
         ),
         cost_estimate=pl.CostEstimate(flops=10**11, bytes_accessed=10**8, transcendentals=0),
         name="reduce_grads",
-    )(*one, *two, *three, *four, *mid, *first, *last, bias, slots, silu, slot_low, ada_weight)
+    )(*one, *two, *three, *four, bias, slots, silu, slot_low, ada_weight)
+
+
+def mlp_back_kernel(
+    proj_jobs,
+    own_ref,
+    pre_ref,
+    down_ref,
+    up_ref,
+    mid_left,
+    mid_right,
+    in_left,
+    in_right,
+    last_left,
+    last_right,
+    all_out,
+    low_out,
+    in_out,
+    bias_out,
+    proj_out,
+    pre_tile,
+    low_tile,
+    part_send,
+    part_got,
+    proj_stage,
+    proj_left,
+    proj_right,
+    p0,
+    p0_got,
+    p1,
+    p1_got,
+    p2,
+    p2_got,
+    p3,
+    p3_got,
+    pre_sems,
+    low_sems,
+    own_sems,
+    part_sems,
+    load_sem,
+    proj_load,
+    p0_sems,
+    p1_sems,
+    p2_sems,
+    p3_sems,
+):
+    dp = lax.axis_index("dp")
+    x = lax.axis_index("tensor")
+    core = dp % 2
+    y = (dp // 2) % 2
+    z = dp // 4
+
+    def device(z_at, y_at, core_at, x_at):
+        return ((z_at * 2 + y_at) * 2 + core_at, x_at)
+
+    y_peer = device(z, 1 - y, core, x)
+
+    def z_peer(ahead):
+        return device(lax.rem(z + ahead, 4), y, core, x)
+
+    barrier = pltpu.get_barrier_semaphore()
+    near = [device(z, y, 1 - core, x), device(z, y, core, 1 - x), device(z, y, 1 - core, 1 - x), y_peer]
+    for peer in near + [z_peer(1), z_peer(2), z_peer(3)]:
+        pl.semaphore_signal(barrier, inc=1, device_id=peer, device_id_type=MESH)
+    pl.semaphore_wait(barrier, 7)
+
+    def remote(source, target, sems, index, peer):
+        return pltpu.make_async_remote_copy(
+            src_ref=source,
+            dst_ref=target,
+            send_sem=sems.at[(0,) + index],
+            recv_sem=sems.at[(1,) + index],
+            device_id=peer,
+            device_id_type=MESH,
+        )
+
+    def added(*terms):
+        total = terms[0].astype(f32)
+        for term in terms[1:]:
+            total = total + term.astype(f32)
+        return total
+
+    def load_left(source, through, target):
+        height = source.shape[1]
+        through = through if height == through.shape[1] else through.at[:, 0:height]
+        copy = pltpu.make_async_copy(source, through, load_sem)
+        copy.start()
+        copy.wait()
+
+        def block(index, carry):
+            rows = pl.ds(pl.multiple_of(index * LANES, LANES), LANES)
+            target[0:height, rows] = through[rows, :].T
+            return carry
+
+        lax.fori_loop(0, source.shape[0] // LANES, block, 0)
+
+    def begin(copy):
+        copy.start()
+
+    def finish(copy):
+        copy.wait()
+
+    def inside(job, count):
+        return jnp.logical_and(job >= 0, job < count)
+
+    core_peer = device(z, y, 1 - core, x)
+    own_rows = own_ref.shape[0]
+    tile_rows = pre_tile.shape[1]
+    hidden = pre_ref.shape[1]
+    half_tiles = own_rows // tile_rows
+
+    def own_span(side):
+        return pl.ds(pl.multiple_of(side * own_rows, 256), own_rows)
+
+    own_copy = remote(own_ref, all_out.at[own_span(core), :], own_sems, (), core_peer)
+    own_copy.start()
+    all_out[own_span(core), :] = own_ref[...]
+    bias_out[...] = jnp.zeros_like(bias_out)
+
+    def tile_span(tile):
+        side = jnp.where(tile < half_tiles, 1 - core, core)
+        begin_row = side * own_rows + lax.rem(tile, half_tiles) * tile_rows
+        return pl.ds(pl.multiple_of(begin_row, 256), tile_rows)
+
+    def part_span(tile):
+        return pl.ds(pl.multiple_of(lax.rem(tile, half_tiles) * tile_rows, 256), tile_rows)
+
+    def pre_copy(tile, slot):
+        return pltpu.make_async_copy(pre_ref.at[tile_span(tile), :], pre_tile.at[slot], pre_sems.at[slot])
+
+    def low_copy(tile, slot):
+        return pltpu.make_async_copy(low_tile.at[slot], low_out.at[tile_span(tile), :], low_sems.at[slot])
+
+    def part_copy(tile):
+        rows = part_span(tile)
+        return remote(part_send.at[rows, :], part_got.at[rows, :], part_sems, (tile,), core_peer)
+
+    pre_copy(0, 0).start()
+    chunk = 768
+
+    def mlp_tile(tile):
+        slot = lax.rem(tile, 2)
+        pre_copy(tile, slot).wait()
+
+        @pl.when(tile + 1 < 2 * half_tiles)
+        def _():
+            pre_copy(tile + 1, 1 - slot).start()
+
+        @pl.when(tile == 0)
+        def _():
+            own_copy.wait()
+
+        @pl.when(tile >= 2)
+        def _():
+            low_copy(tile - 2, slot).wait()
+
+        grads = all_out[tile_span(tile), :]
+        for at in range(0, hidden, chunk):
+            span = slice(at, at + chunk)
+            value = pre_tile[slot, :, span]
+            square = value * value
+            curve = jnp.tanh(GELU_SCALE * (value + GELU_CUBE * (square * value)))
+            slope = 0.5 * (1.0 + curve) + (0.5 * GELU_SCALE) * value * (1.0 - curve * curve) * (
+                1.0 + (3.0 * GELU_CUBE) * square
+            )
+            grad = slope * dot_nt(grads, down_ref[span, :])
+            bias_out[0:1, span] += jnp.sum(grad, axis=0, keepdims=True)
+            low_tile[slot, :, span] = grad.astype(bf16)
+        low_copy(tile, slot).start()
+        part = dot_nt(low_tile[slot], up_ref[...])
+
+        @pl.when(tile < half_tiles)
+        def _():
+            part_send[part_span(tile), :] = part.astype(bf16)
+            part_copy(tile).start()
+
+        @pl.when(tile >= half_tiles)
+        def _():
+            in_out[part_span(tile), :] = part
+
+    mid_jobs = mid_right.shape[1] // TILE
+    in_jobs = -(-in_right.shape[1] // TILE)
+    in_left_over = in_right.shape[1] % TILE
+    proj_rows = mid_left.shape[1] // 32
+    last_rows = last_left.shape[1] // 32
+
+    def proj_right_do(job, slot, action):
+        def copy(source, tile, columns):
+            start = pl.multiple_of(tile * columns, LANES)
+            return pltpu.make_async_copy(
+                source.at[:, pl.ds(start, columns)], proj_right.at[slot, :, pl.ds(0, columns)], proj_load.at[slot]
+            )
+
+        @pl.when(job < mid_jobs)
+        def _():
+            action(copy(mid_right, job, TILE))
+
+        full = in_jobs - (1 if in_left_over else 0)
+
+        @pl.when(inside(job - mid_jobs, full))
+        def _():
+            action(copy(in_right, job - mid_jobs, TILE))
+
+        if in_left_over:
+
+            @pl.when(job == mid_jobs + full)
+            def _():
+                rest = pltpu.make_async_copy(
+                    in_right.at[:, pl.ds(full * TILE, in_left_over)],
+                    proj_right.at[slot, :, pl.ds(0, in_left_over)],
+                    proj_load.at[slot],
+                )
+                action(rest)
+
+        @pl.when(job >= mid_jobs + in_jobs)
+        def _():
+            action(copy(last_right, job - mid_jobs - in_jobs, 2 * TILE))
+
+    def p0_copy(slot):
+        return remote(p0.at[slot, 1 - core], p0_got.at[slot], p0_sems, (slot,), device(z, y, 1 - core, x))
+
+    def route(job):
+        odd = lax.rem(job, 2)
+        first = x + odd * (y - x)
+        second = y + odd * (x - y)
+        over_x = device(z, y, core, 1 - x)
+        over_y = device(z, 1 - y, core, x)
+        toward = tuple(a + odd * (b - a) for a, b in zip(over_x, over_y))
+        onward = tuple(b + odd * (a - b) for a, b in zip(over_x, over_y))
+        return odd, first, second, toward, onward
+
+    def p1_copy(job):
+        odd, first, second, toward, onward = route(job)
+        slot = lax.rem(job, SLOTS)
+        return remote(p1.at[slot, 1 - first], p1_got.at[slot], p1_sems, (slot,), toward)
+
+    def p2_copy(job):
+        odd, first, second, toward, onward = route(job)
+        slot = lax.rem(job, SLOTS)
+        return remote(p2.at[slot, 1 - second], p2_got.at[slot], p2_sems, (slot,), onward)
+
+    def p3_copy(slot, ahead):
+        return remote(
+            p3.at[slot, lax.rem(z + ahead, 4)], p3_got.at[slot, ahead - 1], p3_sems, (slot, ahead - 1), z_peer(ahead)
+        )
+
+    pltpu.make_async_copy(mid_right.at[:, pl.ds(0, TILE)], proj_right.at[0, :, pl.ds(0, TILE)], proj_load.at[0]).start()
+
+    def proj_tick(tick):
+        @pl.when(tick < proj_jobs)
+        def _():
+            slot = lax.rem(tick, 2)
+            odd = slot
+            proj_right_do(tick, slot, finish)
+
+            @pl.when(tick + 1 < proj_jobs)
+            def _():
+                proj_right_do(tick + 1, 1 - slot, begin)
+
+            for at, source in ((0, mid_left), (mid_jobs, in_left), (mid_jobs + in_jobs, last_left)):
+
+                @pl.when(tick == at)
+                def _(source=source):
+                    load_left(source, proj_stage, proj_left)
+
+            shares = [(at_y, at_core, at_x) for at_y in range(2) for at_core in range(2) for at_x in range(2)]
+
+            @pl.when(tick < mid_jobs + in_jobs)
+            def _():
+                def block(at_z, carry):
+                    span = pl.ds(pl.multiple_of(at_z * 8 * proj_rows, 32), 8 * proj_rows)
+                    right = proj_right[slot, :, 0:TILE]
+                    product = jnp.dot(proj_left[span, :], right, preferred_element_type=f32).astype(bf16)
+                    for low, (at_y, at_core, at_x) in enumerate(shares):
+                        p0[lax.rem(tick, SLOTS), at_core, at_x + odd * (at_y - at_x), at_y + odd * (at_x - at_y), at_z] = product[low * proj_rows : (low + 1) * proj_rows, :]
+                    return carry
+
+                lax.fori_loop(0, 4, block, 0)
+
+            @pl.when(tick >= mid_jobs + in_jobs)
+            def _():
+                def block(at_z, carry):
+                    span = pl.ds(pl.multiple_of(at_z * 8 * last_rows, 32), 8 * last_rows)
+                    for half in range(2):
+                        right = proj_right[slot, :, half * TILE : (half + 1) * TILE]
+                        product = jnp.dot(proj_left[span, :], right, preferred_element_type=f32)
+                        begin_row = half * proj_rows // 2
+                        for low, (at_y, at_core, at_x) in enumerate(shares):
+                            p0[lax.rem(tick, SLOTS), at_core, at_x + odd * (at_y - at_x), at_y + odd * (at_x - at_y), at_z, begin_row : begin_row + last_rows, :] = product[
+                                low * last_rows : (low + 1) * last_rows, :
+                            ].astype(bf16)
+                    return carry
+
+                lax.fori_loop(0, 4, block, 0)
+
+        fifth = tick - 4 * GAP
+
+        @pl.when(inside(fifth, proj_jobs))
+        def _():
+            slot = lax.rem(fifth, SLOTS)
+            for ahead in (1, 2, 3):
+                p3_copy(slot, ahead).wait()
+            proj_out[fifth] = added(p3[slot, z], p3_got[slot, 0], p3_got[slot, 1], p3_got[slot, 2])
+
+        fourth = tick - 3 * GAP
+
+        @pl.when(inside(fourth, proj_jobs))
+        def _():
+            slot = lax.rem(fourth, SLOTS)
+            odd, first, second, toward, onward = route(fourth)
+            p2_copy(fourth).wait()
+            p3[slot] = added(p2[slot, second], p2_got[slot]).astype(bf16)
+            for ahead in (1, 2, 3):
+                p3_copy(slot, ahead).start()
+
+        third = tick - 2 * GAP
+
+        @pl.when(inside(third, proj_jobs))
+        def _():
+            slot = lax.rem(third, SLOTS)
+            odd, first, second, toward, onward = route(third)
+            p1_copy(third).wait()
+            p2[slot] = added(p1[slot, first], p1_got[slot]).astype(bf16)
+            p2_copy(third).start()
+
+        second_job = tick - GAP
+
+        @pl.when(inside(second_job, proj_jobs))
+        def _():
+            slot = lax.rem(second_job, SLOTS)
+            p0_copy(slot).wait()
+            p1[slot] = added(p0[slot, core], p0_got[slot]).astype(bf16)
+            p1_copy(second_job).start()
+
+        @pl.when(tick < proj_jobs)
+        def _():
+            p0_copy(lax.rem(tick, SLOTS)).start()
+
+    def tick_body(tick, carry):
+        proj_tick(tick)
+
+        @pl.when(jnp.logical_and(lax.rem(tick, 4) == 3, tick // 4 < 2 * half_tiles))
+        def _():
+            mlp_tile(tick // 4)
+
+        return carry
+
+    lax.fori_loop(0, max(proj_jobs + 4 * GAP, 8 * half_tiles), tick_body, 0)
+    for tile in range(2 * half_tiles - 2, 2 * half_tiles):
+        low_copy(tile, tile % 2).wait()
+    for tile in range(half_tiles):
+        part_copy(tile).wait()
+    in_out[...] = in_out[...] + part_got[...].astype(f32)
+
+
+def mlp_back(own, pre_act, down_weight, up_weight, mid, first, last):
+    rows, width = own.shape
+    hidden = pre_act.shape[1]
+    proj_jobs = mid[1].shape[1] // TILE + -(-first[1].shape[1] // TILE) + last[1].shape[1] // (2 * TILE)
+    proj_tokens, proj_hidden = mid[0].shape
+    tile = (proj_hidden // 32, TILE)
+    dma = pltpu.SemaphoreType.DMA
+
+    def low(*lead):
+        return pltpu.VMEM(lead + tile, bf16)
+
+    return pl.pallas_call(
+        functools.partial(mlp_back_kernel, proj_jobs),
+        out_shape=(
+            jax.ShapeDtypeStruct((2 * rows, width), bf16),
+            jax.ShapeDtypeStruct((2 * rows, hidden), bf16),
+            jax.ShapeDtypeStruct((rows, width), f32),
+            jax.ShapeDtypeStruct((8, hidden), f32),
+            jax.ShapeDtypeStruct((proj_jobs,) + tile, f32),
+        ),
+        in_specs=[whole_spec(), whole_spec(pl.ANY), whole_spec(), whole_spec()] + [whole_spec(pl.ANY)] * 6,
+        out_specs=(whole_spec(), whole_spec(pl.ANY), whole_spec(), whole_spec(), whole_spec()),
+        scratch_shapes=[
+            pltpu.VMEM((2, SHORT, hidden), f32),
+            pltpu.VMEM((2, SHORT, hidden), bf16),
+            pltpu.VMEM((rows, width), bf16),
+            pltpu.VMEM((rows, width), bf16),
+            pltpu.VMEM((proj_tokens, proj_hidden), bf16),
+            pltpu.VMEM((proj_hidden, proj_tokens), bf16),
+            pltpu.VMEM((2, proj_tokens, 2 * TILE), bf16),
+            low(SLOTS, 2, 2, 2, 4),
+            low(SLOTS, 2, 2, 4),
+            low(SLOTS, 2, 2, 4),
+            low(SLOTS, 2, 4),
+            low(SLOTS, 2, 4),
+            low(SLOTS, 4),
+            low(SLOTS, 4),
+            low(SLOTS, 3),
+            dma((2,)),
+            dma((2,)),
+            dma((2,)),
+            dma((2, rows // SHORT)),
+            dma,
+            dma((2,)),
+            dma((2, SLOTS)),
+            dma((2, SLOTS)),
+            dma((2, SLOTS)),
+            dma((2, SLOTS, 3)),
+        ],
+        compiler_params=pltpu.CompilerParams(
+            collective_id=3, has_side_effects=True, vmem_limit_bytes=58 << 20
+        ),
+        cost_estimate=pl.CostEstimate(flops=3 * 10**10, bytes_accessed=5 * 10**7, transcendentals=0),
+        name="mlp_back",
+    )(own, pre_act, down_weight, up_weight, *mid, *first, *last)
 
 
 def fetch_kernel(
     tokens_ref,
     qkv_ref,
+    out_ref,
     cond_ref,
+    bias_ref,
+    ids_ref,
     ada_ref,
     ada_bias_ref,
     tokens_out,
     qkv_out,
+    out_out,
     cond_out,
+    bias_out,
+    ids_out,
     mod_out,
     ada_tile,
     token_hold,
     qkv_hold,
+    out_hold,
     token_sems,
     cond_sems,
     x_sems,
@@ -1518,7 +1754,8 @@
     away = core != x
     pieces = x_sems.shape[1]
     quarter = qkv_ref.shape[0] // 4
-    height = quarter // pieces
+    height = quarter // (pieces - 1)
+    out_quarter = out_ref.shape[0] // 4
 
     def device(z_at, y_at, core_at, x_at):
         return ((z_at * 2 + y_at) * 2 + core_at, x_at)
@@ -1543,49 +1780,60 @@
             device_id_type=MESH,
         )
 
-    def span(y_at, piece):
-        return pl.ds(pl.multiple_of((y_at * 2 + z_near) * quarter + piece * height, 32), height)
+    def part(whole, other, y_at, piece):
+        at = y_at * 2 + z_near
+        if piece == pieces - 1:
+            return other.at[pl.ds(pl.multiple_of(at * out_quarter, 16), out_quarter), :]
+        return whole.at[pl.ds(pl.multiple_of(at * quarter + piece * height, 32), height), :]
 
     def x_copy(piece):
-        return remote(qkv_ref.at[span(y, piece), :], qkv_out.at[span(y, piece), :], x_sems, (piece,), swap_peer)
+        source = part(qkv_ref, out_ref, y, piece)
+        return remote(source, part(qkv_out, out_out, y, piece), x_sems, (piece,), swap_peer)
 
     def y_copy(piece):
-        return remote(qkv_out.at[span(y, piece), :], qkv_out.at[span(y, piece), :], y_sems, (piece,), y_peer)
+        here = part(qkv_out, out_out, y, piece)
+        return remote(here, here, y_sems, (piece,), y_peer)
 
     def z_copy(piece, other):
-        y_at = 1 - y if other else y
-        rows = span(y_at, piece)
-        return remote(qkv_out.at[rows, :], qkv_out.at[rows, :], z_sems, (int(other), piece), z_peer)
+        here = part(qkv_out, out_out, 1 - y if other else y, piece)
+        return remote(here, here, z_sems, (int(other), piece), z_peer)
 
     token_copy = remote(tokens_ref, tokens_out, token_sems, (), swap_peer)
-    cond_copy = remote(cond_ref, cond_out, cond_sems, (), core_peer)
+    cond_copy = remote(cond_ref, cond_out, cond_sems, (0,), core_peer)
+    ids_copy = remote(ids_ref, ids_out, cond_sems, (1,), core_peer)
+    bias_copy = remote(bias_ref, bias_out, cond_sems, (2,), swap_peer)
     local_in = [
         pltpu.make_async_copy(tokens_ref, token_hold, local_sems.at[0]),
         pltpu.make_async_copy(qkv_ref, qkv_hold, local_sems.at[1]),
+        pltpu.make_async_copy(out_ref, out_hold, local_sems.at[2]),
     ]
     local_out = [
-        pltpu.make_async_copy(token_hold, tokens_out, local_sems.at[2]),
-        pltpu.make_async_copy(qkv_hold, qkv_out, local_sems.at[3]),
+        pltpu.make_async_copy(token_hold, tokens_out, local_sems.at[3]),
+        pltpu.make_async_copy(qkv_hold, qkv_out, local_sems.at[4]),
+        pltpu.make_async_copy(out_hold, out_out, local_sems.at[5]),
     ]
 
     @pl.when(away)
     def _():
         for piece in range(pieces):
             x_copy(piece).start()
-        token_copy.start()
+        bias_copy.start()
 
     @pl.when(home)
     def _():
         cond_copy.start()
+        ids_copy.start()
         for copy in local_in:
             copy.start()
         cond_out[...] = cond_ref[...]
+        ids_out[...] = ids_ref[...]
+        bias_out[...] = bias_ref[...]
 
     tile_cols = ada_tile.shape[2]
     tiles = ada_ref.shape[1] // tile_cols
 
     def ada_copy(tile, slot):
-        columns = pl.ds(pl.multiple_of(tile * tile_cols, LANES), tile_cols)
+        columns = pl.ds(tile * tile_cols, tile_cols)
         return pltpu.make_async_copy(ada_ref.at[:, columns], ada_tile.at[slot], ada_sems.at[slot])
 
     ada_copy(0, 0).start()
@@ -1597,31 +1845,37 @@
     cond = cond_out[...].astype(f32)
     low = (cond / (1.0 + jnp.exp(-cond))).astype(bf16)
 
-    def modulate(tile, carry):
-        slot = lax.rem(tile, 2)
+    def modulate(tile):
+        slot = tile % 2
         ada_copy(tile, slot).wait()
 
-        @pl.when(tile + 1 < tiles)
-        def _():
+        if tile + 1 < tiles:
             ada_copy(tile + 1, 1 - slot).start()
 
-        columns = pl.ds(pl.multiple_of(tile * tile_cols, LANES), tile_cols)
+        columns = slice(tile * tile_cols, (tile + 1) * tile_cols)
         product = jnp.dot(low, ada_tile[slot], preferred_element_type=f32)
         mod_out[:, columns] = product + ada_bias_ref[:, columns].astype(f32)
-        return carry
-
-    lax.fori_loop(0, tiles, modulate, 0)
+
+    for tile in range(tiles):
+        modulate(tile)
+        if tile % 2 == 1 and tile // 2 < pieces:
+
+            @pl.when(away)
+            def _(piece=tile // 2):
+                x_copy(piece).wait_recv()
+                y_copy(piece).start()
+                z_copy(piece, False).start()
+                if piece == 0:
+                    token_copy.start()
 
     @pl.when(away)
     def _():
-        for piece in range(pieces):
-            x_copy(piece).wait_recv()
-            y_copy(piece).start()
-            z_copy(piece, False).start()
         for piece in range(pieces):
             y_copy(piece).wait_recv()
             z_copy(piece, True).start()
         token_copy.wait()
+        ids_copy.wait_recv()
+        bias_copy.wait()
         for piece in range(pieces):
             x_copy(piece).wait_send()
             y_copy(piece).wait_send()
@@ -1631,6 +1885,7 @@
     @pl.when(home)
     def _():
         cond_copy.wait_send()
+        ids_copy.wait_send()
         for copy, onward in zip(local_in, local_out):
             copy.wait()
             onward.start()
@@ -1638,29 +1893,33 @@
             copy.wait()
 
 
-def fetch(tokens, qkv, condition, ada_weight, ada_bias):
-    pieces = 3
+def fetch(tokens, qkv, out, condition, bias, ids, ada_weight, ada_bias):
+    pieces = 4
     dma = pltpu.SemaphoreType.DMA
     return pl.pallas_call(
         fetch_kernel,
         out_shape=(
             jax.ShapeDtypeStruct(tokens.shape, bf16),
             jax.ShapeDtypeStruct(qkv.shape, bf16),
+            jax.ShapeDtypeStruct(out.shape, bf16),
             jax.ShapeDtypeStruct(condition.shape, bf16),
+            jax.ShapeDtypeStruct(bias.shape, bf16),
+            jax.ShapeDtypeStruct(ids.shape, jnp.int32),
             jax.ShapeDtypeStruct((condition.shape[0], ada_weight.shape[1]), f32),
         ),
-        in_specs=[whole_spec(pl.ANY), whole_spec(pl.ANY), whole_spec(), whole_spec(pl.ANY), whole_spec()],
-        out_specs=(whole_spec(pl.ANY), whole_spec(pl.ANY), whole_spec(), whole_spec()),
+        in_specs=[whole_spec(pl.ANY)] * 3 + [whole_spec()] * 3 + [whole_spec(pl.ANY), whole_spec()],
+        out_specs=(whole_spec(pl.ANY),) * 3 + (whole_spec(),) * 4,
         scratch_shapes=[
             pltpu.VMEM((2, ada_weight.shape[0], ada_weight.shape[1] // 9), bf16),
             pltpu.VMEM(tokens.shape, bf16),
             pltpu.VMEM(qkv.shape, bf16),
+            pltpu.VMEM(out.shape, bf16),
             dma((2,)),
-            dma((2,)),
+            dma((2, 3)),
             dma((2, pieces)),
             dma((2, pieces)),
             dma((2, 2, pieces)),
-            dma((4,)),
+            dma((6,)),
             dma((2,)),
         ],
         compiler_params=pltpu.CompilerParams(
@@ -1668,7 +1927,7 @@
         ),
         cost_estimate=pl.CostEstimate(flops=10**10, bytes_accessed=3 * 10**7, transcendentals=0),
         name="fetch",
-    )(tokens, qkv, condition, ada_weight, ada_bias.reshape(1, -1))
+    )(tokens, qkv, out, condition, bias, ids, ada_weight, ada_bias.reshape(1, -1))
 
 
 def after(value, earlier):
@@ -1722,11 +1981,19 @@
     def swap(value):
         return jnp.where(home, value, send(value, to_diag))
 
-    tokens, qkv_half, cond_low, modulation = fetch(
-        tokens_in, qkv_weight.reshape(width, 3 * local_cols), condition, ada_weight, ada_bias
-    )
-    packed_ids = send(image_ids, to_core)
-    ids = jnp.where(home, image_ids, packed_ids)
+    bias_pack = jnp.concatenate([qv_bias.reshape(-1), up_bias]).reshape(-1, LANES)
+    tokens, qkv_half, out_half, cond_low, bias_half, ids, modulation = fetch(
+        tokens_in,
+        qkv_weight.reshape(width, 3 * local_cols),
+        out_weight,
+        condition,
+        bias_pack,
+        image_ids.reshape(-1, LANES),
+        ada_weight,
+        ada_bias,
+    )
+    bias_half = bias_half.reshape(-1).astype(f32)
+    unit_ids = ids[:: SHORT // LANES, 0]
 
     def over_x(weight, earlier):
         own = lax.dynamic_slice_in_dim(weight, y * (weight.shape[0] // 2), weight.shape[0] // 2)
@@ -1739,20 +2006,11 @@
         mine = jnp.arange(2).reshape(2, 1, 1) == y
         return jnp.where(home, halves, jnp.where(mine, first[None], second[None])).reshape(weight.shape)
 
-    out_first = over_x(out_weight, tokens)
     up_first = over_x(up_weight, tokens)
-    down_first = over_x(down_weight, up_first)
-    out_half = over_y(out_weight, out_first)
-    up_half = over_y(up_weight, up_first)
     features = jnp.where(home, enc_features, send(enc_features, to_core))
-    rows_low = swap(after(target_rows, up_first))
-    grad_out = swap(after(out_grad, down_first))
-    bias_pack = jnp.concatenate([qv_bias.reshape(-1), up_bias])
-    bias_half = swap(bias_pack).astype(f32)
     qv_half = bias_half[: 2 * local_cols].reshape(2, local_cols)
     up_bias_half = bias_half[2 * local_cols :]
 
-    unit_ids = ids.reshape(-1, SHORT)[:, 0]
     same = unit_ids[:, None] == unit_ids[None, :]
     starts = jnp.argmax(same, axis=1).astype(jnp.int32)
     counts = jnp.sum(same.astype(jnp.int32), axis=1).astype(jnp.int32)
@@ -1791,10 +2049,14 @@
         [qv_half[0], jnp.zeros_like(qv_half[0]), qv_half[1], jnp.zeros((qkv_cols - 3 * local_cols,), f32)]
     )
     qkv = (dot_nn(attn_all, qkv_pad) + qkv_bias).astype(bf16)
-    qkv = after(qkv, (out_first, up_first))
+    qkv, up_first = lax.optimization_barrier((qkv, up_first))
+    up_half = over_y(up_weight, up_first)
+    down_first = over_x(down_weight, up_first)
     attended, log_sums = attend(starts, counts, qkv, heads, out_cols)
     attended, down_first = lax.optimization_barrier((attended, down_first))
     down_half = over_y(down_weight, down_first)
+    rows_low = swap(after(target_rows, down_first))
+    grad_out = swap(after(out_grad, down_first))
     attn_branch = by_unit(reduce_cores(attended, out_pad, dot_nn) + out_bias.astype(f32))
     mid = resid + gate_one * attn_branch
 
@@ -1802,8 +2064,7 @@
     mlp_in = flat((normed_two * (1.0 + scale_two) + shift_two).astype(bf16))
     mlp_all = gather_cores(mlp_in)
     pre_act = dot_nn(mlp_all, up_half) + up_bias_half
-    act_value, act_back = jax.vjp(gelu_tanh, pre_act)
-    hidden = act_value.astype(bf16)
+    hidden = gelu_tanh(pre_act).astype(bf16)
     mlp_branch = by_unit(reduce_cores(hidden, down_half, dot_nn) + down_bias.astype(f32))
     block_value = mid + gate_two * mlp_branch
     block_low = flat(block_value.astype(bf16))
@@ -1826,10 +2087,16 @@
     grad_block = by_unit(grad_out.astype(f32) + dot_nt(grad_first_low, proj_in))
 
     grad_mlp_branch = gate_two * grad_block
-    grad_mlp_all = gather_cores(flat(grad_mlp_branch.astype(bf16)))
-    grad_pre = act_back(dot_nt(grad_mlp_all, down_half))[0]
-    grad_pre_low = grad_pre.astype(bf16)
-    grad_mlp_in = by_unit(reduce_cores(grad_pre_low, up_half, dot_nt))
+    grad_mlp_all, grad_pre_low, grad_mlp_in, up_bias_sums, proj_sum = mlp_back(
+        flat(grad_mlp_branch.astype(bf16)),
+        pre_act,
+        down_half,
+        up_half,
+        (grad_second_low, first_low),
+        (grad_first_low, block_low),
+        (grad_last_low, second_low),
+    )
+    grad_mlp_in = by_unit(grad_mlp_in)
     grad_mid = grad_block + norm_back(normed_two, inv_two, grad_mlp_in * (1.0 + scale_two))
 
     grad_attn_branch = gate_one * grad_mid
@@ -1863,7 +2130,7 @@
     qv_sums = qkv_bias_sums[:2]
     qv_full = lax.dynamic_update_slice_in_dim(jnp.zeros((2, width), f32), qv_sums, core * local_cols, axis=1)
     up_full = lax.dynamic_update_slice_in_dim(
-        jnp.zeros((2 * local_hidden,), f32), jnp.sum(grad_pre, axis=0), core * local_hidden, axis=0
+        jnp.zeros((2 * local_hidden,), f32), up_bias_sums[0], core * local_hidden, axis=0
     )
     pieces = [
         qv_full.reshape(-1),
@@ -1876,14 +2143,11 @@
     ]
     packed = jnp.concatenate(pieces)
     packed = jnp.pad(packed, (0, -packed.shape[0] % (8 * LANES))).reshape(-1, LANES)
-    first_sum, second_sum, proj_sum, sums, slot_sum, silu_sum, cond_sum = reduce_grads(
+    first_sum, second_sum, sums, slot_sum, silu_sum, cond_sum = reduce_grads(
         (grad_mlp_all, hidden),
-        (grad_attn_all, attended),
         (mlp_all, grad_pre_low),
         (attn_all, grad_qkv),
-        (grad_second_low, first_low),
-        (grad_first_low, block_low),
-        (grad_last_low, second_low),
+        (grad_attn_all, attended),
         packed,
         slot_cols,
         jnp.pad(silu_low, ((0, 8 - slots), (0, 0))),
@@ -1898,24 +2162,25 @@
     row_count = width // 16
 
     def columns(tiles):
-        return tiles.transpose(1, 0, 2).reshape(tiles.shape[1], -1)
-
-    def rows(tiles):
-        return tiles.transpose(0, 2, 1).reshape(-1, tiles.shape[1])
+        return tiles.reshape(-1, row_count, LANES).transpose(1, 0, 2).reshape(row_count, -1)
+
+    def rows(tiles, height):
+        return tiles.reshape(-1, height, tiles.shape[-1]).transpose(0, 2, 1).reshape(-1, height)
 
     down_tiles = local_hidden // TILE
-    sum_down = rows(first_sum[:down_tiles])
-    sum_out = rows(first_sum[down_tiles:])[:local_cols]
-    sum_up = columns(second_sum[:down_tiles])
-    sum_qkv = columns(second_sum[down_tiles:])[:, : 3 * local_cols].reshape(row_count, 3, local_cols)
+    sum_down = rows(first_sum[:down_tiles], row_count)
+    sum_up = columns(first_sum[down_tiles:])
+    qkv_tiles = qkv_cols // TILE
+    sum_qkv = columns(second_sum[:qkv_tiles])[:, : 3 * local_cols].reshape(row_count, 3, local_cols)
+    sum_out = rows(second_sum[qkv_tiles:], row_count)[:local_cols]
     mid_tiles = proj_mid.shape[0] // TILE
     in_tiles = -(-width // TILE)
-    sum_mid = rows(proj_sum[:mid_tiles])
-    sum_in = rows(proj_sum[mid_tiles : mid_tiles + in_tiles])[:width]
+    sum_mid = rows(proj_sum[:mid_tiles], proj_sum.shape[1])
+    sum_in = rows(proj_sum[mid_tiles : mid_tiles + in_tiles], proj_sum.shape[1])[:width]
     last_share = proj_last.shape[1] // 32
     last_tiles = proj_sum[mid_tiles + in_tiles :]
     last_tiles = last_tiles.reshape(last_tiles.shape[0] * 2, -1, TILE)[:, :last_share]
-    sum_last = rows(last_tiles)
+    sum_last = rows(last_tiles, last_share)
     found = []
     offset = 0
     for piece in pieces:

time: 702 us -> 679 us (0.967)
  Pallas kernels: 377 us -> 425 us
  matrix products: 161 us -> 124 us
  starting transfers between devices: 58.1 us -> 21.1 us
    pallas_call x1 -> x2, Pallas kernels: 26.4 us -> 147 us  [the longest x1 111 us: mlp_back(): pl.pallas_call(functools.partial(mlp_back_kernel, proj_jobs), out_shape=(...]
    pallas_call x1, Pallas kernels: 252 us -> 168 us  [reduce_grads(): pl.pallas_call(functools.partial(reduce_kernel, grid_rows, first_jobs, se...]
    dot_general x9 -> x6, matrix products: 80.9 us -> 43.2 us  [dot_nt(): lax.dot_general(left_arg, right_arg, (((1,), (1,)), ((), ())), preferred_...]
    ppermute x18 -> x13, starting transfers between devices: 58.1 us -> 21.1 us  [send(): return lax.ppermute(value, ('dp', 'tensor'), pairs_of(move))]
    pallas_call x1, Pallas kernels: 41.8 us -> 54.7 us  [attend_back(): pl.pallas_call(functools.partial(attend_back_kernel, heads, together, fac...]
    pallas_call x4 -> x3, Pallas kernels: 34.4 us -> 31.5 us  [gather_cores(): pl.pallas_call(gather_kernel, out_shape=jax.ShapeDtypeStruct((2, rows, wi...]
    select_n x3 -> x2, other arithmetic: 16.8 us -> 14.8 us  [over_y(): jnp.where(home, halves, jnp.where(mine, first[None], second[None]))]
  transfers between devices with their start and end apart: 18 -> 13, of which waited for: 1 -> 0; matrix products, arithmetic and copies ran while one was open for 28% -> 26% of each run, Pallas kernels for 48% -> 34%
where the time goes in v4:
time: 679 us; the launch traced here: 671 us
  Pallas kernels  425 us (63%)
  matrix products  124 us (18%)
  other arithmetic  50.4 us (7%)
  local copies, waits for them, and re-layouts  47.9 us (7%)
  starting transfers between devices  21.1 us (3%)
    pallas_call x1, Pallas kernels, reduce_grads(): pl.pallas_call(functools.partial(reduce_kernel, grid_rows, first_jobs, se...  168 us
    pallas_call x1, Pallas kernels, mlp_back(): pl.pallas_call(functools.partial(mlp_back_kernel, proj_jobs), out_shape=(...  111 us
    dot_general x9, matrix products, dot_nn(): return jnp.dot(left, right, preferred_element_type=f32)  78 us
    pallas_call x1, Pallas kernels, attend_back(): pl.pallas_call(functools.partial(attend_back_kernel, heads, together, fac...  54.7 us
    dot_general x6, matrix products, dot_nt(): lax.dot_general(left_arg, right_arg, (((1,), (1,)), ((), ())), preferred_...  43.2 us
    pallas_call x1, Pallas kernels, attend(): pl.pallas_call(functools.partial(attend_kernel, heads, 4, factor), out_sh...  36 us
    pallas_call x3, Pallas kernels, gather_cores(): pl.pallas_call(gather_kernel, out_shape=jax.ShapeDtypeStruct((2, rows, wi...  31.5 us
    pallas_call x1, Pallas kernels, fetch(): pl.pallas_call(fetch_kernel, out_shape=(jax.ShapeDtypeStruct(tokens.shape...  23.8 us
  transfers between devices with their start and end apart: 13, of which 0 were waited for; matrix products, arithmetic and copies ran while one was open for 26% of the time, Pallas kernels for 34%

profile of v4, /device:TPU:0, one launch (start us, length us, event | category | flops | bytes accessed | tf_op | source)
XLA Modules:
  0.0 671.1 jit_solution(5859066040116690581)
XLA Ops:
  0.7 6.6 copy.63.qkv_ref
  12.1 23.8 %fetch.1 = (bf16[768,1152]{1,0:T(8,128)(2,1)}, bf16[1152,1728]{1,0:T(8,128)(2,1)}, bf16[576,1152]{1,0:T(8,128)(2,1)}, bf16[6,1152]{1,0:T(8,128)(2,1)}, bf16[27,1...) custom-call(bf16[768,1152]{1,0:T(8,128)(2,1)} %tokens_ref.1, bf16[1152,1728]{1,0:T(8,128)(2,1)} %copy.63.qkv_ref, ...), custom_call_target="tpu_custom_call" | custom-call | flops 10000000000 | bytes 30000000 | tf_op jit(solution)/shard_map/fetch/pallas_call | solution.py:1899
  48.7 24.0 %gather_cores.3 = bf16[2,768,1152]{2,1,0:T(8,128)(2,1)S(1)} custom-call(bf16[768,1152]{1,0:T(8,128)(2,1)S(1)} %fusion.16.own_ref), custom_call_target="tpu_custom_call" | custom-call | bytes 12000000 | tf_op jit(solution)/shard_map/gather_cores/pallas_call | solution.py:535
  74.7 11.7 %add_convert_fusion.qkv_ref = bf16[1536,1792]{1,0:T(8,128)(2,1)} fusion(bf16[1536,1152]{1,0:T(8,128)(2,1)} %bitcast.169, f32[1792]{0:T(1024)S(1)} %concatenate.13, bf16[1152,1728]{1,0:T(8,128)(2,1)} %get-tuple-element.60), kind=kOutput, calls=%fused_computation.11 | convolution fusion | flops 6347292672 | bytes 13032448 | tf_op jit(solution)/shard_map/dot_general | solution.py:2039
  94.5 36.0 %attend.1 = (bf16[1536,768]{1,0:T(8,128)(2,1)S(1)}, f32[48,1,256]{2,1,0:T(1,128)S(1)}) custom-call(s32[6]{0:T(128)S(1)} %get-tuple-element.59.starts, s32[6]{0:T(128)S(1)} %fusion.63.counts, bf16[1536,1792]{1,0:T(8,128)(2,1)S(1)} %copy-done.10), custom_call_target="tpu_custom_call" | custom-call | flops 20000000000 | bytes 13000000 | tf_op jit(solution)/shard_map/attend/pallas_call | solution.py:611
  133.5 4.8 collective-permute-start.2
  141.2 7.2 %fusion.13.up_ref = bf16[1152,2304]{1,0:T(8,128)(2,1)} fusion(bf16[1152,2304]{1,0:T(8,128)(2,1)} %param.30, pred[1152]{0:T(1024)(128)(4,1)S(1)} %broadcast_in_dim.130, pred[]{:T(512)S(6)} %eq.51, bf16[576,2304]{1,0:T(8,128)(2,1)} %collective-permute-done.3, bf16[576,2304]{1,0:T(8,128)(2,1)} %collective-permute-done), kind=kLoop, calls=%fused_computation.25 | loop fusion | flops 5308416 | bytes 15926401 | tf_op jit(solution)/shard_map/jit(_where)/select_n | solution.py:2007
  148.3 6.3 fusion.90
  160.2 15.6 %fusion.7 = (bf16[1536,2304]{1,0:T(8,128)(2,1)}, f32[1536,2304]{1,0:T(8,128)}) fusion(f32[2304]{0:T(1024)S(1)} %slice_bitcast_fusion.4, bf16[1536,1152]{1,0:T(8,128)(2,1)S(1)} %bitcast.171, bf16[1152,2304]{1,0:T(8,128)(2,1)S(1)} %bitcast.183), kind=kOutput, calls=%fused_computation.9 | convolution fusion | flops 8189116416 | bytes 30090240 | tf_op jit(solution)/shard_map/dot_general | solution.py:2039
  175.8 7.6 %fusion.12.down_ref = bf16[2304,1152]{1,0:T(8,128)(2,1)} fusion(bf16[2304,1152]{1,0:T(8,128)(2,1)} %param.32, pred[2304]{0:T(1024)(128)(4,1)S(1)} %broadcast_in_dim.137, pred[]{:T(512)S(6)} %eq.51, bf16[1152,1152]{1,0:T(8,128)(2,1)} %collective-permute-done.4, bf16[1152,1152]{1,0:T(8,128)(2,1)} %collective-permute-done.1), kind=kLoop, calls=%fused_computation.23 | loop fusion | flops 5308416 | bytes 15927553 | tf_op jit(solution)/shard_map/jit(_where)/select_n | solution.py:2007
  183.4 9.6 %fusion.30 = bf16[768,1152]{1,0:T(8,128)(2,1)} fusion(bf16[2304,1152]{1,0:T(8,128)(2,1)} %fusion.12.down_ref, bf16[1536,2304]{1,0:T(8,128)(2,1)} %get-tuple-element.179.one_right, s32[]{:T(128)S(6)} %select_n.132), kind=kOutput, calls=%fused_computation.64 | convolution fusion | flops 4077748224 | bytes 10616836 | tf_op jit(solution)/shard_map/dot_general | solution.py:2039
  199.0 6.1 gather_fusion
  205.2 11.8 %fusion.18 = (bf16[768,1152]{1,0:T(8,128)(2,1)S(1)}, f32[768,1152]{1,0:T(8,128)}) fusion(f32[768,1152]{1,0:T(8,128)} %copy-done.11, f32[3,1152]{1,0:T(4,128)S(1)} %get-tuple-element.162, f32[1152]{0:T(1024)S(1)} %convert_element_type.166, bf16[768,1152]{1,0:T(8,128)(2,1)} %collective-permute-done.5, bf16[2304,1152]{1,0:T(8,128)(2,1)} %fusion.12.down_ref, ...), kind=kOutput, calls=%fused_computation.38 | convolution fusion | flops 4083941376 | bytes 19482628 | tf_op jit(solution)/shard_map/dot_general | solution.py:2039
  216.9 9.9 %multiply_convert_fusion.1 = (bf16[768,2048]{1,0:T(8,128)(2,1)S(1)}, f32[768,2048]{1,0:T(8,128)}) fusion(f32[2048]{0:T(1024)S(1)} %convert_element_type.169, bf16[768,1152]{1,0:T(8,128)(2,1)S(1)} %get-tuple-element.181.in_right, bf16[1152,2048]{1,0:T(8,128)(2,1)} %param.34), kind=kOutput, calls=%fused_computation.20 | convolution fusion | flops 3633315840 | bytes 15933440 | tf_op jit(solution)/shard_map/dot_general | solution.py:2039
  226.9 7.4 %multiply_convert_fusion = (bf16[768,2048]{1,0:T(8,128)(2,1)S(1)}, f32[768,2048]{1,0:T(8,128)S(1)}) fusion(f32[2048]{0:T(1024)S(1)} %convert_element_type.171, bf16[768,2048]{1,0:T(8,128)(2,1)S(1)} %get-tuple-element.183.mid_right, bf16[2048,2048]{1,0:T(8,128)(2,1)S(1)} %bitcast.207), kind=kOutput, calls=%fused_computation.18 | convolution fusion | flops 6451888128 | bytes 20979712 | tf_op jit(solution)/shard_map/dot_general | solution.py:2039
  238.3 4.5 fusion.86
  242.8 14.0 %fusion.88 = (f32[2048]{0:T(1024)S(1)}, bf16[768,2048]{1,0:T(8,128)(2,1)S(1)}) fusion(f32[768,2048]{1,0:T(8,128)} %get-tuple-element.184, f32[2048]{0:T(1024)S(1)} %convert_element_type.169, bf16[768,2048]{1,0:T(8,128)(2,1)S(1)} %get-tuple-element.147.mid_left, bf16[2048,2048]{1,0:T(8,128)(2,1)} %param.36), kind=kOutput, calls=%fused_computation.196 | convolution fusion | flops 6461323264 | bytes 20987904 | tf_op jit(solution)/shard_map/dot_general | solution.py:21
  256.9 6.9 %fusion.35 = (f32[1152]{0:T(1024)S(1)}, f32[768,1152]{1,0:T(8,128)S(1)}) fusion(f32[3,1152]{1,0:T(4,128)S(1)} %get-tuple-element.162, bf16[768,1152]{1,0:T(8,128)(2,1)} %param.43, bf16[768,1152]{1,0:T(8,128)(2,1)} %collective-permute-done.7, pred[]{:T(512)S(6)} %eq.51, bf16[768,2048]{1,0:T(8,128)(2,1)S(1)} %get-tuple-element.149.in_left, ...), kind=kOutput, calls=%fused_computation.72 | convolution fusion | flops 3628301312 | bytes 14960641 | tf_op jit(solution)/shard_map/dot_general | solution.py:21
  267.0 111.2 %mlp_back.1 = (bf16[1536,1152]{1,0:T(8,128)(2,1)}, bf16[1536,2304]{1,0:T(8,128)(2,1)}, f32[768,1152]{1,0:T(8,128)}, f32[8,2304]{1,0:T(8,128)}, f32[17,64,256]{2,1,0:T(8,128)}) custom-call(bf16[768,1152]{1,0:T(8,128)(2,1)} %fusion.36.own_ref, f32[1536,2304]{1,0:T(8,128)} %get-tuple-element.180.pre_ref, bf16[2304,1152]{1,0:T(8,128)(2,1)} %fusion.12.down_ref, ...), custom_call_target="tpu_custom_call" | custom-call | flops 30000001024 | bytes 50000000 | tf_op jit(solution)/shard_map/mlp_back/pallas_call | solution.py:1673
  394.2 54.7 %attend_back.1 = (bf16[1536,1792]{1,0:T(8,128)(2,1)}, f32[8,576]{1,0:T(8,128)S(1)}) custom-call(s32[6]{0:T(128)S(1)} %copy-done.7, s32[6]{0:T(128)S(1)} %copy-done.9, bf16[1536,1792]{1,0:T(8,128)(2,1)} %add_convert_fusion.qkv_ref, f32[48,1,256]{2,1,0:T(1,128)S(1)} %get-tuple-element.79.log_ref, bf16[1536,768]{1,0:T(8,128)(2,1)S(1)} %convolution_convert_fusion.2.grad_ref), custom_call_target="tpu_custom_call" | custom-call | flops 40000000000 | bytes 25000000 | tf_op jit(solution)/shard_map/attend_back/pallas_call | solution.py:698
  449.0 6.7 %convolution_convert_fusion = bf16[768,1152]{1,0:T(8,128)(2,1)} fusion(bf16[1152,1728]{1,0:T(8,128)(2,1)S(1)} %copy-done.26, bf16[1536,1792]{1,0:T(8,128)(2,1)} %get-tuple-element.80.three_right, s32[]{:T(128)S(6)} %select_n.132), kind=kOutput, calls=%fused_computation.65 | convolution fusion | flops 3171778560 | bytes 8503300 | tf_op jit(solution)/shard_map/dot_general | solution.py:21
  465.4 7.8 %fusion.40 = (f32[768]{0:T(1024)S(1)}, f32[768]{0:T(1024)S(1)}, f32[768,1152]{1,0:T(8,128)S(1)}) fusion(f32[3,1152]{1,0:T(4,128)S(1)} %copy-done.36, f32[768]{0:T(1024)S(1)} %copy-done.44, f32[768]{0:T(1024)S(1)} %copy-done.40, bf16[768,1152]{1,0:T(8,128)(2,1)S(1)} %copy-done.14, bf16[768,1152]{1,0:T(8,128)(2,1)} %collective-permute-done.10, ...), kind=kOutput, calls=%fused_computation.80 | convolution fusion | flops 3180624384 | bytes 13985284 | tf_op jit(solution)/shard_map/dot_general | solution.py:21
  473.2 5.2 multiply_reduce_fusion.1
  485.7 167.7 %reduce_grads.1 = (f32[18,144,128]{2,1,0:T(8,128)}, f32[10,144,128]{2,1,0:T(8,128)S(1)}, f32[112,128]{1,0:T(8,128)S(1)}, f32[4,2,2,8,256]{4,3,2,1,0:T(8,128)S(1)...) custom-call(bf16[1536,1152]{1,0:T(8,128)(2,1)} %get-tuple-element.81.one_left, ...), custom_call_target="tpu_custom_call" | custom-call | flops 99999997952 | bytes 100000000 | tf_op jit(solution)/shard_map/reduce_grads/pallas_call | solution.py:1289
  (292 shorter events, 101.6 us)
Async XLA Ops:
  0.7 233.6 %copy-start = (bf16[2048,768]{1,0:T(8,128)(2,1)S(1)}, bf16[2048,768]{1,0:T(8,128)(2,1)}, u32[]{:S(2)}) copy-start(bf16[2048,768]{1,0:T(8,128)(2,1)} %param.38) | copy-start | bytes 9437188
  35.9 50.4 %collective-permute-start = (bf16[576,2304]{1,0:T(8,128)(2,1)}, bf16[576,2304]{1,0:T(8,128)(2,1)}, u32[]{:S(2)}, u32[]{:S(2)}) collective-permute-start(bf16[576,2304]{1,0:T(8,128)(2,1)} %constant_dynamic-slice_fusion.3), channel_id=1, source_target_pairs={{1,2},{2,1},{5,6},{6,5},{9,10},{10,9},{13,14},{14,13},{17,18},{18,... | collective-permute-start | bytes 7962632 | tf_op jit(solution)/shard_map/ppermute | solution.py:471
  42.0 106.3 %copy-start.31 = (f32[3,1152]{1,0:T(4,128)}, f32[3,1152]{1,0:T(4,128)S(1)}, u32[]{:S(2)}) copy-start(f32[3,1152]{1,0:T(4,128)S(1)} %get-tuple-element.167) | copy-start | bytes 41476
  42.0 113.1 %copy-start.33 = (f32[3,1152]{1,0:T(4,128)}, f32[3,1152]{1,0:T(4,128)S(1)}, u32[]{:S(2)}) copy-start(f32[3,1152]{1,0:T(4,128)S(1)} %get-tuple-element.164) | copy-start | bytes 41476
  47.7 25.0 %copy-start.43 = (f32[768]{0:T(1024)}, f32[768]{0:T(1024)S(1)}, u32[]{:S(2)}) copy-start(f32[768]{0:T(1024)S(1)} %add_rsqrt_fusion.1) | copy-start | bytes 9220
  86.4 44.2 %collective-permute-start.1 = (bf16[1152,1152]{1,0:T(8,128)(2,1)}, bf16[1152,1152]{1,0:T(8,128)(2,1)}, u32[]{:S(2)}, u32[]{:S(2)}) collective-permute-start(bf16[1152,1152]{1,0:T(8,128)(2,1)} %constant_dynamic-slice_fusion.2), channel_id=1, source_target_pairs={{1,2},{2,1},{5,6},{6,5},{9,10},{10,9},{13,14},{14,13},{17,18},{18,... | collective-permute-start | bytes 7962632 | tf_op jit(solution)/shard_map/ppermute | solution.py:471
  88.8 41.7 %copy-start.8 = (s32[6]{0:T(128)}, s32[6]{0:T(128)S(1)}, u32[]{:S(2)}) copy-start(s32[6]{0:T(128)S(1)} %fusion.63.counts) | copy-start | bytes 76
  89.5 41.0 %copy-start.6 = (s32[6]{0:T(128)}, s32[6]{0:T(128)S(1)}, u32[]{:S(2)}) copy-start(s32[6]{0:T(128)S(1)} %get-tuple-element.59.starts) | copy-start | bytes 76
  89.5 49.1 %collective-permute-start.3 = (bf16[576,2304]{1,0:T(8,128)(2,1)}, bf16[576,2304]{1,0:T(8,128)(2,1)}, u32[]{:S(2)}, u32[]{:S(2)}) collective-permute-start(bf16[576,2304]{1,0:T(8,128)(2,1)} %collective-permute-done), channel_id=1, source_target_pairs={{1,5},{2,6},{5,1},{6,2},{9,13},{10,14},{13,9},{14,10},{17,21},{18,... | collective-permute-start | bytes 7962632 | tf_op jit(solution)/shard_map/ppermute | solution.py:471
  94.4 36.1 %copy-start.28 = (bf16[576,1152]{1,0:T(8,128)(2,1)S(1)}, bf16[576,1152]{1,0:T(8,128)(2,1)}, u32[]{:S(2)}) copy-start(bf16[576,1152]{1,0:T(8,128)(2,1)} %get-tuple-element.68) | copy-start | bytes 3981316
  133.5 14.9 %collective-permute-start.2 = (bf16[768,1152]{1,0:T(8,128)(2,1)}, bf16[768,1152]{1,0:T(8,128)(2,1)}, u32[]{:S(2)}, u32[]{:S(2)}) collective-permute-start(bf16[768,1152]{1,0:T(8,128)(2,1)} %convolution_convert_fusion.3), channel_id=1, source_target_pairs={{0,2},{1,3},{2,0},{3,1},{4,6},{5,7},{6,4},{7,5},{8,10},{9,11},{10,... | collective-permute-start | bytes 5308424 | tf_op jit(solution)/shard_map/ppermute | solution.py:471
  138.3 55.5 %collective-permute-start.9 = (bf16[1536,768]{1,0:T(8,128)(2,1)}, bf16[1536,768]{1,0:T(8,128)(2,1)}, u32[]{:S(2)}, u32[]{:S(2)}) collective-permute-start(bf16[1536,768]{1,0:T(8,128)(2,1)} %param.40), channel_id=1, source_target_pairs={{0,2},{1,3},{2,0},{3,1},{4,6},{5,7},{6,4},{7,5},{8,10},{9,11},{10,... | collective-permute-start | bytes 7077896 | tf_op jit(solution)/shard_map/ppermute | solution.py:471
  138.6 37.2 %collective-permute-start.4 = (bf16[1152,1152]{1,0:T(8,128)(2,1)}, bf16[1152,1152]{1,0:T(8,128)(2,1)}, u32[]{:S(2)}, u32[]{:S(2)}) collective-permute-start(bf16[1152,1152]{1,0:T(8,128)(2,1)} %collective-permute-done.1), channel_id=1, source_target_pairs={{1,5},{2,6},{5,1},{6,2},{9,13},{10,14},{13,9},{14,10},{17,21},{18,... | collective-permute-start | bytes 7962632 | tf_op jit(solution)/shard_map/ppermute | solution.py:471
  193.0 12.2 %collective-permute-start.5 = (bf16[768,1152]{1,0:T(8,128)(2,1)}, bf16[768,1152]{1,0:T(8,128)(2,1)}, u32[]{:S(2)}, u32[]{:S(2)}) collective-permute-start(bf16[768,1152]{1,0:T(8,128)(2,1)} %fusion.30), channel_id=1, source_target_pairs={{0,2},{1,3},{2,0},{3,1},{4,6},{5,7},{6,4},{7,5},{8,10},{9,11},{10,... | collective-permute-start | bytes 5308424 | tf_op jit(solution)/shard_map/ppermute | solution.py:471
  193.1 5.9 collective-permute-start.8
  197.1 59.7 %collective-permute-start.7 = (bf16[768,1152]{1,0:T(8,128)(2,1)}, bf16[768,1152]{1,0:T(8,128)(2,1)}, u32[]{:S(2)}, u32[]{:S(2)}) collective-permute-start(bf16[768,1152]{1,0:T(8,128)(2,1)} %param.43), channel_id=1, source_target_pairs={{1,2},{2,1},{5,6},{6,5},{9,10},{10,9},{13,14},{14,13},{17,18},{18,... | collective-permute-start | bytes 5308424 | tf_op jit(solution)/shard_map/ppermute | solution.py:471
  267.0 111.2 %copy-start.34 = (f32[3,1152]{1,0:T(4,128)S(1)}, f32[3,1152]{1,0:T(4,128)}, u32[]{:S(2)}) copy-start(f32[3,1152]{1,0:T(4,128)} %copy-done.33) | copy-start | bytes 41476
  267.0 111.2 %copy-start.38 = (f32[768]{0:T(1024)S(1)}, f32[768]{0:T(1024)}, u32[]{:S(2)}) copy-start(f32[768]{0:T(1024)} %copy-done.37) | copy-start | bytes 9220
  267.0 111.2 %copy-start.42 = (f32[768]{0:T(1024)S(1)}, f32[768]{0:T(1024)}, u32[]{:S(2)}) copy-start(f32[768]{0:T(1024)} %copy-done.41) | copy-start | bytes 9220
  394.2 54.7 %copy-start.26 = (bf16[1152,1728]{1,0:T(8,128)(2,1)S(1)}, bf16[1152,1728]{1,0:T(8,128)(2,1)}, u32[]{:S(2)}) copy-start(bf16[1152,1728]{1,0:T(8,128)(2,1)} %get-tuple-element.60) | copy-start | bytes 11943940
  455.7 9.6 %collective-permute-start.10 = (bf16[768,1152]{1,0:T(8,128)(2,1)}, bf16[768,1152]{1,0:T(8,128)(2,1)}, u32[]{:S(2)}, u32[]{:S(2)}) collective-permute-start(bf16[768,1152]{1,0:T(8,128)(2,1)} %convolution_convert_fusion), channel_id=1, source_target_pairs={{0,2},{1,3},{2,0},{3,1},{4,6},{5,7},{6,4},{7,5},{8,10},{9,11},{10,... | collective-permute-start | bytes 5308424 | tf_op jit(solution)/shard_map/ppermute | solution.py:471
  456.0 27.7 %collective-permute-start.6 = (bf16[768,1152]{1,0:T(8,128)(2,1)}, bf16[768,1152]{1,0:T(8,128)(2,1)}, u32[]{:S(2)}, u32[]{:S(2)}) collective-permute-start(bf16[768,1152]{1,0:T(8,128)(2,1)} %copy-done.23), channel_id=1, source_target_pairs={{1,2},{2,1},{5,6},{6,5},{9,10},{10,9},{13,14},{14,13},{17,18},{18,... | collective-permute-start | bytes 5308424 | tf_op jit(solution)/shard_map/ppermute | solution.py:471
  478.8 6.3 collective-permute-start.12
  481.8 185.0 %collective-permute-start.11 = (bf16[768,1152]{1,0:T(8,128)(2,1)}, bf16[768,1152]{1,0:T(8,128)(2,1)}, u32[]{:S(2)}, u32[]{:S(2)}) collective-permute-start(bf16[768,1152]{1,0:T(8,128)(2,1)} %add_convert_fusion.1), channel_id=1, source_target_pairs={{1,2},{2,1},{5,6},{6,5},{9,10},{10,9},{13,14},{14,13},{17,18},{18,... | collective-permute-start | bytes 5308424 | tf_op jit(solution)/shard_map/ppermute | solution.py:471
  (57 other events, 404.2 us)

commit v5 on v4

--- a/solution.py
+++ b/solution.py
@@ -751,10 +751,14 @@
     f1_got,
     f2,
     f2_got,
+    f3,
+    f3_got,
     s0,
     s0_got,
     s1,
     s1_got,
+    far,
+    far_got,
     s2,
     s2_turn,
     s2_swap,
@@ -777,8 +781,10 @@
     f0_sems,
     f1_sems,
     f2_sems,
+    f3_sems,
     s0_sems,
     s1_sems,
+    far_sems,
     s2_sems,
     bias_sems,
     slot_sems,
@@ -899,18 +905,25 @@
     def f1_copy(slot):
         return remote(f1.at[slot, 1 - y], f1_got.at[slot], f1_sems, (slot,), y_peer)
 
-    def f2_copy(slot, ahead):
-        return remote(
-            f2.at[slot, lax.rem(z + ahead, 4)], f2_got.at[slot, ahead - 1], f2_sems, (slot, ahead - 1), z_peer(ahead)
-        )
+    z_low = lax.rem(z, 2)
+    z_high = z // 2
+    near_peer = device(z + 1 - 2 * z_low, y, core, x)
+    far_peer = device(lax.rem(z + 2, 4), y, core, x)
+
+    def f2_copy(slot):
+        return remote(f2.at[slot, 1 - z_low], f2_got.at[slot], f2_sems, (slot,), near_peer)
+
+    def f3_copy(slot):
+        return remote(f3.at[slot, 1 - z_high], f3_got.at[slot], f3_sems, (slot,), far_peer)
 
     def s0_copy(slot):
         return remote(s0.at[slot, 1 - y], s0_got.at[slot], s0_sems, (slot,), y_peer)
 
-    def s1_copy(slot, ahead):
-        return remote(
-            s1.at[slot, lax.rem(z + ahead, 4)], s1_got.at[slot, ahead - 1], s1_sems, (slot, ahead - 1), z_peer(ahead)
-        )
+    def s1_copy(slot):
+        return remote(s1.at[slot, 1 - z_low], s1_got.at[slot], s1_sems, (slot,), near_peer)
+
+    def far_copy(slot):
+        return remote(far.at[slot, 1 - z_high], far_got.at[slot], far_sems, (slot,), far_peer)
 
     def s2_copies(slot):
         turn = remote(s2.at[slot, 1 - x], s2_turn.at[slot], s2_sems, (0, slot), turn_to)
@@ -946,14 +959,22 @@
 
             multiply(first_left, first_right, slot, keep)
 
-        last = tick - 3 * GAP
+        last = tick - 4 * GAP
 
         @pl.when(inside(last, first_jobs))
         def _():
             slot = lax.rem(last, SLOTS)
-            for ahead in (1, 2, 3):
-                f2_copy(slot, ahead).wait()
-            first_out[last] = added(f2[slot, z], f2_got[slot, 0], f2_got[slot, 1], f2_got[slot, 2])
+            f3_copy(slot).wait()
+            first_out[last] = added(f3[slot, z_high], f3_got[slot])
+
+        fourth = tick - 3 * GAP
+
+        @pl.when(inside(fourth, first_jobs))
+        def _():
+            slot = lax.rem(fourth, SLOTS)
+            f2_copy(slot).wait()
+            f3[slot] = added(f2[slot, z_low], f2_got[slot]).astype(bf16)
+            f3_copy(slot).start()
 
         third = tick - 2 * GAP
 
@@ -961,9 +982,11 @@
         def _():
             slot = lax.rem(third, SLOTS)
             f1_copy(slot).wait()
-            f2[slot] = added(f1[slot, y], f1_got[slot]).astype(bf16)
-            for ahead in (1, 2, 3):
-                f2_copy(slot, ahead).start()
+            for low in range(2):
+                for high in range(2):
+                    at = high * 2 + low
+                    f2[slot, low, high] = added(f1[slot, y, at], f1_got[slot, at]).astype(bf16)
+            f2_copy(slot).start()
 
         second = tick - GAP
 
@@ -1026,7 +1049,7 @@
 
             multiply(second_left, second_right, slot, keep)
 
-        last = tick - 3 * GAP
+        last = tick - 4 * GAP
 
         @pl.when(inside(last, second_jobs))
         def _():
@@ -1047,17 +1070,16 @@
             def _():
                 pl.semaphore_signal(second_free, inc=1, device_id=turn_from, device_id_type=MESH)
 
-        third = tick - 2 * GAP
-
-        @pl.when(inside(third, second_jobs))
-        def _():
-            slot = lax.rem(third, SLOTS)
-            for ahead in (1, 2, 3):
-                s1_copy(slot, ahead).wait()
-            s2[slot] = added(s1[slot, z], s1_got[slot, 0], s1_got[slot, 1], s1_got[slot, 2]).astype(bf16)
+        fourth = tick - 3 * GAP
+
+        @pl.when(inside(fourth, second_jobs))
+        def _():
+            slot = lax.rem(fourth, SLOTS)
+            far_copy(slot).wait()
+            s2[slot] = added(far[slot, z_high], far_got[slot]).astype(bf16)
             turn, swap = s2_copies(slot)
 
-            @pl.when(third >= SLOTS)
+            @pl.when(fourth >= SLOTS)
             def _():
                 pl.semaphore_wait(second_free, 1)
 
@@ -1067,15 +1089,26 @@
             def _():
                 swap.start()
 
+        third = tick - 2 * GAP
+
+        @pl.when(inside(third, second_jobs))
+        def _():
+            slot = lax.rem(third, SLOTS)
+            s1_copy(slot).wait()
+            far[slot] = added(s1[slot, z_low], s1_got[slot]).astype(bf16)
+            far_copy(slot).start()
+
         second = tick - GAP
 
         @pl.when(inside(second, second_jobs))
         def _():
             slot = lax.rem(second, SLOTS)
             s0_copy(slot).wait()
-            s1[slot] = added(s0[slot, y], s0_got[slot]).astype(bf16)
-            for ahead in (1, 2, 3):
-                s1_copy(slot, ahead).start()
+            for low in range(2):
+                for high in range(2):
+                    at = high * 2 + low
+                    s1[slot, low, high] = added(s0[slot, y, at], s0_got[slot, at]).astype(bf16)
+            s1_copy(slot).start()
 
         @pl.when(tick < second_jobs)
         def _():
@@ -1218,7 +1251,7 @@
 
         return carry
 
-    ticks = max(first_jobs + 3 * GAP, ada_tiles + 6, -(-3 * (second_jobs + 3 * GAP) // 2))
+    ticks = max(first_jobs + 4 * GAP, ada_tiles + 6, -(-3 * (second_jobs + 4 * GAP) // 2))
     lax.fori_loop(0, ticks, tick_body, 0)
 
 
@@ -1245,12 +1278,16 @@
         low(SLOTS, 2, 4),
         low(SLOTS, 2, 4),
         low(SLOTS, 4),
-        low(SLOTS, 4),
-        low(SLOTS, 3),
+        low(SLOTS, 2, 2),
+        low(SLOTS, 2),
+        low(SLOTS, 2),
+        low(SLOTS),
         low(SLOTS, 2, 4, 2),
         low(SLOTS, 4, 2),
-        low(SLOTS, 4, 2),
-        low(SLOTS, 3, 2),
+        low(SLOTS, 2, 2, 2),
+        low(SLOTS, 2, 2),
+        low(SLOTS, 2, 2),
+        low(SLOTS, 2),
         low(SLOTS, 2),
         low(SLOTS),
         low(SLOTS),
@@ -1272,9 +1309,11 @@
         dma((2,)),
         dma((2, 2, SLOTS)),
         dma((2, SLOTS)),
-        dma((2, SLOTS, 3)),
         dma((2, SLOTS)),
-        dma((2, SLOTS, 3)),
+        dma((2, SLOTS)),
+        dma((2, SLOTS)),
+        dma((2, SLOTS)),
+        dma((2, SLOTS)),
         dma((2, 2, SLOTS)),
         dma((2, 5)),
         dma((2, 2)),
@@ -1725,6 +1764,8 @@
     ids_ref,
     ada_ref,
     ada_bias_ref,
+    up_ref,
+    down_ref,
     tokens_out,
     qkv_out,
     out_out,
@@ -1732,10 +1773,14 @@
     bias_out,
     ids_out,
     mod_out,
+    up_out,
+    down_out,
     ada_tile,
     token_hold,
     qkv_hold,
     out_hold,
+    up_hold,
+    down_hold,
     token_sems,
     cond_sems,
     x_sems,
@@ -1813,11 +1858,20 @@
         pltpu.make_async_copy(out_hold, out_out, local_sems.at[5]),
     ]
 
+    halves_in, halves_out = [], []
+    for at, (source, hold, target) in enumerate(((up_ref, up_hold, up_out), (down_ref, down_hold, down_out))):
+        rows = pl.ds(pl.multiple_of(y * hold.shape[0], 64), hold.shape[0])
+        halves_in.append(pltpu.make_async_copy(source.at[rows, :], hold, local_sems.at[6 + at]))
+        halves_out.append(pltpu.make_async_copy(hold, target, local_sems.at[8 + at]))
+
     @pl.when(away)
     def _():
         for piece in range(pieces):
             x_copy(piece).start()
         bias_copy.start()
+
+    for copy in halves_in:
+        copy.start()
 
     @pl.when(home)
     def _():
@@ -1867,6 +1921,10 @@
                 z_copy(piece, False).start()
                 if piece == 0:
                     token_copy.start()
+
+    for copy, onward in zip(halves_in, halves_out):
+        copy.wait()
+        onward.start()
 
     @pl.when(away)
     def _():
@@ -1892,8 +1950,11 @@
         for copy in local_out:
             copy.wait()
 
-
-def fetch(tokens, qkv, out, condition, bias, ids, ada_weight, ada_bias):
+    for copy in halves_out:
+        copy.wait()
+
+
+def fetch(tokens, qkv, out, condition, bias, ids, ada_weight, ada_bias, up, down):
     pieces = 4
     dma = pltpu.SemaphoreType.DMA
     return pl.pallas_call(
@@ -1906,20 +1967,24 @@
             jax.ShapeDtypeStruct(bias.shape, bf16),
             jax.ShapeDtypeStruct(ids.shape, jnp.int32),
             jax.ShapeDtypeStruct((condition.shape[0], ada_weight.shape[1]), f32),
+            jax.ShapeDtypeStruct((up.shape[0] // 2, up.shape[1]), bf16),
+            jax.ShapeDtypeStruct((down.shape[0] // 2, down.shape[1]), bf16),
         ),
-        in_specs=[whole_spec(pl.ANY)] * 3 + [whole_spec()] * 3 + [whole_spec(pl.ANY), whole_spec()],
-        out_specs=(whole_spec(pl.ANY),) * 3 + (whole_spec(),) * 4,
+        in_specs=[whole_spec(pl.ANY)] * 3 + [whole_spec()] * 3 + [whole_spec(pl.ANY), whole_spec()] + [whole_spec(pl.ANY)] * 2,
+        out_specs=(whole_spec(pl.ANY),) * 3 + (whole_spec(),) * 4 + (whole_spec(pl.ANY),) * 2,
         scratch_shapes=[
             pltpu.VMEM((2, ada_weight.shape[0], ada_weight.shape[1] // 9), bf16),
             pltpu.VMEM(tokens.shape, bf16),
             pltpu.VMEM(qkv.shape, bf16),
             pltpu.VMEM(out.shape, bf16),
+            pltpu.VMEM((up.shape[0] // 2, up.shape[1]), bf16),
+            pltpu.VMEM((down.shape[0] // 2, down.shape[1]), bf16),
             dma((2,)),
             dma((2, 3)),
             dma((2, pieces)),
             dma((2, pieces)),
             dma((2, 2, pieces)),
-            dma((6,)),
+            dma((10,)),
             dma((2,)),
         ],
         compiler_params=pltpu.CompilerParams(
@@ -1927,7 +1992,7 @@
         ),
         cost_estimate=pl.CostEstimate(flops=10**10, bytes_accessed=3 * 10**7, transcendentals=0),
         name="fetch",
-    )(tokens, qkv, out, condition, bias, ids, ada_weight, ada_bias.reshape(1, -1))
+    )(tokens, qkv, out, condition, bias, ids, ada_weight, ada_bias.reshape(1, -1), up, down)
 
 
 def after(value, earlier):
@@ -1982,7 +2047,7 @@
         return jnp.where(home, value, send(value, to_diag))
 
     bias_pack = jnp.concatenate([qv_bias.reshape(-1), up_bias]).reshape(-1, LANES)
-    tokens, qkv_half, out_half, cond_low, bias_half, ids, modulation = fetch(
+    tokens, qkv_half, out_half, cond_low, bias_half, ids, modulation, up_own, down_own = fetch(
         tokens_in,
         qkv_weight.reshape(width, 3 * local_cols),
         out_weight,
@@ -1991,12 +2056,13 @@
         image_ids.reshape(-1, LANES),
         ada_weight,
         ada_bias,
+        up_weight,
+        down_weight,
     )
     bias_half = bias_half.reshape(-1).astype(f32)
     unit_ids = ids[:: SHORT // LANES, 0]
 
-    def over_x(weight, earlier):
-        own = lax.dynamic_slice_in_dim(weight, y * (weight.shape[0] // 2), weight.shape[0] // 2)
+    def over_x(own, earlier):
         return send(after(own, earlier), to_diag)
 
     def over_y(weight, first):
@@ -2006,7 +2072,7 @@
         mine = jnp.arange(2).reshape(2, 1, 1) == y
         return jnp.where(home, halves, jnp.where(mine, first[None], second[None])).reshape(weight.shape)
 
-    up_first = over_x(up_weight, tokens)
+    up_first = over_x(up_own, tokens)
     features = jnp.where(home, enc_features, send(enc_features, to_core))
     qv_half = bias_half[: 2 * local_cols].reshape(2, local_cols)
     up_bias_half = bias_half[2 * local_cols :]
@@ -2051,7 +2117,7 @@
     qkv = (dot_nn(attn_all, qkv_pad) + qkv_bias).astype(bf16)
     qkv, up_first = lax.optimization_barrier((qkv, up_first))
     up_half = over_y(up_weight, up_first)
-    down_first = over_x(down_weight, up_first)
+    down_first = over_x(down_own, up_first)
     attended, log_sums = attend(starts, counts, qkv, heads, out_cols)
     attended, down_first = lax.optimization_barrier((attended, down_first))
     down_half = over_y(down_weight, down_first)
@@ -2076,7 +2142,8 @@
     second_value, second_back = jax.vjp(jax.nn.silu, second_pre)
     second_low = second_value.astype(bf16)
     projected = dot_nn(second_low, proj_last) + proj_last_bias.astype(f32)
-    target_vals = jnp.take(features, rows_low - group * shard_rows, axis=0).astype(f32)
+    chosen = (rows_low - group * shard_rows)[:, None] == jnp.arange(shard_rows, dtype=jnp.int32)[None, :]
+    target_vals = dot_nn(chosen.astype(bf16), features)
     loss_back = jax.vjp(lambda predicted: align_loss(predicted, target_vals), projected)[1]
     grad_projected = loss_back(jnp.ones((), f32))[0]
     grad_last_low = grad_projected.astype(bf16)

time: 679 us -> 667 us (0.982)
  Pallas kernels: 425 us -> 406 us
  starting transfers between devices: 21.1 us -> 39.8 us
  local copies, waits for them, and re-layouts: 47.9 us -> 38 us
    ppermute x13, starting transfers between devices: 21.1 us -> 39.8 us  [send(): return lax.ppermute(value, ('dp', 'tensor'), pairs_of(move))]
    pallas_call x1, Pallas kernels: 111 us -> 125 us  [mlp_back(): pl.pallas_call(functools.partial(mlp_back_kernel, proj_jobs), out_shape=(...]
    pallas_call x1, Pallas kernels: 54.7 us -> 41 us  [attend_back(): pl.pallas_call(functools.partial(attend_back_kernel, heads, together, fac...]
    pallas_call x1, Pallas kernels: 36 us -> 23.7 us  [attend(): pl.pallas_call(functools.partial(attend_kernel, heads, 4, factor), out_sh...]
    dynamic_slice x2 -> x0, local copies, waits for them, and re-layouts: 6.96 us -> none  [over_x(): lax.dynamic_slice_in_dim(weight, y * (weight.shape[0] // 2), weight.shape...]
    pallas_call x1, Pallas kernels: 168 us -> 161 us  [reduce_grads(): pl.pallas_call(functools.partial(reduce_kernel, grid_rows, first_jobs, se...]
    dot_general x9 -> x10, matrix products: 78 us -> 83.2 us  [dot_nn(): return jnp.dot(left, right, preferred_element_type=f32)]
  transfers between devices with their start and end apart: 13 -> 13, of which waited for: 0 -> 0; matrix products, arithmetic and copies ran while one was open for 26% -> 26% of each run, Pallas kernels for 34% -> 32%
where the time goes in v5:
time: 667 us; the launch traced here: 661 us
  Pallas kernels  406 us (61%)
  matrix products  128 us (19%)
  other arithmetic  46.7 us (7%)
  starting transfers between devices  39.8 us (6%)
  local copies, waits for them, and re-layouts  38 us (6%)
    pallas_call x1, Pallas kernels, reduce_grads(): pl.pallas_call(functools.partial(reduce_kernel, grid_rows, first_jobs, se...  161 us
    pallas_call x1, Pallas kernels, mlp_back(): pl.pallas_call(functools.partial(mlp_back_kernel, proj_jobs), out_shape=(...  125 us
    dot_general x10, matrix products, dot_nn(): return jnp.dot(left, right, preferred_element_type=f32)  83.2 us
    dot_general x6, matrix products, dot_nt(): lax.dot_general(left_arg, right_arg, (((1,), (1,)), ((), ())), preferred_...  41.6 us
    pallas_call x1, Pallas kernels, attend_back(): pl.pallas_call(functools.partial(attend_back_kernel, heads, together, fac...  41 us
    ppermute x13, starting transfers between devices, send(): return lax.ppermute(value, ('dp', 'tensor'), pairs_of(move))  39.8 us
    pallas_call x3, Pallas kernels, gather_cores(): pl.pallas_call(gather_kernel, out_shape=jax.ShapeDtypeStruct((2, rows, wi...  28.3 us
    pallas_call x1, Pallas kernels, fetch(): pl.pallas_call(fetch_kernel, out_shape=(jax.ShapeDtypeStruct(tokens.shape...  27 us
  transfers between devices with their start and end apart: 13, of which 0 were waited for; matrix products, arithmetic and copies ran while one was open for 26% of the time, Pallas kernels for 32%

profile of v5, /device:TPU:0, one launch (start us, length us, event | category | flops | bytes accessed | tf_op | source)
XLA Modules:
  0.0 661.1 jit_solution(3413919304905773291)
XLA Ops:
  0.7 6.6 copy.67.qkv_ref
  8.6 27.0 %fetch.1 = (bf16[768,1152]{1,0:T(8,128)(2,1)}, bf16[1152,1728]{1,0:T(8,128)(2,1)}, bf16[576,1152]{1,0:T(8,128)(2,1)}, bf16[6,1152]{1,0:T(8,128)(2,1)}, bf16[27,1...) custom-call(bf16[768,1152]{1,0:T(8,128)(2,1)} %tokens_ref.1, ...), custom_call_target="tpu_custom_call" | custom-call | flops 10000000000 | bytes 30000000 | tf_op jit(solution)/shard_map/fetch/pallas_call | solution.py:1960
  45.1 20.8 %gather_cores.3 = bf16[2,768,1152]{2,1,0:T(8,128)(2,1)S(1)} custom-call(bf16[768,1152]{1,0:T(8,128)(2,1)S(1)} %fusion.17.own_ref), custom_call_target="tpu_custom_call" | custom-call | bytes 12000000 | tf_op jit(solution)/shard_map/gather_cores/pallas_call | solution.py:535
  67.8 11.7 %add_convert_fusion.qkv_ref = bf16[1536,1792]{1,0:T(8,128)(2,1)} fusion(bf16[1536,1152]{1,0:T(8,128)(2,1)} %bitcast.169, f32[1792]{0:T(1024)S(1)} %concatenate.13, bf16[1152,1728]{1,0:T(8,128)(2,1)} %get-tuple-element.62), kind=kOutput, calls=%fused_computation.10 | convolution fusion | flops 6347292672 | bytes 13032448 | tf_op jit(solution)/shard_map/dot_general | solution.py:2105
  87.6 23.7 %attend.1 = (bf16[1536,768]{1,0:T(8,128)(2,1)S(1)}, f32[48,1,256]{2,1,0:T(1,128)S(1)}) custom-call(s32[6]{0:T(128)S(1)} %get-tuple-element.61.starts, s32[6]{0:T(128)S(1)} %fusion.64.counts, bf16[1536,1792]{1,0:T(8,128)(2,1)S(1)} %copy-done.10), custom_call_target="tpu_custom_call" | custom-call | flops 20000000000 | bytes 13000000 | tf_op jit(solution)/shard_map/attend/pallas_call | solution.py:611
  114.3 8.3 %collective-permute-start.2 = (bf16[768,1152]{1,0:T(8,128)(2,1)}, bf16[768,1152]{1,0:T(8,128)(2,1)}, u32[]{:S(2)}, u32[]{:S(2)}) collective-permute-start(bf16[768,1152]{1,0:T(8,128)(2,1)} %convolution_convert_fusion.3), channel_id=1, source_target_pairs={{0,2},{1,3},{2,0},{3,1},{4,6},{5,7},{6,4},{7,5},{8,10},{9,11},{10,... | collective-permute-start | bytes 5308424 | tf_op jit(solution)/shard_map/ppermute | solution.py:471
  125.4 7.2 %fusion.13.up_ref = bf16[1152,2304]{1,0:T(8,128)(2,1)} fusion(bf16[1152,2304]{1,0:T(8,128)(2,1)} %up_ref.1, pred[1152]{0:T(1024)(128)(4,1)S(1)} %broadcast_in_dim.120, pred[]{:T(512)S(6)} %eq.64, bf16[576,2304]{1,0:T(8,128)(2,1)} %collective-permute-done.3, bf16[576,2304]{1,0:T(8,128)(2,1)} %collective-permute-done), kind=kLoop, calls=%fused_computation.24 | loop fusion | flops 5308416 | bytes 15926401 | tf_op jit(solution)/shard_map/jit(_where)/select_n | solution.py:2073
  132.6 6.3 fusion.91
  144.5 15.6 %fusion.7 = (bf16[1536,2304]{1,0:T(8,128)(2,1)}, f32[1536,2304]{1,0:T(8,128)}) fusion(f32[2304]{0:T(1024)S(1)} %slice_bitcast_fusion.4, bf16[1536,1152]{1,0:T(8,128)(2,1)S(1)} %bitcast.171, bf16[1152,2304]{1,0:T(8,128)(2,1)S(1)} %bitcast.183), kind=kOutput, calls=%fused_computation.8 | convolution fusion | flops 8189116416 | bytes 30090240 | tf_op jit(solution)/shard_map/dot_general | solution.py:2105
  160.0 7.6 %fusion.12.down_ref = bf16[2304,1152]{1,0:T(8,128)(2,1)} fusion(bf16[2304,1152]{1,0:T(8,128)(2,1)} %down_ref.1, pred[2304]{0:T(1024)(128)(4,1)S(1)} %broadcast_in_dim.127, pred[]{:T(512)S(6)} %eq.64, bf16[1152,1152]{1,0:T(8,128)(2,1)} %collective-permute-done.4, bf16[1152,1152]{1,0:T(8,128)(2,1)} %collective-permute-done.1), kind=kLoop, calls=%fused_computation.22 | loop fusion | flops 5308416 | bytes 15927553 | tf_op jit(solution)/shard_map/jit(_where)/select_n | solution.py:2073
  167.7 9.6 %fusion.31 = bf16[768,1152]{1,0:T(8,128)(2,1)} fusion(bf16[2304,1152]{1,0:T(8,128)(2,1)} %fusion.12.down_ref, bf16[1536,2304]{1,0:T(8,128)(2,1)} %get-tuple-element.180.one_right, s32[]{:T(128)S(6)} %select_n.113), kind=kOutput, calls=%fused_computation.62 | convolution fusion | flops 4077748224 | bytes 10616836 | tf_op jit(solution)/shard_map/dot_general | solution.py:2105
  180.1 5.4 multiply_reduce_fusion.9
  188.6 11.8 %fusion.19 = (bf16[768,1152]{1,0:T(8,128)(2,1)S(1)}, f32[768,1152]{1,0:T(8,128)}) fusion(f32[768,1152]{1,0:T(8,128)} %copy-done.11, f32[3,1152]{1,0:T(4,128)S(1)} %get-tuple-element.163, f32[1152]{0:T(1024)S(1)} %convert_element_type.164, bf16[768,1152]{1,0:T(8,128)(2,1)} %collective-permute-done.5, bf16[2304,1152]{1,0:T(8,128)(2,1)} %fusion.12.down_ref, ...), kind=kOutput, calls=%fused_computation.39 | convolution fusion | flops 4083941376 | bytes 19482628 | tf_op jit(solution)/shard_map/dot_general | solution.py:2105
  200.4 9.9 %multiply_convert_fusion.1 = (bf16[768,2048]{1,0:T(8,128)(2,1)S(1)}, f32[768,2048]{1,0:T(8,128)}) fusion(f32[2048]{0:T(1024)S(1)} %convert_element_type.167, bf16[768,1152]{1,0:T(8,128)(2,1)S(1)} %get-tuple-element.182.in_right, bf16[1152,2048]{1,0:T(8,128)(2,1)} %param.34), kind=kOutput, calls=%fused_computation.19 | convolution fusion | flops 3633315840 | bytes 15933440 | tf_op jit(solution)/shard_map/dot_general | solution.py:2105
  210.3 7.4 %multiply_convert_fusion = (bf16[768,2048]{1,0:T(8,128)(2,1)S(1)}, f32[768,2048]{1,0:T(8,128)S(1)}) fusion(f32[2048]{0:T(1024)S(1)} %convert_element_type.169, bf16[768,2048]{1,0:T(8,128)(2,1)S(1)} %get-tuple-element.184.mid_right, bf16[2048,2048]{1,0:T(8,128)(2,1)S(1)} %bitcast.207), kind=kOutput, calls=%fused_computation.17 | convolution fusion | flops 6451888128 | bytes 20979712 | tf_op jit(solution)/shard_map/dot_general | solution.py:2105
  221.3 5.7 fusion.87
  227.0 13.5 %fusion.89 = (f32[2048]{0:T(1024)S(1)}, bf16[768,2048]{1,0:T(8,128)(2,1)S(1)}) fusion(f32[768,2048]{1,0:T(8,128)} %get-tuple-element.185, f32[2048]{0:T(1024)S(1)} %convert_element_type.167, bf16[768,2048]{1,0:T(8,128)(2,1)} %get-tuple-element.150.mid_left, bf16[2048,2048]{1,0:T(8,128)(2,1)} %param.36), kind=kOutput, calls=%fused_computation.191 | convolution fusion | flops 6461323264 | bytes 20987904 | tf_op jit(solution)/shard_map/dot_general | solution.py:21
  248.1 125.3 %mlp_back.1 = (bf16[1536,1152]{1,0:T(8,128)(2,1)}, bf16[1536,2304]{1,0:T(8,128)(2,1)}, f32[768,1152]{1,0:T(8,128)}, f32[8,2304]{1,0:T(8,128)}, f32[17,64,256]{2,1,0:T(8,128)}) custom-call(bf16[768,1152]{1,0:T(8,128)(2,1)} %fusion.37.own_ref, f32[1536,2304]{1,0:T(8,128)} %get-tuple-element.181.pre_ref, bf16[2304,1152]{1,0:T(8,128)(2,1)} %fusion.12.down_ref, ...), custom_call_target="tpu_custom_call" | custom-call | flops 30000001024 | bytes 50000000 | tf_op jit(solution)/shard_map/mlp_back/pallas_call | solution.py:1712
  389.7 41.0 %attend_back.1 = (bf16[1536,1792]{1,0:T(8,128)(2,1)}, f32[8,576]{1,0:T(8,128)S(1)}) custom-call(s32[6]{0:T(128)S(1)} %copy-done.7, s32[6]{0:T(128)S(1)} %copy-done.9, bf16[1536,1792]{1,0:T(8,128)(2,1)} %add_convert_fusion.qkv_ref, f32[48,1,256]{2,1,0:T(1,128)S(1)} %get-tuple-element.83.log_ref, bf16[1536,768]{1,0:T(8,128)(2,1)S(1)} %convolution_convert_fusion.2.grad_ref), custom_call_target="tpu_custom_call" | custom-call | flops 40000000000 | bytes 25000000 | tf_op jit(solution)/shard_map/attend_back/pallas_call | solution.py:698
  430.8 6.7 %convolution_convert_fusion = bf16[768,1152]{1,0:T(8,128)(2,1)} fusion(bf16[1152,1728]{1,0:T(8,128)(2,1)S(1)} %copy-done.26, bf16[1536,1792]{1,0:T(8,128)(2,1)} %get-tuple-element.84.three_right, s32[]{:T(128)S(6)} %select_n.113), kind=kOutput, calls=%fused_computation.63 | convolution fusion | flops 3171778560 | bytes 8503300 | tf_op jit(solution)/shard_map/dot_general | solution.py:21
  447.2 7.8 %fusion.41 = (f32[768]{0:T(1024)S(1)}, f32[768]{0:T(1024)S(1)}, f32[768,1152]{1,0:T(8,128)S(1)}) fusion(f32[3,1152]{1,0:T(4,128)S(1)} %copy-done.37, f32[768]{0:T(1024)S(1)} %copy-done.45, f32[768]{0:T(1024)S(1)} %copy-done.41, bf16[768,1152]{1,0:T(8,128)(2,1)S(1)} %copy-done.14, bf16[768,1152]{1,0:T(8,128)(2,1)} %collective-permute-done.10, ...), kind=kOutput, calls=%fused_computation.78 | convolution fusion | flops 3180624384 | bytes 13985284 | tf_op jit(solution)/shard_map/dot_general | solution.py:21
  455.0 5.2 multiply_reduce_fusion.1
  460.6 15.5 %collective-permute-start.12 = (f32[6,6912]{1,0:T(8,128)S(1)}, f32[6,6912]{1,0:T(8,128)S(1)}, u32[]{:S(2)}, u32[]{:S(2)}) collective-permute-start(f32[6,6912]{1,0:T(8,128)S(1)} %fusion.74), channel_id=1, source_target_pairs={{0,2},{1,3},{2,0},{3,1},{4,6},{5,7},{6,4},{7,5},{8,10},{9,11},{10,... | collective-permute-start | bytes 497672 | tf_op jit(solution)/shard_map/ppermute | solution.py:471
  482.5 160.9 %reduce_grads.1 = (f32[18,144,128]{2,1,0:T(8,128)}, f32[10,144,128]{2,1,0:T(8,128)S(1)}, f32[112,128]{1,0:T(8,128)S(1)}, f32[4,2,2,8,256]{4,3,2,1,0:T(8,128)S(1)...) custom-call(bf16[1536,1152]{1,0:T(8,128)(2,1)} %get-tuple-element.85.one_left, ...), custom_call_target="tpu_custom_call" | custom-call | flops 99999997952 | bytes 100000000 | tf_op jit(solution)/shard_map/reduce_grads/pallas_call | solution.py:1328
  (289 shorter events, 98.3 us)
Async XLA Ops:
  0.7 217.1 %copy-start = (bf16[2048,768]{1,0:T(8,128)(2,1)S(1)}, bf16[2048,768]{1,0:T(8,128)(2,1)}, u32[]{:S(2)}) copy-start(bf16[2048,768]{1,0:T(8,128)(2,1)} %param.38) | copy-start | bytes 9437188
  35.7 43.8 %collective-permute-start = (bf16[576,2304]{1,0:T(8,128)(2,1)}, bf16[576,2304]{1,0:T(8,128)(2,1)}, u32[]{:S(2)}, u32[]{:S(2)}) collective-permute-start(bf16[576,2304]{1,0:T(8,128)(2,1)} %get-tuple-element.65), channel_id=1, source_target_pairs={{1,2},{2,1},{5,6},{6,5},{9,10},{10,9},{13,14},{14,13},{17,18},{18,... | collective-permute-start | bytes 7962632 | tf_op jit(solution)/shard_map/ppermute | solution.py:471
  41.9 23.9 %copy-start.36 = (f32[3,1152]{1,0:T(4,128)}, f32[3,1152]{1,0:T(4,128)S(1)}, u32[]{:S(2)}) copy-start(f32[3,1152]{1,0:T(4,128)S(1)} %get-tuple-element.167) | copy-start | bytes 41476
  42.0 90.7 %copy-start.32 = (f32[3,1152]{1,0:T(4,128)}, f32[3,1152]{1,0:T(4,128)S(1)}, u32[]{:S(2)}) copy-start(f32[3,1152]{1,0:T(4,128)S(1)} %get-tuple-element.168) | copy-start | bytes 41476
  42.0 97.5 %copy-start.34 = (f32[3,1152]{1,0:T(4,128)}, f32[3,1152]{1,0:T(4,128)S(1)}, u32[]{:S(2)}) copy-start(f32[3,1152]{1,0:T(4,128)S(1)} %get-tuple-element.165) | copy-start | bytes 41476
  42.0 23.9 %copy-start.40 = (f32[768]{0:T(1024)}, f32[768]{0:T(1024)S(1)}, u32[]{:S(2)}) copy-start(f32[768]{0:T(1024)S(1)} %broadcast_multiply_fusion.5) | copy-start | bytes 9220
  79.5 31.8 %collective-permute-start.1 = (bf16[1152,1152]{1,0:T(8,128)(2,1)}, bf16[1152,1152]{1,0:T(8,128)(2,1)}, u32[]{:S(2)}, u32[]{:S(2)}) collective-permute-start(bf16[1152,1152]{1,0:T(8,128)(2,1)} %get-tuple-element.70), channel_id=1, source_target_pairs={{1,2},{2,1},{5,6},{6,5},{9,10},{10,9},{13,14},{14,13},{17,18},{18,... | collective-permute-start | bytes 7962632 | tf_op jit(solution)/shard_map/ppermute | solution.py:471
  82.0 29.4 %copy-start.8 = (s32[6]{0:T(128)}, s32[6]{0:T(128)S(1)}, u32[]{:S(2)}) copy-start(s32[6]{0:T(128)S(1)} %fusion.64.counts) | copy-start | bytes 76
  82.7 28.7 %copy-start.6 = (s32[6]{0:T(128)}, s32[6]{0:T(128)S(1)}, u32[]{:S(2)}) copy-start(s32[6]{0:T(128)S(1)} %get-tuple-element.61.starts) | copy-start | bytes 76
  82.7 40.2 %collective-permute-start.3 = (bf16[576,2304]{1,0:T(8,128)(2,1)}, bf16[576,2304]{1,0:T(8,128)(2,1)}, u32[]{:S(2)}, u32[]{:S(2)}) collective-permute-start(bf16[576,2304]{1,0:T(8,128)(2,1)} %collective-permute-done), channel_id=1, source_target_pairs={{1,5},{2,6},{5,1},{6,2},{9,13},{10,14},{13,9},{14,10},{17,21},{18,... | collective-permute-start | bytes 7962632 | tf_op jit(solution)/shard_map/ppermute | solution.py:471
  114.3 18.3 %collective-permute-start.2 = (bf16[768,1152]{1,0:T(8,128)(2,1)}, bf16[768,1152]{1,0:T(8,128)(2,1)}, u32[]{:S(2)}, u32[]{:S(2)}) collective-permute-start(bf16[768,1152]{1,0:T(8,128)(2,1)} %convolution_convert_fusion.3), channel_id=1, source_target_pairs={{0,2},{1,3},{2,0},{3,1},{4,6},{5,7},{6,4},{7,5},{8,10},{9,11},{10,... | collective-permute-start | bytes 5308424 | tf_op jit(solution)/shard_map/ppermute | solution.py:471
  122.6 57.5 %collective-permute-start.9 = (bf16[1536,768]{1,0:T(8,128)(2,1)}, bf16[1536,768]{1,0:T(8,128)(2,1)}, u32[]{:S(2)}, u32[]{:S(2)}) collective-permute-start(bf16[1536,768]{1,0:T(8,128)(2,1)} %param.40), channel_id=1, source_target_pairs={{0,2},{1,3},{2,0},{3,1},{4,6},{5,7},{6,4},{7,5},{8,10},{9,11},{10,... | collective-permute-start | bytes 7077896 | tf_op jit(solution)/shard_map/ppermute | solution.py:471
  122.9 37.2 %collective-permute-start.4 = (bf16[1152,1152]{1,0:T(8,128)(2,1)}, bf16[1152,1152]{1,0:T(8,128)(2,1)}, u32[]{:S(2)}, u32[]{:S(2)}) collective-permute-start(bf16[1152,1152]{1,0:T(8,128)(2,1)} %collective-permute-done.1), channel_id=1, source_target_pairs={{1,5},{2,6},{5,1},{6,2},{9,13},{10,14},{13,9},{14,10},{17,21},{18,... | collective-permute-start | bytes 7962632 | tf_op jit(solution)/shard_map/ppermute | solution.py:471
  177.3 11.3 %collective-permute-start.5 = (bf16[768,1152]{1,0:T(8,128)(2,1)}, bf16[768,1152]{1,0:T(8,128)(2,1)}, u32[]{:S(2)}, u32[]{:S(2)}) collective-permute-start(bf16[768,1152]{1,0:T(8,128)(2,1)} %fusion.31), channel_id=1, source_target_pairs={{0,2},{1,3},{2,0},{3,1},{4,6},{5,7},{6,4},{7,5},{8,10},{9,11},{10,... | collective-permute-start | bytes 5308424 | tf_op jit(solution)/shard_map/ppermute | solution.py:471
  177.3 2.8 collective-permute-start.8
  178.2 62.3 %collective-permute-start.7 = (bf16[768,1152]{1,0:T(8,128)(2,1)}, bf16[768,1152]{1,0:T(8,128)(2,1)}, u32[]{:S(2)}, u32[]{:S(2)}) collective-permute-start(bf16[768,1152]{1,0:T(8,128)(2,1)} %param.43), channel_id=1, source_target_pairs={{1,2},{2,1},{5,6},{6,5},{9,10},{10,9},{13,14},{14,13},{17,18},{18,... | collective-permute-start | bytes 5308424 | tf_op jit(solution)/shard_map/ppermute | solution.py:471
  248.1 125.3 %copy-start.35 = (f32[3,1152]{1,0:T(4,128)S(1)}, f32[3,1152]{1,0:T(4,128)}, u32[]{:S(2)}) copy-start(f32[3,1152]{1,0:T(4,128)} %copy-done.34) | copy-start | bytes 41476
  248.1 125.3 %copy-start.39 = (f32[768]{0:T(1024)S(1)}, f32[768]{0:T(1024)}, u32[]{:S(2)}) copy-start(f32[768]{0:T(1024)} %copy-done.38) | copy-start | bytes 9220
  248.1 125.4 %copy-start.43 = (f32[768]{0:T(1024)S(1)}, f32[768]{0:T(1024)}, u32[]{:S(2)}) copy-start(f32[768]{0:T(1024)} %copy-done.42) | copy-start | bytes 9220
  389.7 41.1 %copy-start.26 = (bf16[1152,1728]{1,0:T(8,128)(2,1)S(1)}, bf16[1152,1728]{1,0:T(8,128)(2,1)}, u32[]{:S(2)}) copy-start(bf16[1152,1728]{1,0:T(8,128)(2,1)} %get-tuple-element.62) | copy-start | bytes 11943940
  437.5 9.6 %collective-permute-start.10 = (bf16[768,1152]{1,0:T(8,128)(2,1)}, bf16[768,1152]{1,0:T(8,128)(2,1)}, u32[]{:S(2)}, u32[]{:S(2)}) collective-permute-start(bf16[768,1152]{1,0:T(8,128)(2,1)} %convolution_convert_fusion), channel_id=1, source_target_pairs={{0,2},{1,3},{2,0},{3,1},{4,6},{5,7},{6,4},{7,5},{8,10},{9,11},{10,... | collective-permute-start | bytes 5308424 | tf_op jit(solution)/shard_map/ppermute | solution.py:471
  437.8 42.7 %collective-permute-start.6 = (bf16[768,1152]{1,0:T(8,128)(2,1)}, bf16[768,1152]{1,0:T(8,128)(2,1)}, u32[]{:S(2)}, u32[]{:S(2)}) collective-permute-start(bf16[768,1152]{1,0:T(8,128)(2,1)} %copy-done.24), channel_id=1, source_target_pairs={{1,2},{2,1},{5,6},{6,5},{9,10},{10,9},{13,14},{14,13},{17,18},{18,... | collective-permute-start | bytes 5308424 | tf_op jit(solution)/shard_map/ppermute | solution.py:471
  460.6 21.3 %collective-permute-start.12 = (f32[6,6912]{1,0:T(8,128)S(1)}, f32[6,6912]{1,0:T(8,128)S(1)}, u32[]{:S(2)}, u32[]{:S(2)}) collective-permute-start(f32[6,6912]{1,0:T(8,128)S(1)} %fusion.74), channel_id=1, source_target_pairs={{0,2},{1,3},{2,0},{3,1},{4,6},{5,7},{6,4},{7,5},{8,10},{9,11},{10,... | collective-permute-start | bytes 497672 | tf_op jit(solution)/shard_map/ppermute | solution.py:471
  478.6 178.2 %collective-permute-start.11 = (bf16[768,1152]{1,0:T(8,128)(2,1)}, bf16[768,1152]{1,0:T(8,128)(2,1)}, u32[]{:S(2)}, u32[]{:S(2)}) collective-permute-start(bf16[768,1152]{1,0:T(8,128)(2,1)} %add_convert_fusion.1), channel_id=1, source_target_pairs={{1,2},{2,1},{5,6},{6,5},{9,10},{10,9},{13,14},{14,13},{17,18},{18,... | collective-permute-start | bytes 5308424 | tf_op jit(solution)/shard_map/ppermute | solution.py:471
  (57 other events, 456.9 us)

commit v6 on v5

--- a/solution.py
+++ b/solution.py
@@ -2032,7 +2032,6 @@
     z_far = z // 2
     place = dp * 2 + x
     home = core == x
-    group = (dp // 2) * 2 + x
     local_rows, width = tokens_in.shape
     shard_rows = image_ids.shape[0]
     slots = condition.shape[0]
@@ -2073,7 +2072,8 @@
         return jnp.where(home, halves, jnp.where(mine, first[None], second[None])).reshape(weight.shape)
 
     up_first = over_x(up_own, tokens)
-    features = jnp.where(home, enc_features, send(enc_features, to_core))
+    chosen = (target_rows - dp * shard_rows)[:, None] == jnp.arange(shard_rows, dtype=jnp.int32)[None, :]
+    target_low = jnp.dot(chosen.astype(bf16), enc_features, preferred_element_type=f32).astype(bf16)
     qv_half = bias_half[: 2 * local_cols].reshape(2, local_cols)
     up_bias_half = bias_half[2 * local_cols :]
 
@@ -2121,7 +2121,7 @@
     attended, log_sums = attend(starts, counts, qkv, heads, out_cols)
     attended, down_first = lax.optimization_barrier((attended, down_first))
     down_half = over_y(down_weight, down_first)
-    rows_low = swap(after(target_rows, down_first))
+    target_vals = swap(after(target_low, down_first)).astype(f32)
     grad_out = swap(after(out_grad, down_first))
     attn_branch = by_unit(reduce_cores(attended, out_pad, dot_nn) + out_bias.astype(f32))
     mid = resid + gate_one * attn_branch
@@ -2142,8 +2142,6 @@
     second_value, second_back = jax.vjp(jax.nn.silu, second_pre)
     second_low = second_value.astype(bf16)
     projected = dot_nn(second_low, proj_last) + proj_last_bias.astype(f32)
-    chosen = (rows_low - group * shard_rows)[:, None] == jnp.arange(shard_rows, dtype=jnp.int32)[None, :]
-    target_vals = dot_nn(chosen.astype(bf16), features)
     loss_back = jax.vjp(lambda predicted: align_loss(predicted, target_vals), projected)[1]
     grad_projected = loss_back(jnp.ones((), f32))[0]
     grad_last_low = grad_projected.astype(bf16)

time: 667 us -> 659 us (0.988)
  starting transfers between devices: 39.8 us -> 24.6 us
  Pallas kernels: 406 us -> 418 us
    ppermute x13 -> x12, starting transfers between devices: 39.8 us -> 24.6 us  [send(): return lax.ppermute(value, ('dp', 'tensor'), pairs_of(move))]
    pallas_call x1, Pallas kernels: 41 us -> 54.8 us  [attend_back(): pl.pallas_call(functools.partial(attend_back_kernel, heads, together, fac...]
    pallas_call x1, Pallas kernels: 23.7 us -> 36 us  [attend(): pl.pallas_call(functools.partial(attend_kernel, heads, 4, factor), out_sh...]
    pallas_call x1, Pallas kernels: 125 us -> 114 us  [mlp_back(): pl.pallas_call(functools.partial(mlp_back_kernel, proj_jobs), out_shape=(...]
    dot_general x10 -> x9, matrix products: 83.2 us -> 74.7 us  [dot_nn(): return jnp.dot(left, right, preferred_element_type=f32)]
    unnamed x155 -> x161, local copies, waits for them, and re-layouts: 13.6 us -> 13.8 us
  transfers between devices with their start and end apart: 13 -> 12, of which waited for: 0 -> 0; matrix products, arithmetic and copies ran while one was open for 26% -> 22% of each run, Pallas kernels for 32% -> 34%
where the time goes in v6:
time: 659 us; the launch traced here: 650 us
  Pallas kernels  418 us (63%)
  matrix products  123 us (19%)
  other arithmetic  46.6 us (7%)
  local copies, waits for them, and re-layouts  35 us (5%)
  starting transfers between devices  24.6 us (4%)
    pallas_call x1, Pallas kernels, reduce_grads(): pl.pallas_call(functools.partial(reduce_kernel, grid_rows, first_jobs, se...  158 us
    pallas_call x1, Pallas kernels, mlp_back(): pl.pallas_call(functools.partial(mlp_back_kernel, proj_jobs), out_shape=(...  114 us
    dot_general x9, matrix products, dot_nn(): return jnp.dot(left, right, preferred_element_type=f32)  74.7 us
    pallas_call x1, Pallas kernels, attend_back(): pl.pallas_call(functools.partial(attend_back_kernel, heads, together, fac...  54.8 us
    dot_general x6, matrix products, dot_nt(): lax.dot_general(left_arg, right_arg, (((1,), (1,)), ((), ())), preferred_...  41.5 us
    pallas_call x1, Pallas kernels, attend(): pl.pallas_call(functools.partial(attend_kernel, heads, 4, factor), out_sh...  36 us
    pallas_call x3, Pallas kernels, gather_cores(): pl.pallas_call(gather_kernel, out_shape=jax.ShapeDtypeStruct((2, rows, wi...  28.4 us
    pallas_call x1, Pallas kernels, fetch(): pl.pallas_call(fetch_kernel, out_shape=(jax.ShapeDtypeStruct(tokens.shape...  26.9 us
  transfers between devices with their start and end apart: 12, of which 0 were waited for; matrix products, arithmetic and copies ran while one was open for 22% of the time, Pallas kernels for 34%

profile of v6, /device:TPU:0, one launch (start us, length us, event | category | flops | bytes accessed | tf_op | source)
XLA Modules:
  0.0 649.7 jit_solution(16966455266753613118)
XLA Ops:
  0.7 6.6 %copy.63.qkv_ref = bf16[1152,1728]{1,0:T(8,128)(2,1)} copy(bf16[1152,1728]{0,1:T(8,128)(2,1)} %bitcast.187) | data formatting | bytes 7962624 | tf_op jit(solution)/shard_map/reshape | solution.py:2051
  8.6 26.9 %fetch.1 = (bf16[768,1152]{1,0:T(8,128)(2,1)}, bf16[1152,1728]{1,0:T(8,128)(2,1)}, bf16[576,1152]{1,0:T(8,128)(2,1)}, bf16[6,1152]{1,0:T(8,128)(2,1)}, bf16[27,1...) custom-call(bf16[768,1152]{1,0:T(8,128)(2,1)} %tokens_ref.1, ...), custom_call_target="tpu_custom_call" | custom-call | flops 10000000000 | bytes 30000000 | tf_op jit(solution)/shard_map/fetch/pallas_call | solution.py:1960
  44.9 21.0 %gather_cores.3 = bf16[2,768,1152]{2,1,0:T(8,128)(2,1)S(1)} custom-call(bf16[768,1152]{1,0:T(8,128)(2,1)S(1)} %fusion.17.own_ref), custom_call_target="tpu_custom_call" | custom-call | bytes 12000000 | tf_op jit(solution)/shard_map/gather_cores/pallas_call | solution.py:535
  67.8 11.7 %add_convert_fusion.qkv_ref = bf16[1536,1792]{1,0:T(8,128)(2,1)} fusion(bf16[1536,1152]{1,0:T(8,128)(2,1)} %bitcast.170, f32[1792]{0:T(1024)S(1)} %concatenate.13, bf16[1152,1728]{1,0:T(8,128)(2,1)} %get-tuple-element.62), kind=kOutput, calls=%fused_computation.10 | convolution fusion | flops 6347292672 | bytes 13032448 | tf_op jit(solution)/shard_map/dot_general | solution.py:2105
  87.7 36.0 %attend.1 = (bf16[1536,768]{1,0:T(8,128)(2,1)S(1)}, f32[48,1,256]{2,1,0:T(1,128)S(1)}) custom-call(s32[6]{0:T(128)S(1)} %get-tuple-element.61.starts, s32[6]{0:T(128)S(1)} %fusion.66.counts, bf16[1536,1792]{1,0:T(8,128)(2,1)S(1)} %copy-done.10), custom_call_target="tpu_custom_call" | custom-call | flops 20000000000 | bytes 13000000 | tf_op jit(solution)/shard_map/attend/pallas_call | solution.py:611
  126.7 8.2 %collective-permute-start.2 = (bf16[768,1152]{1,0:T(8,128)(2,1)}, bf16[768,1152]{1,0:T(8,128)(2,1)}, u32[]{:S(2)}, u32[]{:S(2)}) collective-permute-start(bf16[768,1152]{1,0:T(8,128)(2,1)} %convolution_convert_fusion.3), channel_id=1, source_target_pairs={{0,2},{1,3},{2,0},{3,1},{4,6},{5,7},{6,4},{7,5},{8,10},{9,11},{10,... | collective-permute-start | bytes 5308424 | tf_op jit(solution)/shard_map/ppermute | solution.py:471
  137.4 7.1 %fusion.13.up_ref = bf16[1152,2304]{1,0:T(8,128)(2,1)} fusion(bf16[1152,2304]{1,0:T(8,128)(2,1)} %up_ref.1, pred[1152]{0:T(1024)(128)(4,1)S(1)} %broadcast_in_dim.120, pred[]{:T(512)S(6)} %eq.64, bf16[576,2304]{1,0:T(8,128)(2,1)} %collective-permute-done.3, bf16[576,2304]{1,0:T(8,128)(2,1)} %collective-permute-done), kind=kLoop, calls=%fused_computation.24 | loop fusion | flops 5308416 | bytes 15926401 | tf_op jit(solution)/shard_map/jit(_where)/select_n | solution.py:2072
  144.5 6.2 fusion.93
  156.4 15.6 %fusion.7 = (bf16[1536,2304]{1,0:T(8,128)(2,1)}, f32[1536,2304]{1,0:T(8,128)}) fusion(f32[2304]{0:T(1024)S(1)} %slice_bitcast_fusion.4, bf16[1536,1152]{1,0:T(8,128)(2,1)S(1)} %bitcast.172, bf16[1152,2304]{1,0:T(8,128)(2,1)S(1)} %bitcast.184), kind=kOutput, calls=%fused_computation.8 | convolution fusion | flops 8189116416 | bytes 30090240 | tf_op jit(solution)/shard_map/dot_general | solution.py:2105
  172.0 7.6 %fusion.12.down_ref = bf16[2304,1152]{1,0:T(8,128)(2,1)} fusion(bf16[2304,1152]{1,0:T(8,128)(2,1)} %down_ref.1, pred[2304]{0:T(1024)(128)(4,1)S(1)} %broadcast_in_dim.127, pred[]{:T(512)S(6)} %eq.64, bf16[1152,1152]{1,0:T(8,128)(2,1)} %collective-permute-done.4, bf16[1152,1152]{1,0:T(8,128)(2,1)} %collective-permute-done.1), kind=kLoop, calls=%fused_computation.22 | loop fusion | flops 5308416 | bytes 15927553 | tf_op jit(solution)/shard_map/jit(_where)/select_n | solution.py:2072
  179.7 9.6 %fusion.31 = bf16[768,1152]{1,0:T(8,128)(2,1)} fusion(bf16[2304,1152]{1,0:T(8,128)(2,1)} %fusion.12.down_ref, bf16[1536,2304]{1,0:T(8,128)(2,1)} %get-tuple-element.182.one_right, s32[]{:T(128)S(6)} %select_n.104), kind=kOutput, calls=%fused_computation.65 | convolution fusion | flops 4077748224 | bytes 10616836 | tf_op jit(solution)/shard_map/dot_general | solution.py:2105
  196.4 9.4 %fusion.19 = (bf16[768,1152]{1,0:T(8,128)(2,1)S(1)}, f32[768,1152]{1,0:T(8,128)}) fusion(f32[768,1152]{1,0:T(8,128)S(1)} %copy-done.12, f32[3,1152]{1,0:T(4,128)S(1)} %get-tuple-element.165, f32[1152]{0:T(1024)S(1)} %convert_element_type.170, bf16[768,1152]{1,0:T(8,128)(2,1)} %collective-permute-done.5, bf16[2304,1152]{1,0:T(8,128)(2,1)S(1)} %copy-done.22, ...), kind=kOutput, calls=%fused_computation.39 | convolution fusion | flops 4083941376 | bytes 19482628 | tf_op jit(solution)/shard_map/dot_general | solution.py:2105
  205.8 6.9 %multiply_convert_fusion.1 = (bf16[768,2048]{1,0:T(8,128)(2,1)S(1)}, f32[768,2048]{1,0:T(8,128)}) fusion(f32[2048]{0:T(1024)S(1)} %convert_element_type.173, bf16[768,1152]{1,0:T(8,128)(2,1)S(1)} %get-tuple-element.184.in_right, bf16[1152,2048]{1,0:T(8,128)(2,1)S(1)} %bitcast.186), kind=kOutput, calls=%fused_computation.19 | convolution fusion | flops 3633315840 | bytes 15933440 | tf_op jit(solution)/shard_map/dot_general | solution.py:2105
  212.7 9.2 %multiply_convert_fusion = (bf16[768,2048]{1,0:T(8,128)(2,1)S(1)}, f32[768,2048]{1,0:T(8,128)}) fusion(f32[2048]{0:T(1024)S(1)} %convert_element_type.175, bf16[768,2048]{1,0:T(8,128)(2,1)S(1)} %get-tuple-element.186.mid_right, bf16[2048,2048]{1,0:T(8,128)(2,1)S(1)} %bitcast.208), kind=kOutput, calls=%fused_computation.17 | convolution fusion | flops 6451888128 | bytes 20979712 | tf_op jit(solution)/shard_map/dot_general | solution.py:2105
  225.9 5.6 fusion.89
  231.5 13.5 %fusion.91 = (f32[2048]{0:T(1024)S(1)}, bf16[768,2048]{1,0:T(8,128)(2,1)S(1)}) fusion(f32[768,2048]{1,0:T(8,128)} %get-tuple-element.187, f32[2048]{0:T(1024)S(1)} %convert_element_type.173, bf16[768,2048]{1,0:T(8,128)(2,1)} %get-tuple-element.151.mid_left, bf16[2048,2048]{1,0:T(8,128)(2,1)} %param.36), kind=kOutput, calls=%fused_computation.194 | convolution fusion | flops 6461323264 | bytes 20987904 | tf_op jit(solution)/shard_map/dot_general | solution.py:21
  245.1 4.3 fusion.36
  252.6 113.6 %mlp_back.1 = (bf16[1536,1152]{1,0:T(8,128)(2,1)}, bf16[1536,2304]{1,0:T(8,128)(2,1)}, f32[768,1152]{1,0:T(8,128)}, f32[8,2304]{1,0:T(8,128)}, f32[17,64,256]{2,1,0:T(8,128)}) custom-call(bf16[768,1152]{1,0:T(8,128)(2,1)} %fusion.37.own_ref, f32[1536,2304]{1,0:T(8,128)} %get-tuple-element.183.pre_ref, bf16[2304,1152]{1,0:T(8,128)(2,1)} %fusion.12.down_ref, ...), custom_call_target="tpu_custom_call" | custom-call | flops 30000001024 | bytes 50000000 | tf_op jit(solution)/shard_map/mlp_back/pallas_call | solution.py:1712
  366.3 4.2 fusion.42
  382.4 54.8 %attend_back.1 = (bf16[1536,1792]{1,0:T(8,128)(2,1)}, f32[8,576]{1,0:T(8,128)S(1)}) custom-call(s32[6]{0:T(128)S(1)} %copy-done.7, s32[6]{0:T(128)S(1)} %copy-done.9, bf16[1536,1792]{1,0:T(8,128)(2,1)} %add_convert_fusion.qkv_ref, f32[48,1,256]{2,1,0:T(1,128)S(1)} %get-tuple-element.83.log_ref, bf16[1536,768]{1,0:T(8,128)(2,1)S(1)} %convolution_convert_fusion.2.grad_ref), custom_call_target="tpu_custom_call" | custom-call | flops 40000000000 | bytes 25000000 | tf_op jit(solution)/shard_map/attend_back/pallas_call | solution.py:698
  437.3 6.8 %convolution_convert_fusion = bf16[768,1152]{1,0:T(8,128)(2,1)} fusion(bf16[1152,1728]{1,0:T(8,128)(2,1)S(1)} %copy-done.27, bf16[1536,1792]{1,0:T(8,128)(2,1)} %get-tuple-element.84.three_right, s32[]{:T(128)S(6)} %select_n.104), kind=kOutput, calls=%fused_computation.66 | convolution fusion | flops 3171778560 | bytes 8503300 | tf_op jit(solution)/shard_map/dot_general | solution.py:21
  453.7 7.8 %fusion.41 = (f32[768]{0:T(1024)S(1)}, f32[768]{0:T(1024)S(1)}, f32[768,1152]{1,0:T(8,128)S(1)}) fusion(f32[3,1152]{1,0:T(4,128)S(1)} %copy-done.38, f32[768]{0:T(1024)S(1)} %copy-done.46, f32[768]{0:T(1024)S(1)} %copy-done.42, bf16[768,1152]{1,0:T(8,128)(2,1)S(1)} %copy-done.15, bf16[768,1152]{1,0:T(8,128)(2,1)} %collective-permute-done.9, ...), kind=kOutput, calls=%fused_computation.81 | convolution fusion | flops 3180624384 | bytes 13985284 | tf_op jit(solution)/shard_map/dot_general | solution.py:21
  461.5 5.2 multiply_reduce_fusion.1
  474.0 157.9 %reduce_grads.1 = (f32[18,144,128]{2,1,0:T(8,128)}, f32[10,144,128]{2,1,0:T(8,128)S(1)}, f32[112,128]{1,0:T(8,128)S(1)}, f32[4,2,2,8,256]{4,3,2,1,0:T(8,128)S(1)...) custom-call(bf16[1536,1152]{1,0:T(8,128)(2,1)} %get-tuple-element.85.one_left, ...), custom_call_target="tpu_custom_call" | custom-call | flops 99999997952 | bytes 100000000 | tf_op jit(solution)/shard_map/reduce_grads/pallas_call | solution.py:1328
  (293 shorter events, 91.4 us)
Async XLA Ops:
  0.7 221.3 %copy-start = (bf16[2048,768]{1,0:T(8,128)(2,1)S(1)}, bf16[2048,768]{1,0:T(8,128)(2,1)}, u32[]{:S(2)}) copy-start(bf16[2048,768]{1,0:T(8,128)(2,1)} %param.38) | copy-start | bytes 9437188
  35.6 44.0 %collective-permute-start = (bf16[576,2304]{1,0:T(8,128)(2,1)}, bf16[576,2304]{1,0:T(8,128)(2,1)}, u32[]{:S(2)}, u32[]{:S(2)}) collective-permute-start(bf16[576,2304]{1,0:T(8,128)(2,1)} %get-tuple-element.65), channel_id=1, source_target_pairs={{1,2},{2,1},{5,6},{6,5},{9,10},{10,9},{13,14},{14,13},{17,18},{18,... | collective-permute-start | bytes 7962632 | tf_op jit(solution)/shard_map/ppermute | solution.py:471
  41.7 24.1 %copy-start.37 = (f32[3,1152]{1,0:T(4,128)}, f32[3,1152]{1,0:T(4,128)S(1)}, u32[]{:S(2)}) copy-start(f32[3,1152]{1,0:T(4,128)S(1)} %get-tuple-element.169) | copy-start | bytes 41476
  41.7 102.7 %copy-start.33 = (f32[3,1152]{1,0:T(4,128)}, f32[3,1152]{1,0:T(4,128)S(1)}, u32[]{:S(2)}) copy-start(f32[3,1152]{1,0:T(4,128)S(1)} %get-tuple-element.170) | copy-start | bytes 41476
  41.8 109.5 %copy-start.35 = (f32[3,1152]{1,0:T(4,128)}, f32[3,1152]{1,0:T(4,128)S(1)}, u32[]{:S(2)}) copy-start(f32[3,1152]{1,0:T(4,128)S(1)} %get-tuple-element.167) | copy-start | bytes 41476
  41.8 24.1 %copy-start.41 = (f32[768]{0:T(1024)}, f32[768]{0:T(1024)S(1)}, u32[]{:S(2)}) copy-start(f32[768]{0:T(1024)S(1)} %broadcast_multiply_fusion.5) | copy-start | bytes 9220
  79.5 44.3 %collective-permute-start.1 = (bf16[1152,1152]{1,0:T(8,128)(2,1)}, bf16[1152,1152]{1,0:T(8,128)(2,1)}, u32[]{:S(2)}, u32[]{:S(2)}) collective-permute-start(bf16[1152,1152]{1,0:T(8,128)(2,1)} %get-tuple-element.70), channel_id=1, source_target_pairs={{1,2},{2,1},{5,6},{6,5},{9,10},{10,9},{13,14},{14,13},{17,18},{18,... | collective-permute-start | bytes 7962632 | tf_op jit(solution)/shard_map/ppermute | solution.py:471
  82.1 41.7 %copy-start.8 = (s32[6]{0:T(128)}, s32[6]{0:T(128)S(1)}, u32[]{:S(2)}) copy-start(s32[6]{0:T(128)S(1)} %fusion.66.counts) | copy-start | bytes 76
  82.8 41.0 %copy-start.6 = (s32[6]{0:T(128)}, s32[6]{0:T(128)S(1)}, u32[]{:S(2)}) copy-start(s32[6]{0:T(128)S(1)} %get-tuple-element.61.starts) | copy-start | bytes 76
  82.8 52.4 %collective-permute-start.3 = (bf16[576,2304]{1,0:T(8,128)(2,1)}, bf16[576,2304]{1,0:T(8,128)(2,1)}, u32[]{:S(2)}, u32[]{:S(2)}) collective-permute-start(bf16[576,2304]{1,0:T(8,128)(2,1)} %collective-permute-done), channel_id=1, source_target_pairs={{1,5},{2,6},{5,1},{6,2},{9,13},{10,14},{13,9},{14,10},{17,21},{18,... | collective-permute-start | bytes 7962632 | tf_op jit(solution)/shard_map/ppermute | solution.py:471
  87.7 36.1 %copy-start.30 = (bf16[576,1152]{1,0:T(8,128)(2,1)S(1)}, bf16[576,1152]{1,0:T(8,128)(2,1)}, u32[]{:S(2)}) copy-start(bf16[576,1152]{1,0:T(8,128)(2,1)} %get-tuple-element.72) | copy-start | bytes 3981316
  126.7 17.7 %collective-permute-start.2 = (bf16[768,1152]{1,0:T(8,128)(2,1)}, bf16[768,1152]{1,0:T(8,128)(2,1)}, u32[]{:S(2)}, u32[]{:S(2)}) collective-permute-start(bf16[768,1152]{1,0:T(8,128)(2,1)} %convolution_convert_fusion.3), channel_id=1, source_target_pairs={{0,2},{1,3},{2,0},{3,1},{4,6},{5,7},{6,4},{7,5},{8,10},{9,11},{10,... | collective-permute-start | bytes 5308424 | tf_op jit(solution)/shard_map/ppermute | solution.py:471
  135.2 36.8 %collective-permute-start.4 = (bf16[1152,1152]{1,0:T(8,128)(2,1)}, bf16[1152,1152]{1,0:T(8,128)(2,1)}, u32[]{:S(2)}, u32[]{:S(2)}) collective-permute-start(bf16[1152,1152]{1,0:T(8,128)(2,1)} %collective-permute-done.1), channel_id=1, source_target_pairs={{1,5},{2,6},{5,1},{6,2},{9,13},{10,14},{13,9},{14,10},{17,21},{18,... | collective-permute-start | bytes 7962632 | tf_op jit(solution)/shard_map/ppermute | solution.py:471
  189.2 7.1 %collective-permute-start.5 = (bf16[768,1152]{1,0:T(8,128)(2,1)}, bf16[768,1152]{1,0:T(8,128)(2,1)}, u32[]{:S(2)}, u32[]{:S(2)}) collective-permute-start(bf16[768,1152]{1,0:T(8,128)(2,1)} %fusion.31), channel_id=1, source_target_pairs={{0,2},{1,3},{2,0},{3,1},{4,6},{5,7},{6,4},{7,5},{8,10},{9,11},{10,... | collective-permute-start | bytes 5308424 | tf_op jit(solution)/shard_map/ppermute | solution.py:471
  193.3 28.6 %collective-permute-start.8 = (bf16[768,768]{1,0:T(8,128)(2,1)S(1)}, bf16[768,768]{1,0:T(8,128)(2,1)S(1)}, u32[]{:S(2)}, u32[]{:S(2)}) collective-permute-start(bf16[768,768]{1,0:T(8,128)(2,1)S(1)} %fusion.52), channel_id=1, source_target_pairs={{1,2},{2,1},{5,6},{6,5},{9,10},{10,9},{13,14},{14,13},{17,18},{18,... | collective-permute-start | bytes 3538952 | tf_op jit(solution)/shard_map/ppermute | solution.py:471
  194.2 50.8 %collective-permute-start.7 = (bf16[768,1152]{1,0:T(8,128)(2,1)}, bf16[768,1152]{1,0:T(8,128)(2,1)}, u32[]{:S(2)}, u32[]{:S(2)}) collective-permute-start(bf16[768,1152]{1,0:T(8,128)(2,1)} %param.43), channel_id=1, source_target_pairs={{1,2},{2,1},{5,6},{6,5},{9,10},{10,9},{13,14},{14,13},{17,18},{18,... | collective-permute-start | bytes 5308424 | tf_op jit(solution)/shard_map/ppermute | solution.py:471
  252.6 113.6 %copy-start.36 = (f32[3,1152]{1,0:T(4,128)S(1)}, f32[3,1152]{1,0:T(4,128)}, u32[]{:S(2)}) copy-start(f32[3,1152]{1,0:T(4,128)} %copy-done.35) | copy-start | bytes 41476
  252.6 113.6 %copy-start.40 = (f32[768]{0:T(1024)S(1)}, f32[768]{0:T(1024)}, u32[]{:S(2)}) copy-start(f32[768]{0:T(1024)} %copy-done.39) | copy-start | bytes 9220
  252.6 113.6 %copy-start.44 = (f32[768]{0:T(1024)S(1)}, f32[768]{0:T(1024)}, u32[]{:S(2)}) copy-start(f32[768]{0:T(1024)} %copy-done.43) | copy-start | bytes 9220
  382.4 54.8 %copy-start.27 = (bf16[1152,1728]{1,0:T(8,128)(2,1)S(1)}, bf16[1152,1728]{1,0:T(8,128)(2,1)}, u32[]{:S(2)}) copy-start(bf16[1152,1728]{1,0:T(8,128)(2,1)} %get-tuple-element.62) | copy-start | bytes 11943940
  444.1 9.6 %collective-permute-start.9 = (bf16[768,1152]{1,0:T(8,128)(2,1)}, bf16[768,1152]{1,0:T(8,128)(2,1)}, u32[]{:S(2)}, u32[]{:S(2)}) collective-permute-start(bf16[768,1152]{1,0:T(8,128)(2,1)} %convolution_convert_fusion), channel_id=1, source_target_pairs={{0,2},{1,3},{2,0},{3,1},{4,6},{5,7},{6,4},{7,5},{8,10},{9,11},{10,... | collective-permute-start | bytes 5308424 | tf_op jit(solution)/shard_map/ppermute | solution.py:471
  444.4 27.6 %collective-permute-start.6 = (bf16[768,1152]{1,0:T(8,128)(2,1)}, bf16[768,1152]{1,0:T(8,128)(2,1)}, u32[]{:S(2)}, u32[]{:S(2)}) collective-permute-start(bf16[768,1152]{1,0:T(8,128)(2,1)} %copy-done.25), channel_id=1, source_target_pairs={{1,2},{2,1},{5,6},{6,5},{9,10},{10,9},{13,14},{14,13},{17,18},{18,... | collective-permute-start | bytes 5308424 | tf_op jit(solution)/shard_map/ppermute | solution.py:471
  467.2 6.3 collective-permute-start.11
  470.1 175.2 %collective-permute-start.10 = (bf16[768,1152]{1,0:T(8,128)(2,1)}, bf16[768,1152]{1,0:T(8,128)(2,1)}, u32[]{:S(2)}, u32[]{:S(2)}) collective-permute-start(bf16[768,1152]{1,0:T(8,128)(2,1)} %add_convert_fusion.1), channel_id=1, source_target_pairs={{1,2},{2,1},{5,6},{6,5},{9,10},{10,9},{13,14},{14,13},{17,18},{18,... | collective-permute-start | bytes 5308424 | tf_op jit(solution)/shard_map/ppermute | solution.py:471
  (59 other events, 407.2 us)
